TPU v7x, 256 devices: a whole 4x4x8 slice. The times are simulated.
256 devices in a mesh: blk: 128 (over x_hi, z, y, core), grp: 2 (over x_lo).
Axes of the slice: x: 4 (x_hi: 2, x_lo: 2; x = x_hi * 2 + x_lo), y: 4, z: 8, core: 2. Of those that a mesh axis runs over, the one named last changes fastest.
Arguments:
- layer_one: bfloat16 [14336, 1024], P(('blk', 'grp')), may hold values from -6 to 6
- layer_two: bfloat16 [14336, 1024], P(('blk', 'grp')), may hold values from -6 to 6
- spread: int32 [2], replicated, may hold values from 1024 to 4096
Outputs:
- profiles: float32 [2, 14336], P(None, ('blk', 'grp'))
- alignment: float32 [], replicated
All inputs are finite; a program needn't handle non-finite values.
Results may differ from a plain program's by a relative error of at most 0.0003.
Values may be sent and summed in bfloat16 or wider, within the bound.
No kernel may reach another device: no remote copies, remote signals or barrier semaphores. Data moves between devices by JAX's collectives and lax.ppermute only.
A program may use at most 128 MiB of HBM per device.

v0:
```python
import functools

import jax
import jax.numpy as jnp
from jax import lax
from jax.sharding import Mesh
from jax.sharding import PartitionSpec as P

D = 1024
BLK = ("blk_0", "blk_1", "blk_2", "blk_3")
BLK_GRP = ("blk_0", "blk_1", "blk_2", "blk_3", "grp")


def by_axis(array, axes):
    return functools.reduce(lax.psum, axes, array)


def kernel_block(rows, sq_rows, cols, scale, offset):
    sq_cols = jnp.sum(cols.astype(jnp.float32) ** 2, axis=1)
    inner = lax.dot_general(
        rows, cols, (((1,), (1,)), ((), ())), preferred_element_type=jnp.float32
    )
    dist = sq_rows[:, None] + sq_cols[None, :] - 2.0 * inner
    return jnp.exp(-dist / (2.0 * scale)) - offset


def shards(layer_one, layer_two, spread):
    scales = spread.astype(jnp.float32)
    offsets = jnp.exp(-D / scales)
    stacked = jnp.stack([layer_one, layer_two])
    paired = lax.all_gather(stacked, "grp", axis=1, tiled=True)
    sq_pair = jnp.sum(paired.astype(jnp.float32) ** 2, axis=2)
    block = lax.all_gather(stacked, BLK, axis=1, tiled=True)
    first = kernel_block(paired[0], sq_pair[0], block[0], scales[0], offsets[0])
    second = kernel_block(paired[1], sq_pair[1], block[1], scales[1], offsets[1])
    first, second = (first, second)
    rows_acc = jnp.stack([jnp.sum(first, axis=1), jnp.sum(second, axis=1)])
    prods = jnp.stack([jnp.sum(first * second), jnp.sum(first * first), jnp.sum(second * second)])
    rows_acc, prods = (rows_acc, prods)
    own_rows = lax.psum_scatter(rows_acc, "grp", scatter_dimension=1, tiled=True)
    total = own_rows.shape[1] * lax.axis_size(BLK) * lax.axis_size("grp")
    row_terms = jnp.stack(
        [
            jnp.sum(own_rows[0]),
            jnp.sum(own_rows[1]),
            jnp.sum(own_rows[0] * own_rows[1]),
            jnp.sum(own_rows[0] * own_rows[0]),
            jnp.sum(own_rows[1] * own_rows[1]),
        ]
    )
    prods = by_axis(prods, BLK_GRP)
    row_terms = by_axis(row_terms, BLK_GRP)
    sum_one, sum_two = (row_terms[0], row_terms[1])
    c_cross, c_one, c_two = (row_terms[2], row_terms[3], row_terms[4])
    h_cross = prods[0] - 2.0 * c_cross / total + sum_one * sum_two / (total * total)
    h_one = prods[1] - 2.0 * c_one / total + sum_one * sum_one / (total * total)
    h_two = prods[2] - 2.0 * c_two / total + sum_two * sum_two / (total * total)
    alignment = h_cross / jnp.sqrt(h_one * h_two)
    profiles = jnp.stack(
        [own_rows[0] / jnp.sqrt(c_one / total), own_rows[1] / jnp.sqrt(c_two / total)]
    )
    return (profiles, alignment)


def solution(mesh):
    finer = Mesh(
        mesh.devices.reshape(2, 8, 4, 2, mesh.shape["grp"]),
        ("blk_0", "blk_1", "blk_2", "blk_3", "grp"),
    )
    return jax.shard_map(
        shards,
        mesh=finer,
        in_specs=(P(BLK_GRP, None), P(BLK_GRP, None), P()),
        out_specs=(P(None, BLK_GRP), P()),
        check_vma=False,
    )
```

profile of v0, /device:TPU:6, one launch (start us, length us, event | category | flops | bytes accessed | tf_op | source)
XLA Modules:
  0.0 310.7 jit_solution(16533642095395601667)
XLA Ops:
  7.2 0.0 all-gather.2.cloned.1.call-start
  7.2 1.7 pad_maximum_fusion
  8.9 0.0 all-gather.2.cloned.1.call-update
  8.9 0.7 convert_element_type.14
  9.6 0.6 fusion.16
  11.5 1.3 dynamic-slice
  13.4 0.7 divide_exponential_fusion
  14.0 0.6 fusion.17
  14.6 8.2 %all_gather.6 = bf16[2,112,1024]{2,1,0:T(8,128)(2,1)S(1)} all-gather(bf16[2,56,1024]{2,1,0:T(8,128)(2,1)} %pad_maximum_fusion), channel_id=1, replica_groups=mesh['blk_0'=2,'blk_1'=8,'blk_2'=4,'blk_3'=2,'grp'=2] {'grp'}, dimensions={1}, use_global_device_ids=true | all-gather | bytes 688128 | tf_op jit(solution)/shard_map/all_gather | solution.py:31
  22.9 0.2 multiply_reduce_fusion.5
  23.0 186.7 %all-gather.2.cloned.1.call-done = bf16[2,7168,1024]{2,1,0:T(8,128)(2,1)} async-done(((bf16[2,56,1024]{2,1,0:T(8,128)(2,1)}), bf16[2,7168,1024]{2,1,0:T(8,128)(2,1)}) %all-gather.2.cloned.1.call-update) | async-done | bytes 29360144 | tf_op jit(solution)/shard_map/all_gather | solution.py:33
  209.8 12.8 %multiply_reduce_fusion.1 = (f32[7168]{0:T(1024)S(1)}, f32[7168]{0:T(1024)S(1)}) fusion(bf16[2,7168,1024]{2,1,0:T(8,128)(2,1)} %all-gather.2.cloned.1.call-done), kind=kLoop, calls=%fused_computation.1 | loop fusion | flops 44025856 | bytes 29417472 | tf_op jit(solution)/shard_map/reduce_sum | solution.py:19
  222.6 9.0 %fusion.10 = f32[112,7168]{1,0:T(8,128)S(1)} fusion(bf16[2,7168,1024]{2,1,0:T(8,128)(2,1)} %all-gather.2.cloned.1.call-done, f32[]{:T(128)} %bitcast.12, f32[]{:T(128)} %bitcast.11, f32[7168]{0:T(1024)S(1)} %get-tuple-element.3, f32[112]{0:T(128)S(1)} %get-tuple-element.26, bf16[2,112,1024]{2,1,0:T(8,128)(2,1)S(1)} %all_gather.6), kind=kOutput, calls=%fused_computation.14 | convolution fusion | flops 1648984064 | bytes 18150912 | tf_op jit(solution)/shard_map/dot_general | solution.py:20
  231.6 10.3 %multiply_reduce_fusion.4 = (f32[]{:T(128)}, f32[]{:T(128)}, f32[112]{0:T(128)S(1)}, f32[]{:T(128)}, f32[112]{0:T(128)S(1)}) fusion(f32[112,7168]{1,0:T(8,128)S(1)} %fusion.10, f32[]{:T(128)} %bitcast.6, f32[]{:T(128)} %bitcast.5, bf16[2,7168,1024]{2,1,0:T(8,128)(2,1)} %all-gather.2.cloned.1.call-done, bf16[2,112,1024]{2,1,0:T(8,128)(2,1)S(1)} %all_gather.6, ...), kind=kOutput, calls=%fused_computation.20 | convolution fusion | flops 1655406336 | bytes 18151820 | tf_op jit(solution)/shard_map/dot_general | solution.py:20
  241.9 4.9 %all-reduce = f32[2,112]{1,0:T(2,128)S(1)} all-reduce(f32[2,112]{1,0:T(2,128)S(1)} %pad_maximum_fusion.1), channel_id=2, replica_groups=mesh['blk_0'=2,'blk_1'=8,'blk_2'=4,'blk_3'=2,'grp'=2] {'grp'}, use_global_device_ids=true, to_apply=%region_5.0.clone | all-reduce | flops 224 | bytes 1792
  246.8 0.1 constant_dynamic-slice_fusion
  246.9 0.7 multiply_reduce_fusion.6
  247.6 2.0 pad_maximum_fusion.3
  249.6 3.2 %stack.64 = f32[5]{0:T(128)S(1)} concatenate(f32[1]{0:T(128)} %bitcast.14, f32[1]{0:T(128)} %bitcast.15, f32[1]{0:T(128)} %bitcast.16, f32[1]{0:T(128)} %bitcast.17, f32[1]{0:T(128)} %bitcast.18), dimensions={0} | concatenate | bytes 40 | tf_op jit(solution)/shard_map/stack | solution.py:42
  252.8 6.4 %all-reduce.5 = (f32[5]{0:T(128)S(1)}, f32[3]{0:T(128)S(1)}) all-reduce(f32[5]{0:T(128)S(1)} %stack.64, f32[3]{0:T(128)S(1)} %pad_maximum_fusion.3), channel_id=1, replica_groups=mesh['blk_0'=2,'blk_1'=8,'blk_2'=4,'blk_3'=2,'grp'=2] {'blk_0'}, use_global_device_ids=true, to_apply=%region_11.0 | all-reduce | flops 8 | bytes 64 | tf_op jit(solution)/shard_map/psum | solution.py:15
  259.3 15.5 %all-reduce.1 = (f32[5]{0:T(128)S(1)}, f32[3]{0:T(128)S(1)}) all-reduce(f32[5]{0:T(128)S(1)} %get-tuple-element.22, f32[3]{0:T(128)S(1)} %get-tuple-element.23), channel_id=1, replica_groups=mesh['blk_0'=2,'blk_1'=8,'blk_2'=4,'blk_3'=2,'grp'=2] {'blk_1'}, use_global_device_ids=true, to_apply=%region_12.0 | all-reduce | flops 8 | bytes 64 | tf_op jit(solution)/shard_map/psum | solution.py:15
  274.8 10.5 %all-reduce.2 = (f32[5]{0:T(128)S(1)}, f32[3]{0:T(128)S(1)}) all-reduce(f32[5]{0:T(128)S(1)} %get-tuple-element.14, f32[3]{0:T(128)S(1)} %get-tuple-element.15), channel_id=1, replica_groups=mesh['blk_0'=2,'blk_1'=8,'blk_2'=4,'blk_3'=2,'grp'=2] {'blk_2'}, use_global_device_ids=true, to_apply=%region_13.0 | all-reduce | flops 8 | bytes 64 | tf_op jit(solution)/shard_map/psum | solution.py:15
  285.2 2.4 all-reduce.4
  287.7 4.9 %all-reduce.3 = (f32[5]{0:T(128)S(1)}, f32[3]{0:T(128)S(1)}) all-reduce(f32[5]{0:T(128)S(1)} %get-tuple-element.20, f32[3]{0:T(128)S(1)} %get-tuple-element.21), channel_id=1, replica_groups=mesh['blk_0'=2,'blk_1'=8,'blk_2'=4,'blk_3'=2,'grp'=2] {'grp'}, use_global_device_ids=true, to_apply=%region_15.0 | all-reduce | flops 8 | bytes 64 | tf_op jit(solution)/shard_map/psum | solution.py:15
  292.6 0.7 fusion.14
  302.1 0.6 pad_maximum_fusion.2
  (3 shorter events, 0.0 us)
Async XLA Ops:
  7.2 202.6 %all-gather.2.cloned.1.call-start = ((), (), s32[]{:S(2)}) async-start(), calls=%async_computation | async-start | bytes 29589504 | tf_op jit(solution)/shard_map/all_gather | solution.py:33
Sparse Core Ops, SparseCore 0:
  11.7 198.0 all-gather.1
where the time goes:
time: 313 us; the launch traced here: 311 us
  waiting for transfers between devices  187 us (60%)
  blocking collectives  52.9 us (17%)
  between operations  26 us (8%)
  matrix products  19.3 us (6%)
  other arithmetic  19.2 us (6%)
  local copies, waits for them, and re-layouts  6.45 us (2%)
    all_gather x1, waiting for transfers between devices, shards(): block = lax.all_gather(stacked, BLK, axis=1, tiled=True)  187 us
    psum x5, blocking collectives, by_axis(): return functools.reduce(lax.psum, axes, array)  39.8 us
    dot_general x2, matrix products, kernel_block(): lax.dot_general(rows, cols, (((1,), (1,)), ((), ())), preferred_element_t...  19.3 us
    reduce_sum x1, other arithmetic, kernel_block(): sq_cols = jnp.sum(cols.astype(jnp.float32) ** 2, axis=1)  12.8 us
    all_gather x1, blocking collectives, shards(): paired = lax.all_gather(stacked, 'grp', axis=1, tiled=True)  8.22 us
  transfers between devices with their start and end apart: 1, of which 1 were waited for; matrix products, arithmetic and copies ran while one was open for 1% of the time, Pallas kernels for 0%

commit v1 on v0

v1 whole, which is shorter than its diff:
```python
import functools
import math

import jax
import jax.numpy as jnp
from jax import lax
from jax.experimental import pallas as pl
from jax.experimental.pallas import tpu as pltpu
from jax.sharding import Mesh
from jax.sharding import PartitionSpec as P

D = 1024
AXES = ("x_hi", "z", "y", "core", "x_lo")
LINE = ("z", "core")
NX, NY, NZ, NC = (4, 4, 8, 2)
LOG2E = math.log2(math.e)


def linear(x, y, z, core):
    return (((x // 2 * NZ + z) * NY + y) * NC + core) * 2 + x % 2


def move(array, where):
    pairs = []
    for x in range(NX):
        for y in range(NY):
            for z in range(NZ):
                for core in range(NC):
                    tx, ty, tz, tcore = where(x, y, z, core)
                    pairs.append((linear(x, y, z, core), linear(tx % NX, ty % NY, tz % NZ, tcore % NC)))
    return lax.ppermute(array, AXES, pairs)


def shift(array, first, second):
    def where(x, y, z, core):
        dx, dy = (first, second) if core == 0 else (second, first)
        return x + dx, y + dy, z, core

    return move(array, where)


def gram_body(spread_ref, z_ref, *refs):
    pieces, out_ref, scaled_ref = refs[:-2], refs[-2], refs[-1]
    width = z_ref.shape[1]
    scales = [spread_ref[0].astype(jnp.float32), spread_ref[1].astype(jnp.float32)]
    factors = []
    offsets = []
    for layer in range(2):
        scale = jnp.full((1, 128), scales[layer], jnp.float32)
        factors.append((LOG2E / scale)[:, :1])
        offsets.append(jnp.exp(-D / scale)[:, :1])
        for start in range(0, width, 128):
            rows = z_ref[layer, start : start + 128, :].astype(jnp.float32)
            square = rows * rows
            folded = square[:, :128]
            for lane in range(128, D, 128):
                folded = folded + square[:, lane : lane + 128]
            sums = jnp.sum(folded.T, axis=0, keepdims=True)
            scaled_ref[layer : layer + 1, start : start + 128] = sums * (0.5 * factors[layer])
    sums = [jnp.zeros((8, width), jnp.float32) for _ in range(5)]

    def fold(array):
        parts = array.reshape(array.shape[0] // 8, 8, width)
        return jnp.sum(parts, axis=0)

    for piece in pieces:
        tall = piece.shape[1]
        step = 112 if tall % 112 == 0 else tall
        for start in range(0, tall, step):
            kernels = []
            for layer in range(2):
                rows = piece[layer, start : start + step, :]
                inner = lax.dot_general(
                    rows, z_ref[layer], (((1,), (1,)), ((), ())), preferred_element_type=jnp.float32
                )
                wide = rows.astype(jnp.float32)
                norms = jnp.sum(wide * wide, axis=1, keepdims=True) * (0.5 * factors[layer])
                power = inner * factors[layer] - norms - scaled_ref[layer : layer + 1, :]
                kernels.append(jnp.exp2(power) - offsets[layer])
            one, two = kernels
            for at, term in enumerate((one, two, one * two, one * one, two * two)):
                sums[at] = sums[at] + fold(term)
    for at in range(5):
        out_ref[at : at + 1, :] = jnp.sum(sums[at], axis=0, keepdims=True)
    out_ref[5:8, :] = jnp.zeros((3, width), jnp.float32)


def gram(spread, line, pieces):
    width = line.shape[1]
    vmem = pl.BlockSpec(memory_space=pltpu.VMEM)
    rows = sum(piece.shape[1] for piece in pieces)
    return pl.pallas_call(
        gram_body,
        out_shape=jax.ShapeDtypeStruct((8, width), jnp.float32),
        in_specs=[pl.BlockSpec(memory_space=pltpu.SMEM), vmem] + [vmem] * len(pieces),
        out_specs=vmem,
        scratch_shapes=[pltpu.VMEM((2, width), jnp.float32)],
        compiler_params=pltpu.CompilerParams(vmem_limit_bytes=40 << 20),
        cost_estimate=pl.CostEstimate(
            flops=4 * rows * width * D, bytes_accessed=4 * (rows + width) * D, transcendentals=2 * rows * width
        ),
        name="gram",
    )(spread, line, *pieces)


def shards(layer_one, layer_two, spread):
    own = jnp.stack([layer_one, layer_two])
    count = own.shape[1]
    line = lax.all_gather(own, LINE, axis=1, tiled=True)
    near = [shift(own, 1, 0), shift(own, -1, 0), shift(own, 2, 0)]
    strip = jnp.concatenate([own] + near, axis=1)
    pieces = [strip, shift(strip, 0, 1), shift(strip, 0, -1), shift(strip, 0, 2)]
    part = gram(spread, line, pieces)
    part = part + move(part, lambda x, y, z, core: (x, y, z, core ^ 1))
    for bit in (1, 2, 4):
        part = part + move(part, lambda x, y, z, core: (x, y, z ^ bit, core))
    total = count * lax.axis_size(AXES)
    r_one, r_two = part[0], part[1]
    scalars = jnp.stack(
        [r_one, r_two, part[2], part[3], part[4], r_one * r_two, r_one * r_one, r_two * r_two]
    )
    scalars = jnp.sum(scalars.reshape(8, part.shape[1] // 128, 128), axis=1)
    scalars = scalars + move(scalars, lambda x, y, z, core: (x ^ 1, y, z, core))
    scalars = scalars + move(scalars, lambda x, y, z, core: (x ^ 2, y, z, core))
    scalars = lax.psum(scalars, "y")
    scalars = jnp.sum(scalars, axis=1)
    sum_one, sum_two, f_cross, f_one, f_two, c_cross, c_one, c_two = (scalars[at] for at in range(8))
    h_cross = f_cross - 2.0 * c_cross / total + sum_one * sum_two / (total * total)
    h_one = f_one - 2.0 * c_one / total + sum_one * sum_one / (total * total)
    h_two = f_two - 2.0 * c_two / total + sum_two * sum_two / (total * total)
    alignment = h_cross / jnp.sqrt(h_one * h_two)
    mine = lax.dynamic_slice(part, (0, lax.axis_index(LINE) * count), (2, count))
    profiles = mine / jnp.sqrt(jnp.stack([c_one, c_two]) / total)[:, None]
    return (profiles, alignment)


def solution(mesh):
    finer = Mesh(mesh.devices.reshape(2, NZ, NY, NC, 2), AXES)
    return jax.shard_map(
        shards,
        mesh=finer,
        in_specs=(P(AXES, None), P(AXES, None), P()),
        out_specs=(P(None, AXES), P()),
        check_vma=False,
    )
```

time: 313 us -> 122 us (0.39)
  waiting for transfers between devices: 187 us -> 49.6 us
  blocking collectives: 52.9 us -> 10.4 us
  starting transfers between devices: 0.04 us -> 20.2 us
  matrix products: 19.3 us -> 0 us
  other arithmetic: 19.2 us -> 3.62 us
  Pallas kernels: 0 us -> 10.4 us
  between operations: 26 us -> 22.8 us
    all_gather x1, waiting for transfers between devices: 187 us -> 7.05 us  [shards(): line = lax.all_gather(own, LINE, axis=1, tiled=True)]
    ppermute x0 -> x12, waiting for transfers between devices: none -> 42.5 us  [move(): return lax.ppermute(array, AXES, pairs)]
    psum x5 -> x1, blocking collectives: 39.8 us -> 10.4 us  [shards(): scalars = lax.psum(scalars, 'y')]
    ppermute x0 -> x12, starting transfers between devices: none -> 20.2 us  [move(): return lax.ppermute(array, AXES, pairs)]
    dot_general x2 -> x0, matrix products: 19.3 us -> none  [kernel_block(): lax.dot_general(rows, cols, (((1,), (1,)), ((), ())), preferred_element_t...]
    reduce_sum x3 -> x2, other arithmetic: 13.7 us -> 0.14 us  [the longest x1 0.12 us: shards(): scalars = jnp.sum(scalars, axis=1)]
    pallas_call x0 -> x1, Pallas kernels: none -> 10.4 us  [gram(): pl.pallas_call(gram_body, out_shape=jax.ShapeDtypeStruct((8, width), jnp....]
    all_gather x1 -> x0, blocking collectives: 8.22 us -> none  [shards(): paired = lax.all_gather(stacked, 'grp', axis=1, tiled=True)]
  transfers between devices with their start and end apart: 1 -> 13, of which waited for: 1 -> 12; matrix products, arithmetic and copies ran while one was open for 1% -> 1% of each run, Pallas kernels for 0% -> 0%
where the time goes in v1:
time: 122 us
  waiting for transfers between devices  49.6 us (41%)
  between operations  22.8 us (19%)
  starting transfers between devices  20.2 us (17%)
  Pallas kernels  10.4 us (9%)
  blocking collectives  10.4 us (9%)
  local copies, waits for them, and re-layouts  4.82 us (4%)
  other arithmetic  3.62 us (3%)
    ppermute x12, waiting for transfers between devices, move(): return lax.ppermute(array, AXES, pairs)  42.5 us
    ppermute x12, starting transfers between devices, move(): return lax.ppermute(array, AXES, pairs)  20.2 us
    psum x1, blocking collectives, shards(): scalars = lax.psum(scalars, 'y')  10.4 us
    pallas_call x1, Pallas kernels, gram(): pl.pallas_call(gram_body, out_shape=jax.ShapeDtypeStruct((8, width), jnp....  10.4 us
    all_gather x1, waiting for transfers between devices, shards(): line = lax.all_gather(own, LINE, axis=1, tiled=True)  7.05 us
    unnamed x8, local copies, waits for them, and re-layouts  4.13 us
  transfers between devices with their start and end apart: 13, of which 12 were waited for; matrix products, arithmetic and copies ran while one was open for 1% of the time, Pallas kernels for 0%

profile of v1, /device:TPU:6, one launch (start us, length us, event | category | flops | bytes accessed | tf_op | source)
XLA Modules:
  0.0 121.8 jit_solution(1651494692727450897)
XLA Ops:
  7.2 1.7 %pad_maximum_fusion.1 = bf16[2,56,1024]{2,1,0:T(8,128)(2,1)} fusion(bf16[1,56,1024]{2,1,0:T(8,128)(2,1)} %bitcast.7, bf16[1,56,1024]{2,1,0:T(8,128)(2,1)} %bitcast.9), kind=kLoop, calls=%fused_computation.1 | loop fusion | flops 114688 | bytes 458752 | tf_op jit(solution)/shard_map/stack | solution.py:107
  8.9 1.5 %collective-permute-start.2 = (bf16[2,56,1024]{2,1,0:T(8,128)(2,1)}, bf16[2,56,1024]{2,1,0:T(8,128)(2,1)S(1)}, u32[]{:S(2)}, u32[]{:S(2)}) collective-permute-start(bf16[2,56,1024]{2,1,0:T(8,128)(2,1)} %pad_maximum_fusion.1), channel_id=1, source_target_pairs={{0,128},{2,10},{16,144},{18,26},{32,160},{34,42},{48,176},{50,58},... | collective-permute-start | bytes 688136 | tf_op jit(solution)/shard_map/ppermute | solution.py:31
  10.4 1.7 %collective-permute-start.1 = (bf16[2,56,1024]{2,1,0:T(8,128)(2,1)}, bf16[2,56,1024]{2,1,0:T(8,128)(2,1)S(1)}, u32[]{:S(2)}, u32[]{:S(2)}) collective-permute-start(bf16[2,56,1024]{2,1,0:T(8,128)(2,1)} %pad_maximum_fusion.1), channel_id=1, source_target_pairs={{0,129},{2,14},{16,145},{18,30},{32,161},{34,46},{48,177},{50,62},... | collective-permute-start | bytes 688136 | tf_op jit(solution)/shard_map/ppermute | solution.py:31
  12.1 1.6 %collective-permute-start = (bf16[2,56,1024]{2,1,0:T(8,128)(2,1)}, bf16[2,56,1024]{2,1,0:T(8,128)(2,1)S(1)}, u32[]{:S(2)}, u32[]{:S(2)}) collective-permute-start(bf16[2,56,1024]{2,1,0:T(8,128)(2,1)} %pad_maximum_fusion.1), channel_id=1, source_target_pairs={{0,1},{2,6},{16,17},{18,22},{32,33},{34,38},{48,49},{50,54},{64,65... | collective-permute-start | bytes 688136 | tf_op jit(solution)/shard_map/ppermute | solution.py:31
  13.7 3.2 %collective-permute-done.2 = bf16[2,56,1024]{2,1,0:T(8,128)(2,1)S(1)} collective-permute-done((bf16[2,56,1024]{2,1,0:T(8,128)(2,1)}, bf16[2,56,1024]{2,1,0:T(8,128)(2,1)S(1)}, u32[]{:S(2)}, u32[]{:S(2)}) %collective-permute-start.2) | collective-permute-done | bytes 229408 | tf_op jit(solution)/shard_map/ppermute | solution.py:31
  16.9 2.4 %collective-permute-done.1 = bf16[2,56,1024]{2,1,0:T(8,128)(2,1)S(1)} collective-permute-done((bf16[2,56,1024]{2,1,0:T(8,128)(2,1)}, bf16[2,56,1024]{2,1,0:T(8,128)(2,1)S(1)}, u32[]{:S(2)}, u32[]{:S(2)}) %collective-permute-start.1) | collective-permute-done | bytes 229408 | tf_op jit(solution)/shard_map/ppermute | solution.py:31
  19.2 1.0 pad_maximum_fusion.refs_0_
  20.2 1.7 %collective-permute-start.3 = (bf16[2,224,1024]{2,1,0:T(8,128)(2,1)S(1)}, bf16[2,224,1024]{2,1,0:T(8,128)(2,1)S(1)}, u32[]{:S(2)}, u32[]{:S(2)}) collective-permute-start(bf16[2,224,1024]{2,1,0:T(8,128)(2,1)S(1)} %pad_maximum_fusion.refs_0_), channel_id=1, source_target_pairs={{0,4},{2,3},{16,20},{18,19},{32,36},{34,35},{48,52},{50,51},{64,68... | collective-permute-start | bytes 2752520 | tf_op jit(solution)/shard_map/ppermute | solution.py:31
  21.9 1.7 %collective-permute-start.4 = (bf16[2,224,1024]{2,1,0:T(8,128)(2,1)S(1)}, bf16[2,224,1024]{2,1,0:T(8,128)(2,1)S(1)}, u32[]{:S(2)}, u32[]{:S(2)}) collective-permute-start(bf16[2,224,1024]{2,1,0:T(8,128)(2,1)S(1)} %pad_maximum_fusion.refs_0_), channel_id=1, source_target_pairs={{0,12},{2,131},{16,28},{18,147},{32,44},{34,163},{48,60},{50,179},... | collective-permute-start | bytes 2752520 | tf_op jit(solution)/shard_map/ppermute | solution.py:31
  23.6 2.0 %collective-permute-start.5 = (bf16[2,224,1024]{2,1,0:T(8,128)(2,1)S(1)}, bf16[2,224,1024]{2,1,0:T(8,128)(2,1)S(1)}, u32[]{:S(2)}, u32[]{:S(2)}) collective-permute-start(bf16[2,224,1024]{2,1,0:T(8,128)(2,1)S(1)} %pad_maximum_fusion.refs_0_), channel_id=1, source_target_pairs={{0,8},{2,130},{16,24},{18,146},{32,40},{34,162},{48,56},{50,178},{... | collective-permute-start | bytes 2752520 | tf_op jit(solution)/shard_map/ppermute | solution.py:31
  25.5 9.4 %collective-permute-done.3.refs_1_ = bf16[2,224,1024]{2,1,0:T(8,128)(2,1)S(1)} collective-permute-done((bf16[2,224,1024]{2,1,0:T(8,128)(2,1)S(1)}, bf16[2,224,1024]{2,1,0:T(8,128)(2,1)S(1)}, u32[]{:S(2)}, u32[]{:S(2)}) %collective-permute-start.3) | collective-permute-done | bytes 917536 | tf_op jit(solution)/shard_map/ppermute | solution.py:31
  35.3 10.7 %collective-permute-done.5.refs_3_ = bf16[2,224,1024]{2,1,0:T(8,128)(2,1)S(1)} collective-permute-done((bf16[2,224,1024]{2,1,0:T(8,128)(2,1)S(1)}, bf16[2,224,1024]{2,1,0:T(8,128)(2,1)S(1)}, u32[]{:S(2)}, u32[]{:S(2)}) %collective-permute-start.5) | collective-permute-done | bytes 917536 | tf_op jit(solution)/shard_map/ppermute | solution.py:31
  46.0 0.9 copy-done.1
  46.9 7.1 %all-gather.2.cloned.1.call-done.z_ref = bf16[2,896,1024]{2,1,0:T(8,128)(2,1)} async-done(((bf16[2,56,1024]{2,1,0:T(8,128)(2,1)}), bf16[2,896,1024]{2,1,0:T(8,128)(2,1)}) %all-gather.2.cloned.1.call-update) | async-done | bytes 3670032 | tf_op jit(solution)/shard_map/all_gather | solution.py:109
  54.0 2.0 %copy-done = bf16[2,896,1024]{2,1,0:T(8,128)(2,1)S(1)} copy-done((bf16[2,896,1024]{2,1,0:T(8,128)(2,1)S(1)}, bf16[2,896,1024]{2,1,0:T(8,128)(2,1)}, u32[]{:S(2)}) %copy-start) | copy-done | bytes 3670040
  56.0 1.2 copy-done.2
  57.2 10.4 %gram.1 = f32[8,896]{1,0:T(8,128)S(1)} custom-call(s32[2]{0:T(128)S(1)} %copy-done.3, bf16[2,896,1024]{2,1,0:T(8,128)(2,1)S(1)} %copy-done, bf16[2,224,1024]{2,1,0:T(8,128)(2,1)S(1)} %pad_maximum_fusion.refs_0_, bf16[2,224,1024]{2,1,0:T(8,128)(2,1)S(1)} %collective-permute-done.3.refs_1_, bf16[2,224,1024]{2,1,0:T(8,128)(2,1)S(1)} %collective-permute-done.4.refs_2_, ...), custom_call_target="tpu_custom_call" | custom-call | flops 3288334336 | bytes 7340032 | tf_op jit(solution)/shard_map/gram/pallas_call | solution.py:92
  67.5 0.5 collective-permute-start.6
  68.0 1.0 collective-permute-done.6
  69.0 1.8 %collective-permute-start.7 = (f32[8,896]{1,0:T(8,128)S(1)}, f32[8,896]{1,0:T(8,128)S(1)}, u32[]{:S(2)}, u32[]{:S(2)}) collective-permute-start(f32[8,896]{1,0:T(8,128)S(1)} %add.40), channel_id=1, source_target_pairs={{0,16},{2,18},{16,0},{18,2},{32,48},{34,50},{48,32},{50,34},{64,80... | collective-permute-start | bytes 86024 | tf_op jit(solution)/shard_map/ppermute | solution.py:31
  70.8 2.0 %collective-permute-done.7 = f32[8,896]{1,0:T(8,128)S(1)} collective-permute-done((f32[8,896]{1,0:T(8,128)S(1)}, f32[8,896]{1,0:T(8,128)S(1)}, u32[]{:S(2)}, u32[]{:S(2)}) %collective-permute-start.7) | collective-permute-done | bytes 28704 | tf_op jit(solution)/shard_map/ppermute | solution.py:31
  72.9 1.9 %collective-permute-start.8 = (f32[8,896]{1,0:T(8,128)S(1)}, f32[8,896]{1,0:T(8,128)S(1)}, u32[]{:S(2)}, u32[]{:S(2)}) collective-permute-start(f32[8,896]{1,0:T(8,128)S(1)} %add.41), channel_id=1, source_target_pairs={{0,32},{2,34},{16,48},{18,50},{32,0},{34,2},{48,16},{50,18},{64,96... | collective-permute-start | bytes 86024 | tf_op jit(solution)/shard_map/ppermute | solution.py:31
  74.8 2.8 %collective-permute-done.8 = f32[8,896]{1,0:T(8,128)S(1)} collective-permute-done((f32[8,896]{1,0:T(8,128)S(1)}, f32[8,896]{1,0:T(8,128)S(1)}, u32[]{:S(2)}, u32[]{:S(2)}) %collective-permute-start.8) | collective-permute-done | bytes 28704 | tf_op jit(solution)/shard_map/ppermute | solution.py:31
  77.7 3.5 %collective-permute-start.9 = (f32[8,896]{1,0:T(8,128)S(1)}, f32[8,896]{1,0:T(8,128)S(1)}, u32[]{:S(2)}, u32[]{:S(2)}) collective-permute-start(f32[8,896]{1,0:T(8,128)S(1)} %add.42), channel_id=1, source_target_pairs={{0,64},{2,66},{16,80},{18,82},{32,96},{34,98},{48,112},{50,114},{6... | collective-permute-start | bytes 86024 | tf_op jit(solution)/shard_map/ppermute | solution.py:31
  81.2 4.3 %collective-permute-done.9 = f32[8,896]{1,0:T(8,128)S(1)} collective-permute-done((f32[8,896]{1,0:T(8,128)S(1)}, f32[8,896]{1,0:T(8,128)S(1)}, u32[]{:S(2)}, u32[]{:S(2)}) %collective-permute-start.9) | collective-permute-done | bytes 28704 | tf_op jit(solution)/shard_map/ppermute | solution.py:31
  85.5 0.9 collective-permute-start.10
  86.5 2.8 %collective-permute-done.10 = f32[8,128]{1,0:T(8,128)S(1)} collective-permute-done((f32[8,128]{1,0:T(8,128)S(1)}, f32[8,128]{1,0:T(8,128)S(1)}, u32[]{:S(2)}, u32[]{:S(2)}) %collective-permute-start.10) | collective-permute-done | bytes 4128 | tf_op jit(solution)/shard_map/ppermute | solution.py:31
  89.2 1.5 %collective-permute-start.11 = (f32[8,128]{1,0:T(8,128)S(1)}, f32[8,128]{1,0:T(8,128)S(1)}, u32[]{:S(2)}, u32[]{:S(2)}) collective-permute-start(f32[8,128]{1,0:T(8,128)S(1)} %add.46), channel_id=1, source_target_pairs={{0,128},{2,130},{16,144},{18,146},{32,160},{34,162},{48,176},{50,1... | collective-permute-start | bytes 12296 | tf_op jit(solution)/shard_map/ppermute | solution.py:31
  90.7 3.7 %collective-permute-done.11 = f32[8,128]{1,0:T(8,128)S(1)} collective-permute-done((f32[8,128]{1,0:T(8,128)S(1)}, f32[8,128]{1,0:T(8,128)S(1)}, u32[]{:S(2)}, u32[]{:S(2)}) %collective-permute-start.11) | collective-permute-done | bytes 4128 | tf_op jit(solution)/shard_map/ppermute | solution.py:31
  94.3 10.4 %psum.7 = f32[8,128]{1,0:T(8,128)S(1)} all-reduce(f32[8,128]{1,0:T(8,128)S(1)} %add.47), channel_id=1, replica_groups=mesh['x_hi'=2,'z'=8,'y'=4,'core'=2,'x_lo'=2] {'y'}, use_global_device_ids=true, to_apply=%region_1.0 | all-reduce | flops 1024 | bytes 8192 | tf_op jit(solution)/shard_map/psum | solution.py:125
  105.0 0.7 fusion
  112.5 0.6 dynamic-slice_divide_fusion
  (20 shorter events, 0.7 us)
Async XLA Ops:
  7.2 46.8 %copy-start.3 = (s32[2]{0:T(128)S(1)}, s32[2]{0:T(128)}, u32[]{:S(2)}) copy-start(s32[2]{0:T(128)} %spread_ref.1) | copy-start | bytes 28
  7.2 46.8 %all-gather.2.cloned.1.call-start = ((), (), s32[]{:S(2)}) async-start(), calls=%async_computation | async-start | bytes 3899392 | tf_op jit(solution)/shard_map/all_gather | solution.py:109
  8.9 7.9 %collective-permute-start.2 = (bf16[2,56,1024]{2,1,0:T(8,128)(2,1)}, bf16[2,56,1024]{2,1,0:T(8,128)(2,1)S(1)}, u32[]{:S(2)}, u32[]{:S(2)}) collective-permute-start(bf16[2,56,1024]{2,1,0:T(8,128)(2,1)} %pad_maximum_fusion.1), channel_id=1, source_target_pairs={{0,128},{2,10},{16,144},{18,26},{32,160},{34,42},{48,176},{50,58},... | collective-permute-start | bytes 688136 | tf_op jit(solution)/shard_map/ppermute | solution.py:31
  10.4 8.8 %collective-permute-start.1 = (bf16[2,56,1024]{2,1,0:T(8,128)(2,1)}, bf16[2,56,1024]{2,1,0:T(8,128)(2,1)S(1)}, u32[]{:S(2)}, u32[]{:S(2)}) collective-permute-start(bf16[2,56,1024]{2,1,0:T(8,128)(2,1)} %pad_maximum_fusion.1), channel_id=1, source_target_pairs={{0,129},{2,14},{16,145},{18,30},{32,161},{34,46},{48,177},{50,62},... | collective-permute-start | bytes 688136 | tf_op jit(solution)/shard_map/ppermute | solution.py:31
  12.1 7.1 %collective-permute-start = (bf16[2,56,1024]{2,1,0:T(8,128)(2,1)}, bf16[2,56,1024]{2,1,0:T(8,128)(2,1)S(1)}, u32[]{:S(2)}, u32[]{:S(2)}) collective-permute-start(bf16[2,56,1024]{2,1,0:T(8,128)(2,1)} %pad_maximum_fusion.1), channel_id=1, source_target_pairs={{0,1},{2,6},{16,17},{18,22},{32,33},{34,38},{48,49},{50,54},{64,65... | collective-permute-start | bytes 688136 | tf_op jit(solution)/shard_map/ppermute | solution.py:31
  20.2 14.7 %collective-permute-start.3 = (bf16[2,224,1024]{2,1,0:T(8,128)(2,1)S(1)}, bf16[2,224,1024]{2,1,0:T(8,128)(2,1)S(1)}, u32[]{:S(2)}, u32[]{:S(2)}) collective-permute-start(bf16[2,224,1024]{2,1,0:T(8,128)(2,1)S(1)} %pad_maximum_fusion.refs_0_), channel_id=1, source_target_pairs={{0,4},{2,3},{16,20},{18,19},{32,36},{34,35},{48,52},{50,51},{64,68... | collective-permute-start | bytes 2752520 | tf_op jit(solution)/shard_map/ppermute | solution.py:31
  21.9 13.4 %collective-permute-start.4 = (bf16[2,224,1024]{2,1,0:T(8,128)(2,1)S(1)}, bf16[2,224,1024]{2,1,0:T(8,128)(2,1)S(1)}, u32[]{:S(2)}, u32[]{:S(2)}) collective-permute-start(bf16[2,224,1024]{2,1,0:T(8,128)(2,1)S(1)} %pad_maximum_fusion.refs_0_), channel_id=1, source_target_pairs={{0,12},{2,131},{16,28},{18,147},{32,44},{34,163},{48,60},{50,179},... | collective-permute-start | bytes 2752520 | tf_op jit(solution)/shard_map/ppermute | solution.py:31
  23.6 22.4 %collective-permute-start.5 = (bf16[2,224,1024]{2,1,0:T(8,128)(2,1)S(1)}, bf16[2,224,1024]{2,1,0:T(8,128)(2,1)S(1)}, u32[]{:S(2)}, u32[]{:S(2)}) collective-permute-start(bf16[2,224,1024]{2,1,0:T(8,128)(2,1)S(1)} %pad_maximum_fusion.refs_0_), channel_id=1, source_target_pairs={{0,8},{2,130},{16,24},{18,146},{32,40},{34,162},{48,56},{50,178},{... | collective-permute-start | bytes 2752520 | tf_op jit(solution)/shard_map/ppermute | solution.py:31
  46.0 0.9 copy-start.1
  54.0 2.0 %copy-start = (bf16[2,896,1024]{2,1,0:T(8,128)(2,1)S(1)}, bf16[2,896,1024]{2,1,0:T(8,128)(2,1)}, u32[]{:S(2)}) copy-start(bf16[2,896,1024]{2,1,0:T(8,128)(2,1)} %all-gather.2.cloned.1.call-done.z_ref) | copy-start | bytes 11010052
  56.0 1.2 copy-start.2
  67.5 1.5 %collective-permute-start.6 = (f32[8,896]{1,0:T(8,128)S(1)}, f32[8,896]{1,0:T(8,128)S(1)}, u32[]{:S(2)}, u32[]{:S(2)}) collective-permute-start(f32[8,896]{1,0:T(8,128)S(1)} %gram.1), channel_id=1, source_target_pairs={{0,2},{2,0},{16,18},{18,16},{32,34},{34,32},{48,50},{50,48},{64,66... | collective-permute-start | bytes 86024 | tf_op jit(solution)/shard_map/ppermute | solution.py:31
  69.0 3.9 %collective-permute-start.7 = (f32[8,896]{1,0:T(8,128)S(1)}, f32[8,896]{1,0:T(8,128)S(1)}, u32[]{:S(2)}, u32[]{:S(2)}) collective-permute-start(f32[8,896]{1,0:T(8,128)S(1)} %add.40), channel_id=1, source_target_pairs={{0,16},{2,18},{16,0},{18,2},{32,48},{34,50},{48,32},{50,34},{64,80... | collective-permute-start | bytes 86024 | tf_op jit(solution)/shard_map/ppermute | solution.py:31
  72.9 4.8 %collective-permute-start.8 = (f32[8,896]{1,0:T(8,128)S(1)}, f32[8,896]{1,0:T(8,128)S(1)}, u32[]{:S(2)}, u32[]{:S(2)}) collective-permute-start(f32[8,896]{1,0:T(8,128)S(1)} %add.41), channel_id=1, source_target_pairs={{0,32},{2,34},{16,48},{18,50},{32,0},{34,2},{48,16},{50,18},{64,96... | collective-permute-start | bytes 86024 | tf_op jit(solution)/shard_map/ppermute | solution.py:31
  77.7 7.8 %collective-permute-start.9 = (f32[8,896]{1,0:T(8,128)S(1)}, f32[8,896]{1,0:T(8,128)S(1)}, u32[]{:S(2)}, u32[]{:S(2)}) collective-permute-start(f32[8,896]{1,0:T(8,128)S(1)} %add.42), channel_id=1, source_target_pairs={{0,64},{2,66},{16,80},{18,82},{32,96},{34,98},{48,112},{50,114},{6... | collective-permute-start | bytes 86024 | tf_op jit(solution)/shard_map/ppermute | solution.py:31
  85.5 3.7 %collective-permute-start.10 = (f32[8,128]{1,0:T(8,128)S(1)}, f32[8,128]{1,0:T(8,128)S(1)}, u32[]{:S(2)}, u32[]{:S(2)}) collective-permute-start(f32[8,128]{1,0:T(8,128)S(1)} %maximum_reduce_fusion), channel_id=1, source_target_pairs={{0,1},{2,3},{16,17},{18,19},{32,33},{34,35},{48,49},{50,51},{64,65... | collective-permute-start | bytes 12296 | tf_op jit(solution)/shard_map/ppermute | solution.py:31
  89.2 5.1 %collective-permute-start.11 = (f32[8,128]{1,0:T(8,128)S(1)}, f32[8,128]{1,0:T(8,128)S(1)}, u32[]{:S(2)}, u32[]{:S(2)}) collective-permute-start(f32[8,128]{1,0:T(8,128)S(1)} %add.46), channel_id=1, source_target_pairs={{0,128},{2,130},{16,144},{18,146},{32,160},{34,162},{48,176},{50,1... | collective-permute-start | bytes 12296 | tf_op jit(solution)/shard_map/ppermute | solution.py:31
Sparse Core Ops, SparseCore 0:
  9.9 44.0 all-gather.1

commit v2 on v1

--- a/solution.py
+++ b/solution.py
@@ -95,12 +95,55 @@
         in_specs=[pl.BlockSpec(memory_space=pltpu.SMEM), vmem] + [vmem] * len(pieces),
         out_specs=vmem,
         scratch_shapes=[pltpu.VMEM((2, width), jnp.float32)],
-        compiler_params=pltpu.CompilerParams(vmem_limit_bytes=40 << 20),
+        compiler_params=pltpu.CompilerParams(vmem_limit_bytes=16 << 20),
         cost_estimate=pl.CostEstimate(
             flops=4 * rows * width * D, bytes_accessed=4 * (rows + width) * D, transcendentals=2 * rows * width
         ),
         name="gram",
     )(spread, line, *pieces)
+
+
+def swap(array):
+    return move(array, lambda x, y, z, core: (x, y, z, 1 - core))
+
+
+def line_sum(array):
+    array = array + swap(array)
+    for bit in (1, 2, 4):
+        array = array + move(array, lambda x, y, z, core: (x, y, z ^ bit, core))
+    return array
+
+
+def plane_sum(array):
+    for stage in range(2):
+        parts = [shift(array, *((step, 0) if stage == 0 else (0, step))) for step in (1, -1, 2)]
+        array = (array + parts[2]) + (parts[0] + parts[1])
+    return 0.5 * (array + swap(array))
+
+
+def finish_body(total, count, part_ref, sums_ref, profiles_ref, alignment_ref):
+    sums = jnp.sum(sums_ref[...], axis=1, keepdims=True)
+    sum_one, sum_two, f_cross, f_one, f_two, c_cross, c_one, c_two = (sums[at : at + 1, :] for at in range(8))
+    h_cross = f_cross - 2.0 * c_cross / total + sum_one * sum_two / (total * total)
+    h_one = f_one - 2.0 * c_one / total + sum_one * sum_one / (total * total)
+    h_two = f_two - 2.0 * c_two / total + sum_two * sum_two / (total * total)
+    alignment_ref[...] = h_cross / jnp.sqrt(h_one * h_two)
+    width = part_ref.shape[1]
+    first = (lax.axis_index("z") * NC + lax.axis_index("core")) * count
+    rows = pltpu.roll(part_ref[...], lax.rem(width - first, width), 1)
+    roots = jnp.sqrt(jnp.concatenate([c_one, c_two], axis=0) / total)
+    profiles_ref[...] = rows[:2, :count] / roots
+
+
+def finish(part, sums, total, count):
+    vmem = pl.BlockSpec(memory_space=pltpu.VMEM)
+    return pl.pallas_call(
+        functools.partial(finish_body, float(total), count),
+        out_shape=(jax.ShapeDtypeStruct((2, count), jnp.float32), jax.ShapeDtypeStruct((1, 1), jnp.float32)),
+        in_specs=[vmem, vmem],
+        out_specs=(vmem, vmem),
+        name="finish",
+    )(part, sums)
 
 
 def shards(layer_one, layer_two, spread):
@@ -110,28 +153,12 @@
     near = [shift(own, 1, 0), shift(own, -1, 0), shift(own, 2, 0)]
     strip = jnp.concatenate([own] + near, axis=1)
     pieces = [strip, shift(strip, 0, 1), shift(strip, 0, -1), shift(strip, 0, 2)]
-    part = gram(spread, line, pieces)
-    part = part + move(part, lambda x, y, z, core: (x, y, z, core ^ 1))
-    for bit in (1, 2, 4):
-        part = part + move(part, lambda x, y, z, core: (x, y, z ^ bit, core))
-    total = count * lax.axis_size(AXES)
+    part = line_sum(gram(spread, line, pieces))
     r_one, r_two = part[0], part[1]
-    scalars = jnp.stack(
-        [r_one, r_two, part[2], part[3], part[4], r_one * r_two, r_one * r_one, r_two * r_two]
-    )
-    scalars = jnp.sum(scalars.reshape(8, part.shape[1] // 128, 128), axis=1)
-    scalars = scalars + move(scalars, lambda x, y, z, core: (x ^ 1, y, z, core))
-    scalars = scalars + move(scalars, lambda x, y, z, core: (x ^ 2, y, z, core))
-    scalars = lax.psum(scalars, "y")
-    scalars = jnp.sum(scalars, axis=1)
-    sum_one, sum_two, f_cross, f_one, f_two, c_cross, c_one, c_two = (scalars[at] for at in range(8))
-    h_cross = f_cross - 2.0 * c_cross / total + sum_one * sum_two / (total * total)
-    h_one = f_one - 2.0 * c_one / total + sum_one * sum_one / (total * total)
-    h_two = f_two - 2.0 * c_two / total + sum_two * sum_two / (total * total)
-    alignment = h_cross / jnp.sqrt(h_one * h_two)
-    mine = lax.dynamic_slice(part, (0, lax.axis_index(LINE) * count), (2, count))
-    profiles = mine / jnp.sqrt(jnp.stack([c_one, c_two]) / total)[:, None]
-    return (profiles, alignment)
+    sums = jnp.stack([r_one, r_two, part[2], part[3], part[4], r_one * r_two, r_one * r_one, r_two * r_two])
+    sums = plane_sum(jnp.sum(sums.reshape(8, part.shape[1] // 128, 128), axis=1))
+    profiles, alignment = finish(part, sums, count * lax.axis_size(AXES), count)
+    return (profiles, alignment.reshape(()))
 
 
 def solution(mesh):

time: 122 us -> 113 us (0.926)
  blocking collectives: 10.4 us -> 0 us
  between operations: 22.8 us -> 14.1 us
  starting transfers between devices: 20.2 us -> 26.9 us
  waiting for transfers between devices: 49.6 us -> 51.5 us
  Pallas kernels: 10.4 us -> 11.8 us
    psum x1 -> x0, blocking collectives: 10.4 us -> none  [shards(): scalars = lax.psum(scalars, 'y')]
    ppermute x12 -> x17, starting transfers between devices: 20.2 us -> 26.9 us  [move(): return lax.ppermute(array, AXES, pairs)]
    pallas_call x0 -> x1, Pallas kernels: none -> 1.47 us  [finish(): pl.pallas_call(functools.partial(finish_body, float(total), count), out_s...]
    ppermute x12 -> x17, waiting for transfers between devices: 42.5 us -> 43.9 us  [move(): return lax.ppermute(array, AXES, pairs)]
    unnamed x8 -> x10, local copies, waits for them, and re-layouts: 4.13 us -> 4.17 us
  transfers between devices with their start and end apart: 13 -> 18, of which waited for: 12 -> 14; matrix products, arithmetic and copies ran while one was open for 1% -> 1% of each run, Pallas kernels for 0% -> 0%
where the time goes in v2:
time: 113 us; the launch traced here: 112 us
  waiting for transfers between devices  51.5 us (46%)
  starting transfers between devices  26.9 us (24%)
  between operations  14.1 us (12%)
  Pallas kernels  11.8 us (10%)
  local copies, waits for them, and re-layouts  4.18 us (4%)
  other arithmetic  3.38 us (3%)
    ppermute x17, waiting for transfers between devices, move(): return lax.ppermute(array, AXES, pairs)  43.9 us
    ppermute x17, starting transfers between devices, move(): return lax.ppermute(array, AXES, pairs)  26.9 us
    pallas_call x1, Pallas kernels, gram(): pl.pallas_call(gram_body, out_shape=jax.ShapeDtypeStruct((8, width), jnp....  10.3 us
    all_gather x1, waiting for transfers between devices, shards(): line = lax.all_gather(own, LINE, axis=1, tiled=True)  7.57 us
    unnamed x10, local copies, waits for them, and re-layouts  4.17 us
  transfers between devices with their start and end apart: 18, of which 14 were waited for; matrix products, arithmetic and copies ran while one was open for 1% of the time, Pallas kernels for 0%

profile of v2, /device:TPU:6, one launch (start us, length us, event | category | flops | bytes accessed | tf_op | source)
XLA Modules:
  0.0 111.9 jit_solution(5757804923358612470)
XLA Ops:
  7.2 1.7 %pad_maximum_fusion.1 = bf16[2,56,1024]{2,1,0:T(8,128)(2,1)} fusion(bf16[1,56,1024]{2,1,0:T(8,128)(2,1)} %bitcast.7, bf16[1,56,1024]{2,1,0:T(8,128)(2,1)} %bitcast.9), kind=kLoop, calls=%fused_computation.1 | loop fusion | flops 114688 | bytes 458752 | tf_op jit(solution)/shard_map/stack | solution.py:150
  8.9 1.5 %collective-permute-start.2 = (bf16[2,56,1024]{2,1,0:T(8,128)(2,1)}, bf16[2,56,1024]{2,1,0:T(8,128)(2,1)S(1)}, u32[]{:S(2)}, u32[]{:S(2)}) collective-permute-start(bf16[2,56,1024]{2,1,0:T(8,128)(2,1)} %pad_maximum_fusion.1), channel_id=1, source_target_pairs={{0,128},{2,10},{16,144},{18,26},{32,160},{34,42},{48,176},{50,58},... | collective-permute-start | bytes 688136 | tf_op jit(solution)/shard_map/ppermute | solution.py:31
  10.4 1.7 %collective-permute-start.1 = (bf16[2,56,1024]{2,1,0:T(8,128)(2,1)}, bf16[2,56,1024]{2,1,0:T(8,128)(2,1)S(1)}, u32[]{:S(2)}, u32[]{:S(2)}) collective-permute-start(bf16[2,56,1024]{2,1,0:T(8,128)(2,1)} %pad_maximum_fusion.1), channel_id=1, source_target_pairs={{0,129},{2,14},{16,145},{18,30},{32,161},{34,46},{48,177},{50,62},... | collective-permute-start | bytes 688136 | tf_op jit(solution)/shard_map/ppermute | solution.py:31
  12.1 1.6 %collective-permute-start = (bf16[2,56,1024]{2,1,0:T(8,128)(2,1)}, bf16[2,56,1024]{2,1,0:T(8,128)(2,1)S(1)}, u32[]{:S(2)}, u32[]{:S(2)}) collective-permute-start(bf16[2,56,1024]{2,1,0:T(8,128)(2,1)} %pad_maximum_fusion.1), channel_id=1, source_target_pairs={{0,1},{2,6},{16,17},{18,22},{32,33},{34,38},{48,49},{50,54},{64,65... | collective-permute-start | bytes 688136 | tf_op jit(solution)/shard_map/ppermute | solution.py:31
  13.7 3.2 %collective-permute-done.2 = bf16[2,56,1024]{2,1,0:T(8,128)(2,1)S(1)} collective-permute-done((bf16[2,56,1024]{2,1,0:T(8,128)(2,1)}, bf16[2,56,1024]{2,1,0:T(8,128)(2,1)S(1)}, u32[]{:S(2)}, u32[]{:S(2)}) %collective-permute-start.2) | collective-permute-done | bytes 229408 | tf_op jit(solution)/shard_map/ppermute | solution.py:31
  16.9 2.4 %collective-permute-done.1 = bf16[2,56,1024]{2,1,0:T(8,128)(2,1)S(1)} collective-permute-done((bf16[2,56,1024]{2,1,0:T(8,128)(2,1)}, bf16[2,56,1024]{2,1,0:T(8,128)(2,1)S(1)}, u32[]{:S(2)}, u32[]{:S(2)}) %collective-permute-start.1) | collective-permute-done | bytes 229408 | tf_op jit(solution)/shard_map/ppermute | solution.py:31
  19.2 1.0 pad_maximum_fusion.refs_0_
  20.2 3.3 %collective-permute-start.5 = (bf16[2,224,1024]{2,1,0:T(8,128)(2,1)S(1)}, bf16[2,224,1024]{2,1,0:T(8,128)(2,1)S(1)}, u32[]{:S(2)}, u32[]{:S(2)}) collective-permute-start(bf16[2,224,1024]{2,1,0:T(8,128)(2,1)S(1)} %pad_maximum_fusion.refs_0_), channel_id=1, source_target_pairs={{0,8},{2,130},{16,24},{18,146},{32,40},{34,162},{48,56},{50,178},{... | collective-permute-start | bytes 2752520 | tf_op jit(solution)/shard_map/ppermute | solution.py:31
  23.5 1.1 collective-permute-start.4
  24.6 1.0 collective-permute-start.3
  25.5 9.8 %collective-permute-done.5.refs_3_ = bf16[2,224,1024]{2,1,0:T(8,128)(2,1)S(1)} collective-permute-done((bf16[2,224,1024]{2,1,0:T(8,128)(2,1)S(1)}, bf16[2,224,1024]{2,1,0:T(8,128)(2,1)S(1)}, u32[]{:S(2)}, u32[]{:S(2)}) %collective-permute-start.5) | collective-permute-done | bytes 917536 | tf_op jit(solution)/shard_map/ppermute | solution.py:31
  35.3 10.1 %collective-permute-done.4.refs_2_ = bf16[2,224,1024]{2,1,0:T(8,128)(2,1)S(1)} collective-permute-done((bf16[2,224,1024]{2,1,0:T(8,128)(2,1)S(1)}, bf16[2,224,1024]{2,1,0:T(8,128)(2,1)S(1)}, u32[]{:S(2)}, u32[]{:S(2)}) %collective-permute-start.4) | collective-permute-done | bytes 917536 | tf_op jit(solution)/shard_map/ppermute | solution.py:31
  45.4 0.9 copy-done.1
  46.4 7.6 %all-gather.2.cloned.1.call-done.z_ref = bf16[2,896,1024]{2,1,0:T(8,128)(2,1)} async-done(((bf16[2,56,1024]{2,1,0:T(8,128)(2,1)}), bf16[2,896,1024]{2,1,0:T(8,128)(2,1)}) %all-gather.2.cloned.1.call-update) | async-done | bytes 3670032 | tf_op jit(solution)/shard_map/all_gather | solution.py:152
  54.0 2.0 %copy-done = bf16[2,896,1024]{2,1,0:T(8,128)(2,1)S(1)} copy-done((bf16[2,896,1024]{2,1,0:T(8,128)(2,1)S(1)}, bf16[2,896,1024]{2,1,0:T(8,128)(2,1)}, u32[]{:S(2)}) %copy-start) | copy-done | bytes 3670040
  56.0 1.2 %copy-done.2 = bf16[2,224,1024]{2,1,0:T(8,128)(2,1)S(1)} copy-done((bf16[2,224,1024]{2,1,0:T(8,128)(2,1)S(1)}, bf16[2,224,1024]{2,1,0:T(8,128)(2,1)}, u32[]{:S(2)}) %copy-start.2) | copy-done | bytes 917528
  57.2 10.3 %gram.1 = f32[8,896]{1,0:T(8,128)S(1)} custom-call(s32[2]{0:T(128)S(1)} %copy-done.3, bf16[2,896,1024]{2,1,0:T(8,128)(2,1)S(1)} %copy-done, bf16[2,224,1024]{2,1,0:T(8,128)(2,1)S(1)} %pad_maximum_fusion.refs_0_, bf16[2,224,1024]{2,1,0:T(8,128)(2,1)S(1)} %copy-done.2, bf16[2,224,1024]{2,1,0:T(8,128)(2,1)S(1)} %collective-permute-done.4.refs_2_, ...), custom_call_target="tpu_custom_call" | custom-call | flops 3288334336 | bytes 7340032 | tf_op jit(solution)/shard_map/gram/pallas_call | solution.py:92
  68.0 1.0 collective-permute-done.6
  69.0 1.8 %collective-permute-start.7 = (f32[8,896]{1,0:T(8,128)S(1)}, f32[8,896]{1,0:T(8,128)S(1)}, u32[]{:S(2)}, u32[]{:S(2)}) collective-permute-start(f32[8,896]{1,0:T(8,128)S(1)} %add.33), channel_id=1, source_target_pairs={{0,16},{2,18},{16,0},{18,2},{32,48},{34,50},{48,32},{50,34},{64,80... | collective-permute-start | bytes 86024 | tf_op jit(solution)/shard_map/ppermute | solution.py:31
  70.8 2.0 %collective-permute-done.7 = f32[8,896]{1,0:T(8,128)S(1)} collective-permute-done((f32[8,896]{1,0:T(8,128)S(1)}, f32[8,896]{1,0:T(8,128)S(1)}, u32[]{:S(2)}, u32[]{:S(2)}) %collective-permute-start.7) | collective-permute-done | bytes 28704 | tf_op jit(solution)/shard_map/ppermute | solution.py:31
  72.9 2.0 %collective-permute-start.8 = (f32[8,896]{1,0:T(8,128)S(1)}, f32[8,896]{1,0:T(8,128)S(1)}, u32[]{:S(2)}, u32[]{:S(2)}) collective-permute-start(f32[8,896]{1,0:T(8,128)S(1)} %add.34), channel_id=1, source_target_pairs={{0,32},{2,34},{16,48},{18,50},{32,0},{34,2},{48,16},{50,18},{64,96... | collective-permute-start | bytes 86024 | tf_op jit(solution)/shard_map/ppermute | solution.py:31
  74.8 2.8 %collective-permute-done.8 = f32[8,896]{1,0:T(8,128)S(1)} collective-permute-done((f32[8,896]{1,0:T(8,128)S(1)}, f32[8,896]{1,0:T(8,128)S(1)}, u32[]{:S(2)}, u32[]{:S(2)}) %collective-permute-start.8) | collective-permute-done | bytes 28704 | tf_op jit(solution)/shard_map/ppermute | solution.py:31
  77.7 3.5 %collective-permute-start.9 = (f32[8,896]{1,0:T(8,128)S(1)}, f32[8,896]{1,0:T(8,128)S(1)}, u32[]{:S(2)}, u32[]{:S(2)}) collective-permute-start(f32[8,896]{1,0:T(8,128)S(1)} %add.35), channel_id=1, source_target_pairs={{0,64},{2,66},{16,80},{18,82},{32,96},{34,98},{48,112},{50,114},{6... | collective-permute-start | bytes 86024 | tf_op jit(solution)/shard_map/ppermute | solution.py:31
  81.2 4.3 %collective-permute-done.9 = f32[8,896]{1,0:T(8,128)S(1)} collective-permute-done((f32[8,896]{1,0:T(8,128)S(1)}, f32[8,896]{1,0:T(8,128)S(1)}, u32[]{:S(2)}, u32[]{:S(2)}) %collective-permute-start.9) | collective-permute-done | bytes 28704 | tf_op jit(solution)/shard_map/ppermute | solution.py:31
  86.5 2.4 %collective-permute-start.11 = (f32[8,128]{1,0:T(8,128)S(1)}, f32[8,128]{1,0:T(8,128)S(1)}, u32[]{:S(2)}, u32[]{:S(2)}) collective-permute-start(f32[8,128]{1,0:T(8,128)S(1)} %maximum_reduce_fusion), channel_id=1, source_target_pairs={{0,1},{2,6},{16,17},{18,22},{32,33},{34,38},{48,49},{50,54},{64,65... | collective-permute-start | bytes 12296 | tf_op jit(solution)/shard_map/ppermute | solution.py:31
  89.1 1.3 %collective-permute-done.12 = f32[8,128]{1,0:T(8,128)S(1)} collective-permute-done((f32[8,128]{1,0:T(8,128)S(1)}, f32[8,128]{1,0:T(8,128)S(1)}, u32[]{:S(2)}, u32[]{:S(2)}) %collective-permute-start.12) | collective-permute-done | bytes 4128 | tf_op jit(solution)/shard_map/ppermute | solution.py:31
  90.4 3.5 %collective-permute-done.10 = f32[8,128]{1,0:T(8,128)S(1)} collective-permute-done((f32[8,128]{1,0:T(8,128)S(1)}, f32[8,128]{1,0:T(8,128)S(1)}, u32[]{:S(2)}, u32[]{:S(2)}) %collective-permute-start.10) | collective-permute-done | bytes 4128 | tf_op jit(solution)/shard_map/ppermute | solution.py:31
  94.0 2.7 %collective-permute-start.15 = (f32[8,128]{1,0:T(8,128)S(1)}, f32[8,128]{1,0:T(8,128)S(1)}, u32[]{:S(2)}, u32[]{:S(2)}) collective-permute-start(f32[8,128]{1,0:T(8,128)S(1)} %add_add_fusion.1), channel_id=1, source_target_pairs={{0,12},{2,131},{16,28},{18,147},{32,44},{34,163},{48,60},{50,179},... | collective-permute-start | bytes 12296 | tf_op jit(solution)/shard_map/ppermute | solution.py:31
  96.7 2.7 %collective-permute-start.13 = (f32[8,128]{1,0:T(8,128)S(1)}, f32[8,128]{1,0:T(8,128)S(1)}, u32[]{:S(2)}, u32[]{:S(2)}) collective-permute-start(f32[8,128]{1,0:T(8,128)S(1)} %add_add_fusion.1), channel_id=1, source_target_pairs={{0,8},{2,130},{16,24},{18,146},{32,40},{34,162},{48,56},{50,178},{... | collective-permute-start | bytes 12296 | tf_op jit(solution)/shard_map/ppermute | solution.py:31
  99.4 2.1 %collective-permute-done.14 = f32[8,128]{1,0:T(8,128)S(1)} collective-permute-done((f32[8,128]{1,0:T(8,128)S(1)}, f32[8,128]{1,0:T(8,128)S(1)}, u32[]{:S(2)}, u32[]{:S(2)}) %collective-permute-start.14) | collective-permute-done | bytes 4128 | tf_op jit(solution)/shard_map/ppermute | solution.py:31
  101.8 1.2 %collective-permute-done.16 = f32[8,128]{1,0:T(8,128)S(1)} collective-permute-done((f32[8,128]{1,0:T(8,128)S(1)}, f32[8,128]{1,0:T(8,128)S(1)}, u32[]{:S(2)}, u32[]{:S(2)}) %collective-permute-start.16) | collective-permute-done | bytes 4128 | tf_op jit(solution)/shard_map/ppermute | solution.py:31
  103.6 1.5 %finish.1 = (f32[2,56]{1,0:T(2,128)}, f32[1,1]{1,0:T(1,128)}) custom-call(f32[8,896]{1,0:T(8,128)} %copy-done.4, f32[8,128]{1,0:T(8,128)} %add_multiply_fusion.sums_ref), custom_call_target="tpu_custom_call" | custom-call | tf_op jit(solution)/shard_map/finish/pallas_call | solution.py:140
  (29 shorter events, 2.8 us)
Async XLA Ops:
  7.2 46.8 %copy-start.3 = (s32[2]{0:T(128)S(1)}, s32[2]{0:T(128)}, u32[]{:S(2)}) copy-start(s32[2]{0:T(128)} %spread_ref.1) | copy-start | bytes 28
  7.2 46.8 %all-gather.2.cloned.1.call-start = ((), (), s32[]{:S(2)}) async-start(), calls=%async_computation | async-start | bytes 3899392 | tf_op jit(solution)/shard_map/all_gather | solution.py:152
  8.9 7.9 %collective-permute-start.2 = (bf16[2,56,1024]{2,1,0:T(8,128)(2,1)}, bf16[2,56,1024]{2,1,0:T(8,128)(2,1)S(1)}, u32[]{:S(2)}, u32[]{:S(2)}) collective-permute-start(bf16[2,56,1024]{2,1,0:T(8,128)(2,1)} %pad_maximum_fusion.1), channel_id=1, source_target_pairs={{0,128},{2,10},{16,144},{18,26},{32,160},{34,42},{48,176},{50,58},... | collective-permute-start | bytes 688136 | tf_op jit(solution)/shard_map/ppermute | solution.py:31
  10.4 8.8 %collective-permute-start.1 = (bf16[2,56,1024]{2,1,0:T(8,128)(2,1)}, bf16[2,56,1024]{2,1,0:T(8,128)(2,1)S(1)}, u32[]{:S(2)}, u32[]{:S(2)}) collective-permute-start(bf16[2,56,1024]{2,1,0:T(8,128)(2,1)} %pad_maximum_fusion.1), channel_id=1, source_target_pairs={{0,129},{2,14},{16,145},{18,30},{32,161},{34,46},{48,177},{50,62},... | collective-permute-start | bytes 688136 | tf_op jit(solution)/shard_map/ppermute | solution.py:31
  12.1 7.1 %collective-permute-start = (bf16[2,56,1024]{2,1,0:T(8,128)(2,1)}, bf16[2,56,1024]{2,1,0:T(8,128)(2,1)S(1)}, u32[]{:S(2)}, u32[]{:S(2)}) collective-permute-start(bf16[2,56,1024]{2,1,0:T(8,128)(2,1)} %pad_maximum_fusion.1), channel_id=1, source_target_pairs={{0,1},{2,6},{16,17},{18,22},{32,33},{34,38},{48,49},{50,54},{64,65... | collective-permute-start | bytes 688136 | tf_op jit(solution)/shard_map/ppermute | solution.py:31
  20.2 15.1 %collective-permute-start.5 = (bf16[2,224,1024]{2,1,0:T(8,128)(2,1)S(1)}, bf16[2,224,1024]{2,1,0:T(8,128)(2,1)S(1)}, u32[]{:S(2)}, u32[]{:S(2)}) collective-permute-start(bf16[2,224,1024]{2,1,0:T(8,128)(2,1)S(1)} %pad_maximum_fusion.refs_0_), channel_id=1, source_target_pairs={{0,8},{2,130},{16,24},{18,146},{32,40},{34,162},{48,56},{50,178},{... | collective-permute-start | bytes 2752520 | tf_op jit(solution)/shard_map/ppermute | solution.py:31
  23.5 21.9 %collective-permute-start.4 = (bf16[2,224,1024]{2,1,0:T(8,128)(2,1)S(1)}, bf16[2,224,1024]{2,1,0:T(8,128)(2,1)S(1)}, u32[]{:S(2)}, u32[]{:S(2)}) collective-permute-start(bf16[2,224,1024]{2,1,0:T(8,128)(2,1)S(1)} %pad_maximum_fusion.refs_0_), channel_id=1, source_target_pairs={{0,12},{2,131},{16,28},{18,147},{32,44},{34,163},{48,60},{50,179},... | collective-permute-start | bytes 2752520 | tf_op jit(solution)/shard_map/ppermute | solution.py:31
  24.6 20.9 %collective-permute-start.3 = (bf16[2,224,1024]{2,1,0:T(8,128)(2,1)S(1)}, bf16[2,224,1024]{2,1,0:T(8,128)(2,1)S(1)}, u32[]{:S(2)}, u32[]{:S(2)}) collective-permute-start(bf16[2,224,1024]{2,1,0:T(8,128)(2,1)S(1)} %pad_maximum_fusion.refs_0_), channel_id=1, source_target_pairs={{0,4},{2,3},{16,20},{18,19},{32,36},{34,35},{48,52},{50,51},{64,68... | collective-permute-start | bytes 2752520 | tf_op jit(solution)/shard_map/ppermute | solution.py:31
  45.4 0.9 copy-start.1
  54.0 2.0 %copy-start = (bf16[2,896,1024]{2,1,0:T(8,128)(2,1)S(1)}, bf16[2,896,1024]{2,1,0:T(8,128)(2,1)}, u32[]{:S(2)}) copy-start(bf16[2,896,1024]{2,1,0:T(8,128)(2,1)} %all-gather.2.cloned.1.call-done.z_ref) | copy-start | bytes 11010052
  56.0 1.2 %copy-start.2 = (bf16[2,224,1024]{2,1,0:T(8,128)(2,1)S(1)}, bf16[2,224,1024]{2,1,0:T(8,128)(2,1)}, u32[]{:S(2)}) copy-start(bf16[2,224,1024]{2,1,0:T(8,128)(2,1)} %copy-done.1) | copy-start | bytes 2752516
  67.5 1.5 %collective-permute-start.6 = (f32[8,896]{1,0:T(8,128)S(1)}, f32[8,896]{1,0:T(8,128)S(1)}, u32[]{:S(2)}, u32[]{:S(2)}) collective-permute-start(f32[8,896]{1,0:T(8,128)S(1)} %gram.1), channel_id=1, source_target_pairs={{0,2},{2,0},{16,18},{18,16},{32,34},{34,32},{48,50},{50,48},{64,66... | collective-permute-start | bytes 86024 | tf_op jit(solution)/shard_map/ppermute | solution.py:31
  69.0 3.9 %collective-permute-start.7 = (f32[8,896]{1,0:T(8,128)S(1)}, f32[8,896]{1,0:T(8,128)S(1)}, u32[]{:S(2)}, u32[]{:S(2)}) collective-permute-start(f32[8,896]{1,0:T(8,128)S(1)} %add.33), channel_id=1, source_target_pairs={{0,16},{2,18},{16,0},{18,2},{32,48},{34,50},{48,32},{50,34},{64,80... | collective-permute-start | bytes 86024 | tf_op jit(solution)/shard_map/ppermute | solution.py:31
  72.9 4.8 %collective-permute-start.8 = (f32[8,896]{1,0:T(8,128)S(1)}, f32[8,896]{1,0:T(8,128)S(1)}, u32[]{:S(2)}, u32[]{:S(2)}) collective-permute-start(f32[8,896]{1,0:T(8,128)S(1)} %add.34), channel_id=1, source_target_pairs={{0,32},{2,34},{16,48},{18,50},{32,0},{34,2},{48,16},{50,18},{64,96... | collective-permute-start | bytes 86024 | tf_op jit(solution)/shard_map/ppermute | solution.py:31
  77.7 7.8 %collective-permute-start.9 = (f32[8,896]{1,0:T(8,128)S(1)}, f32[8,896]{1,0:T(8,128)S(1)}, u32[]{:S(2)}, u32[]{:S(2)}) collective-permute-start(f32[8,896]{1,0:T(8,128)S(1)} %add.35), channel_id=1, source_target_pairs={{0,64},{2,66},{16,80},{18,82},{32,96},{34,98},{48,112},{50,114},{6... | collective-permute-start | bytes 86024 | tf_op jit(solution)/shard_map/ppermute | solution.py:31
  85.4 18.2 %copy-start.4 = (f32[8,896]{1,0:T(8,128)}, f32[8,896]{1,0:T(8,128)S(1)}, u32[]{:S(2)}) copy-start(f32[8,896]{1,0:T(8,128)S(1)} %add.36.part_ref) | copy-start | bytes 86020
  85.5 4.9 %collective-permute-start.12 = (f32[8,128]{1,0:T(8,128)S(1)}, f32[8,128]{1,0:T(8,128)S(1)}, u32[]{:S(2)}, u32[]{:S(2)}) collective-permute-start(f32[8,128]{1,0:T(8,128)S(1)} %maximum_reduce_fusion), channel_id=1, source_target_pairs={{0,129},{2,14},{16,145},{18,30},{32,161},{34,46},{48,177},{50,62},... | collective-permute-start | bytes 12296 | tf_op jit(solution)/shard_map/ppermute | solution.py:31
  86.5 4.0 %collective-permute-start.11 = (f32[8,128]{1,0:T(8,128)S(1)}, f32[8,128]{1,0:T(8,128)S(1)}, u32[]{:S(2)}, u32[]{:S(2)}) collective-permute-start(f32[8,128]{1,0:T(8,128)S(1)} %maximum_reduce_fusion), channel_id=1, source_target_pairs={{0,1},{2,6},{16,17},{18,22},{32,33},{34,38},{48,49},{50,54},{64,65... | collective-permute-start | bytes 12296 | tf_op jit(solution)/shard_map/ppermute | solution.py:31
  88.8 5.1 %collective-permute-start.10 = (f32[8,128]{1,0:T(8,128)S(1)}, f32[8,128]{1,0:T(8,128)S(1)}, u32[]{:S(2)}, u32[]{:S(2)}) collective-permute-start(f32[8,128]{1,0:T(8,128)S(1)} %maximum_reduce_fusion), channel_id=1, source_target_pairs={{0,128},{2,10},{16,144},{18,26},{32,160},{34,42},{48,176},{50,58},... | collective-permute-start | bytes 12296 | tf_op jit(solution)/shard_map/ppermute | solution.py:31
  94.0 5.5 %collective-permute-start.15 = (f32[8,128]{1,0:T(8,128)S(1)}, f32[8,128]{1,0:T(8,128)S(1)}, u32[]{:S(2)}, u32[]{:S(2)}) collective-permute-start(f32[8,128]{1,0:T(8,128)S(1)} %add_add_fusion.1), channel_id=1, source_target_pairs={{0,12},{2,131},{16,28},{18,147},{32,44},{34,163},{48,60},{50,179},... | collective-permute-start | bytes 12296 | tf_op jit(solution)/shard_map/ppermute | solution.py:31
  96.7 4.8 %collective-permute-start.14 = (f32[8,128]{1,0:T(8,128)S(1)}, f32[8,128]{1,0:T(8,128)S(1)}, u32[]{:S(2)}, u32[]{:S(2)}) collective-permute-start(f32[8,128]{1,0:T(8,128)S(1)} %add_add_fusion.1), channel_id=1, source_target_pairs={{0,4},{2,3},{16,20},{18,19},{32,36},{34,35},{48,52},{50,51},{64,68... | collective-permute-start | bytes 12296 | tf_op jit(solution)/shard_map/ppermute | solution.py:31
  96.7 5.1 %collective-permute-start.13 = (f32[8,128]{1,0:T(8,128)S(1)}, f32[8,128]{1,0:T(8,128)S(1)}, u32[]{:S(2)}, u32[]{:S(2)}) collective-permute-start(f32[8,128]{1,0:T(8,128)S(1)} %add_add_fusion.1), channel_id=1, source_target_pairs={{0,8},{2,130},{16,24},{18,146},{32,40},{34,162},{48,56},{50,178},{... | collective-permute-start | bytes 12296 | tf_op jit(solution)/shard_map/ppermute | solution.py:31
  101.8 1.2 %collective-permute-start.16 = (f32[8,128]{1,0:T(8,128)S(1)}, f32[8,128]{1,0:T(8,128)S(1)}, u32[]{:S(2)}, u32[]{:S(2)}) collective-permute-start(f32[8,128]{1,0:T(8,128)S(1)} %add_add_fusion), channel_id=1, source_target_pairs={{0,2},{2,0},{16,18},{18,16},{32,34},{34,32},{48,50},{50,48},{64,66... | collective-permute-start | bytes 12296 | tf_op jit(solution)/shard_map/ppermute | solution.py:31
Sparse Core Ops, SparseCore 0:
  9.9 44.0 all-gather.1

commit v3 on v2

--- a/solution.py
+++ b/solution.py
@@ -11,7 +11,6 @@
 
 D = 1024
 AXES = ("x_hi", "z", "y", "core", "x_lo")
-LINE = ("z", "core")
 NX, NY, NZ, NC = (4, 4, 8, 2)
 LOG2E = math.log2(math.e)
 
@@ -39,72 +38,104 @@
     return move(array, where)
 
 
-def gram_body(spread_ref, z_ref, *refs):
-    pieces, out_ref, scaled_ref = refs[:-2], refs[-2], refs[-1]
+def fold_squares(rows):
+    wide = rows.astype(jnp.float32)
+    square = wide * wide
+    folded = square[:, :128]
+    for lane in range(128, D, 128):
+        folded = folded + square[:, lane : lane + 128]
+    return folded
+
+
+def shuffled(array, moves, unit):
+    lanes = lax.broadcasted_iota(jnp.int32, array.shape, 1)
+    width = array.shape[1]
+    result = array
+    by_step = {}
+    for old, fresh in moves.items():
+        by_step.setdefault(fresh - old, []).append(fresh)
+    for step, places in by_step.items():
+        if step == 0:
+            continue
+        rolled = pltpu.roll(array, (step * unit) % width, 1)
+        for place in places:
+            inside = (lanes >= place * unit) & (lanes < (place + 1) * unit)
+            result = jnp.where(inside, rolled, result)
+    return result
+
+
+def gram_body(n_line, spread_ref, *refs):
+    line, pieces = refs[:n_line], refs[n_line:-3]
+    out_ref, z_ref, norm_ref = refs[-3:]
     width = z_ref.shape[1]
-    scales = [spread_ref[0].astype(jnp.float32), spread_ref[1].astype(jnp.float32)]
-    factors = []
-    offsets = []
-    for layer in range(2):
-        scale = jnp.full((1, 128), scales[layer], jnp.float32)
-        factors.append((LOG2E / scale)[:, :1])
-        offsets.append(jnp.exp(-D / scale)[:, :1])
-        for start in range(0, width, 128):
-            rows = z_ref[layer, start : start + 128, :].astype(jnp.float32)
-            square = rows * rows
-            folded = square[:, :128]
-            for lane in range(128, D, 128):
-                folded = folded + square[:, lane : lane + 128]
-            sums = jnp.sum(folded.T, axis=0, keepdims=True)
-            scaled_ref[layer : layer + 1, start : start + 128] = sums * (0.5 * factors[layer])
-    sums = [jnp.zeros((8, width), jnp.float32) for _ in range(5)]
-
-    def fold(array):
-        parts = array.reshape(array.shape[0] // 8, 8, width)
-        return jnp.sum(parts, axis=0)
-
-    for piece in pieces:
-        tall = piece.shape[1]
-        step = 112 if tall % 112 == 0 else tall
-        for start in range(0, tall, step):
+    tall = pieces[0].shape[1]
+    lanes = 128
+    scales = [jnp.full((1, lanes), spread_ref[layer].astype(jnp.float32), jnp.float32) for layer in range(2)]
+    factors = [LOG2E / scale for scale in scales]
+    offsets = [jnp.exp(-D / scale) for scale in scales]
+    at = 0
+    for ref in line:
+        z_ref[:, at : at + ref.shape[1], :] = ref[...]
+        at += ref.shape[1]
+    for index, piece in enumerate(pieces):
+        for layer in range(2):
+            norms = jnp.sum(fold_squares(piece[layer]), axis=1, keepdims=True)
+            rows = slice(index * tall, (index + 1) * tall)
+            norm_ref[layer, rows, :] = jnp.broadcast_to(norms, (tall, lanes)) * (0.5 * factors[layer])
+    columns = []
+    for start in range(0, width, lanes):
+        z = [z_ref[layer, start : start + lanes, :] for layer in range(2)]
+        z_norms = [
+            jnp.sum(fold_squares(z[layer]).T, axis=0, keepdims=True) * (0.5 * factors[layer]) for layer in range(2)
+        ]
+        sums = [jnp.zeros((8, lanes), jnp.float32) for _ in range(5)]
+        for index, piece in enumerate(pieces):
             kernels = []
             for layer in range(2):
-                rows = piece[layer, start : start + step, :]
                 inner = lax.dot_general(
-                    rows, z_ref[layer], (((1,), (1,)), ((), ())), preferred_element_type=jnp.float32
+                    piece[layer], z[layer], (((1,), (1,)), ((), ())), preferred_element_type=jnp.float32
                 )
-                wide = rows.astype(jnp.float32)
-                norms = jnp.sum(wide * wide, axis=1, keepdims=True) * (0.5 * factors[layer])
-                power = inner * factors[layer] - norms - scaled_ref[layer : layer + 1, :]
-                kernels.append(jnp.exp2(power) - offsets[layer])
+                norms = norm_ref[layer, index * tall : (index + 1) * tall, :]
+                kernels.append(jnp.exp2(inner * factors[layer] - norms - z_norms[layer]) - offsets[layer])
             one, two = kernels
-            for at, term in enumerate((one, two, one * two, one * one, two * two)):
-                sums[at] = sums[at] + fold(term)
-    for at in range(5):
-        out_ref[at : at + 1, :] = jnp.sum(sums[at], axis=0, keepdims=True)
-    out_ref[5:8, :] = jnp.zeros((3, width), jnp.float32)
+            for row, term in enumerate((one, two, one * two, one * one, two * two)):
+                sums[row] = sums[row] + jnp.sum(term.reshape(tall // 8, 8, lanes), axis=0)
+        rows = [jnp.sum(term, axis=0, keepdims=True) for term in sums]
+        columns.append(jnp.concatenate(rows + [jnp.zeros((3, lanes), jnp.float32)], axis=0))
+    local = jnp.concatenate(columns, axis=1)
+    count = width // (NZ * NC)
+    other = {0: 1, 1: 0, 14: 15, 15: 14}
+    other.update({place: place + 6 for place in range(2, 8)})
+    other.update({place: place - 6 for place in range(8, 14)})
+    local = jnp.where(lax.axis_index("core") == 0, local, shuffled(local, other, count))
+    near = {0: 0, 1: 1, 2: 14, 3: 15, 4: 12, 5: 13, 6: 10, 7: 11, 8: 3, 9: 2, 10: 5, 11: 4, 12: 7, 13: 6, 14: 8, 15: 9}
+    out_ref[...] = pltpu.roll(shuffled(local, near, count), lax.axis_index("z") * (NC * count), 1)
 
 
 def gram(spread, line, pieces):
-    width = line.shape[1]
     vmem = pl.BlockSpec(memory_space=pltpu.VMEM)
     rows = sum(piece.shape[1] for piece in pieces)
+    width = sum(part.shape[1] for part in line)
     return pl.pallas_call(
-        gram_body,
+        functools.partial(gram_body, len(line)),
         out_shape=jax.ShapeDtypeStruct((8, width), jnp.float32),
-        in_specs=[pl.BlockSpec(memory_space=pltpu.SMEM), vmem] + [vmem] * len(pieces),
+        in_specs=[pl.BlockSpec(memory_space=pltpu.SMEM)] + [vmem] * (len(line) + len(pieces)),
         out_specs=vmem,
-        scratch_shapes=[pltpu.VMEM((2, width), jnp.float32)],
-        compiler_params=pltpu.CompilerParams(vmem_limit_bytes=16 << 20),
+        scratch_shapes=[pltpu.VMEM((2, width, D), jnp.bfloat16), pltpu.VMEM((2, rows, 128), jnp.float32)],
+        compiler_params=pltpu.CompilerParams(vmem_limit_bytes=24 << 20),
         cost_estimate=pl.CostEstimate(
             flops=4 * rows * width * D, bytes_accessed=4 * (rows + width) * D, transcendentals=2 * rows * width
         ),
         name="gram",
-    )(spread, line, *pieces)
+    )(spread, *line, *pieces)
 
 
 def swap(array):
     return move(array, lambda x, y, z, core: (x, y, z, 1 - core))
+
+
+def around(array):
+    return move(array, lambda x, y, z, core: (x, y, z + 1 - 2 * core, core))
 
 
 def line_sum(array):
@@ -149,10 +180,18 @@
 def shards(layer_one, layer_two, spread):
     own = jnp.stack([layer_one, layer_two])
     count = own.shape[1]
-    line = lax.all_gather(own, LINE, axis=1, tiled=True)
-    near = [shift(own, 1, 0), shift(own, -1, 0), shift(own, 2, 0)]
+    chip = jnp.concatenate([own, swap(own)], axis=1)
+    near = [shift(own, step, 0) for step in (1, -1, 2)]
     strip = jnp.concatenate([own] + near, axis=1)
-    pieces = [strip, shift(strip, 0, 1), shift(strip, 0, -1), shift(strip, 0, 2)]
+    first, strip = lax.optimization_barrier((around(chip), strip))
+    pieces = [strip] + [shift(strip, 0, step) for step in (1, -1, 2)]
+    ring = [first]
+    for _ in range(2):
+        ring.append(around(ring[-1]))
+    last = around(ring[-1][:, :count])
+    pieces, late = lax.optimization_barrier((pieces, ring))
+    ends = jnp.concatenate([last, swap(last)], axis=1)
+    line = [chip] + ring + [swap(block) for block in late] + [ends]
     part = line_sum(gram(spread, line, pieces))
     r_one, r_two = part[0], part[1]
     sums = jnp.stack([r_one, r_two, part[2], part[3], part[4], r_one * r_two, r_one * r_one, r_two * r_two])

time: 113 us -> 108 us (0.956)
  the two profiles are of different devices: /device:TPU:6 before, /device:TPU:1 now
where the time goes in v3:
time: 108 us
  starting transfers between devices  53.4 us (49%)
  waiting for transfers between devices  40.6 us (38%)
  Pallas kernels  10.5 us (10%)
  other arithmetic  2.77 us (3%)
    ppermute x26, starting transfers between devices, move(): return lax.ppermute(array, AXES, pairs)  53.4 us
    ppermute x26, waiting for transfers between devices, move(): return lax.ppermute(array, AXES, pairs)  40.6 us
    pallas_call x1, Pallas kernels, gram(): pl.pallas_call(functools.partial(gram_body, len(line)), out_shape=jax.Sha...  9.03 us
  transfers between devices with their start and end apart: 26, of which 18 were waited for; matrix products, arithmetic and copies ran while one was open for 0% of the time, Pallas kernels for 0%

profile of v3, /device:TPU:1, one launch (start us, length us, event | category | flops | bytes accessed | tf_op | source)
XLA Modules:
  0.0 108.1 jit_solution(17774234323944671815)
XLA Ops:
  0.7 1.0 pad_maximum_fusion.3
  1.7 3.3 %collective-permute-start = (bf16[2,56,1024]{2,1,0:T(8,128)(2,1)S(1)}, bf16[2,56,1024]{2,1,0:T(8,128)(2,1)S(1)}, u32[]{:S(2)}, u32[]{:S(2)}) collective-permute-start(bf16[2,56,1024]{2,1,0:T(8,128)(2,1)S(1)} %pad_maximum_fusion.3), channel_id=1, source_target_pairs={{0,2},{2,0},{16,18},{18,16},{32,34},{34,32},{48,50},{50,48},{64,66... | collective-permute-start | bytes 688136 | tf_op jit(solution)/shard_map/ppermute | solution.py:30
  5.0 1.1 %collective-permute-done = bf16[2,56,1024]{2,1,0:T(8,128)(2,1)S(1)} collective-permute-done((bf16[2,56,1024]{2,1,0:T(8,128)(2,1)S(1)}, bf16[2,56,1024]{2,1,0:T(8,128)(2,1)S(1)}, u32[]{:S(2)}, u32[]{:S(2)}) %collective-permute-start) | collective-permute-done | bytes 229408 | tf_op jit(solution)/shard_map/ppermute | solution.py:30
  7.1 3.9 %collective-permute-start.1 = (bf16[2,112,1024]{2,1,0:T(8,128)(2,1)S(1)}, bf16[2,112,1024]{2,1,0:T(8,128)(2,1)S(1)}, u32[]{:S(2)}, u32[]{:S(2)}) collective-permute-start(bf16[2,112,1024]{2,1,0:T(8,128)(2,1)S(1)} %pad_maximum_fusion.1.refs_0_), channel_id=1, source_target_pairs={{0,16},{2,114},{16,32},{18,2},{32,48},{34,18},{48,64},{50,34},{64,... | collective-permute-start | bytes 1376264 | tf_op jit(solution)/shard_map/ppermute | solution.py:30
  11.0 2.7 %collective-permute-start.3 = (bf16[2,56,1024]{2,1,0:T(8,128)(2,1)S(1)}, bf16[2,56,1024]{2,1,0:T(8,128)(2,1)S(1)}, u32[]{:S(2)}, u32[]{:S(2)}) collective-permute-start(bf16[2,56,1024]{2,1,0:T(8,128)(2,1)S(1)} %pad_maximum_fusion.3), channel_id=1, source_target_pairs={{0,129},{2,14},{16,145},{18,30},{32,161},{34,46},{48,177},{50,62},... | collective-permute-start | bytes 688136 | tf_op jit(solution)/shard_map/ppermute | solution.py:30
  13.8 1.6 %collective-permute-start.4 = (bf16[2,56,1024]{2,1,0:T(8,128)(2,1)S(1)}, bf16[2,56,1024]{2,1,0:T(8,128)(2,1)S(1)}, u32[]{:S(2)}, u32[]{:S(2)}) collective-permute-start(bf16[2,56,1024]{2,1,0:T(8,128)(2,1)S(1)} %pad_maximum_fusion.3), channel_id=1, source_target_pairs={{0,128},{2,10},{16,144},{18,26},{32,160},{34,42},{48,176},{50,58},... | collective-permute-start | bytes 688136 | tf_op jit(solution)/shard_map/ppermute | solution.py:30
  15.4 1.3 %collective-permute-done.3 = bf16[2,56,1024]{2,1,0:T(8,128)(2,1)S(1)} collective-permute-done((bf16[2,56,1024]{2,1,0:T(8,128)(2,1)S(1)}, bf16[2,56,1024]{2,1,0:T(8,128)(2,1)S(1)}, u32[]{:S(2)}, u32[]{:S(2)}) %collective-permute-start.3) | collective-permute-done | bytes 229408 | tf_op jit(solution)/shard_map/ppermute | solution.py:30
  16.7 5.6 %collective-permute-done.2 = bf16[2,56,1024]{2,1,0:T(8,128)(2,1)S(1)} collective-permute-done((bf16[2,56,1024]{2,1,0:T(8,128)(2,1)S(1)}, bf16[2,56,1024]{2,1,0:T(8,128)(2,1)S(1)}, u32[]{:S(2)}, u32[]{:S(2)}) %collective-permute-start.2) | collective-permute-done | bytes 229408 | tf_op jit(solution)/shard_map/ppermute | solution.py:30
  22.4 1.1 %collective-permute-start.5 = (bf16[2,112,1024]{2,1,0:T(8,128)(2,1)S(1)}, bf16[2,112,1024]{2,1,0:T(8,128)(2,1)S(1)}, u32[]{:S(2)}, u32[]{:S(2)}) collective-permute-start(bf16[2,112,1024]{2,1,0:T(8,128)(2,1)S(1)} %collective-permute-done.1.refs_1_), channel_id=1, source_target_pairs={{0,16},{2,114},{16,32},{18,2},{32,48},{34,18},{48,64},{50,34},{64,... | collective-permute-start | bytes 1376264 | tf_op jit(solution)/shard_map/ppermute | solution.py:30
  23.5 2.4 %collective-permute-start.9 = (bf16[2,224,1024]{2,1,0:T(8,128)(2,1)S(1)}, bf16[2,224,1024]{2,1,0:T(8,128)(2,1)S(1)}, u32[]{:S(2)}, u32[]{:S(2)}) collective-permute-start(bf16[2,224,1024]{2,1,0:T(8,128)(2,1)S(1)} %pad_maximum_fusion.refs_8_), channel_id=1, source_target_pairs={{0,8},{2,130},{16,24},{18,146},{32,40},{34,162},{48,56},{50,178},{... | collective-permute-start | bytes 2752520 | tf_op jit(solution)/shard_map/ppermute | solution.py:30
  27.4 2.7 %collective-permute-done.5.refs_2_ = bf16[2,112,1024]{2,1,0:T(8,128)(2,1)S(1)} collective-permute-done((bf16[2,112,1024]{2,1,0:T(8,128)(2,1)S(1)}, bf16[2,112,1024]{2,1,0:T(8,128)(2,1)S(1)}, u32[]{:S(2)}, u32[]{:S(2)}) %collective-permute-start.5) | collective-permute-done | bytes 458784 | tf_op jit(solution)/shard_map/ppermute | solution.py:30
  30.1 2.2 %collective-permute-start.6 = (bf16[2,112,1024]{2,1,0:T(8,128)(2,1)S(1)}, bf16[2,112,1024]{2,1,0:T(8,128)(2,1)S(1)}, u32[]{:S(2)}, u32[]{:S(2)}) collective-permute-start(bf16[2,112,1024]{2,1,0:T(8,128)(2,1)S(1)} %collective-permute-done.5.refs_2_), channel_id=1, source_target_pairs={{0,16},{2,114},{16,32},{18,2},{32,48},{34,18},{48,64},{50,34},{64,... | collective-permute-start | bytes 1376264 | tf_op jit(solution)/shard_map/ppermute | solution.py:30
  32.3 5.4 %collective-permute-done.6.refs_3_ = bf16[2,112,1024]{2,1,0:T(8,128)(2,1)S(1)} collective-permute-done((bf16[2,112,1024]{2,1,0:T(8,128)(2,1)S(1)}, bf16[2,112,1024]{2,1,0:T(8,128)(2,1)S(1)}, u32[]{:S(2)}, u32[]{:S(2)}) %collective-permute-start.6) | collective-permute-done | bytes 458784 | tf_op jit(solution)/shard_map/ppermute | solution.py:30
  37.8 3.5 %collective-permute-start.13 = (bf16[2,56,1024]{2,1,0:T(8,128)(2,1)S(1)}, bf16[2,56,1024]{2,1,0:T(8,128)(2,1)S(1)}, u32[]{:S(2)}, u32[]{:S(2)}) collective-permute-start(bf16[2,56,1024]{2,1,0:T(8,128)(2,1)S(1)} %slice.19), channel_id=1, source_target_pairs={{0,16},{2,114},{16,32},{18,2},{32,48},{34,18},{48,64},{50,34},{64,... | collective-permute-start | bytes 688136 | tf_op jit(solution)/shard_map/ppermute | solution.py:30
  41.3 5.7 %collective-permute-done.8.refs_10_ = bf16[2,224,1024]{2,1,0:T(8,128)(2,1)S(1)} collective-permute-done((bf16[2,224,1024]{2,1,0:T(8,128)(2,1)S(1)}, bf16[2,224,1024]{2,1,0:T(8,128)(2,1)S(1)}, u32[]{:S(2)}, u32[]{:S(2)}) %collective-permute-start.8) | collective-permute-done | bytes 917536 | tf_op jit(solution)/shard_map/ppermute | solution.py:30
  47.1 2.3 %collective-permute-start.10 = (bf16[2,112,1024]{2,1,0:T(8,128)(2,1)S(1)}, bf16[2,112,1024]{2,1,0:T(8,128)(2,1)S(1)}, u32[]{:S(2)}, u32[]{:S(2)}) collective-permute-start(bf16[2,112,1024]{2,1,0:T(8,128)(2,1)S(1)} %collective-permute-done.1.refs_1_), channel_id=1, source_target_pairs={{0,2},{2,0},{16,18},{18,16},{32,34},{34,32},{48,50},{50,48},{64,66... | collective-permute-start | bytes 1376264 | tf_op jit(solution)/shard_map/ppermute | solution.py:30
  49.9 3.5 %collective-permute-start.14 = (bf16[2,56,1024]{2,1,0:T(8,128)(2,1)S(1)}, bf16[2,56,1024]{2,1,0:T(8,128)(2,1)S(1)}, u32[]{:S(2)}, u32[]{:S(2)}) collective-permute-start(bf16[2,56,1024]{2,1,0:T(8,128)(2,1)S(1)} %collective-permute-done.13), channel_id=1, source_target_pairs={{0,2},{2,0},{16,18},{18,16},{32,34},{34,32},{48,50},{50,48},{64,66... | collective-permute-start | bytes 688136 | tf_op jit(solution)/shard_map/ppermute | solution.py:30
  53.4 1.1 %collective-permute-done.14 = bf16[2,56,1024]{2,1,0:T(8,128)(2,1)S(1)} collective-permute-done((bf16[2,56,1024]{2,1,0:T(8,128)(2,1)S(1)}, bf16[2,56,1024]{2,1,0:T(8,128)(2,1)S(1)}, u32[]{:S(2)}, u32[]{:S(2)}) %collective-permute-start.14) | collective-permute-done | bytes 229408 | tf_op jit(solution)/shard_map/ppermute | solution.py:30
  54.6 9.0 %gram.1 = f32[8,896]{1,0:T(8,128)S(1)} custom-call(s32[2]{0:T(128)S(1)} %copy-done, bf16[2,112,1024]{2,1,0:T(8,128)(2,1)S(1)} %pad_maximum_fusion.1.refs_0_, bf16[2,112,1024]{2,1,0:T(8,128)(2,1)S(1)} %collective-permute-done.1.refs_1_, bf16[2,112,1024]{2,1,0:T(8,128)(2,1)S(1)} %collective-permute-done.5.refs_2_, ...), custom_call_target="tpu_custom_call" | custom-call | flops 3288334336 | bytes 7340032 | tf_op jit(solution)/shard_map/gram/pallas_call | solution.py:119
  64.9 8.1 %collective-permute-start.16 = (f32[8,896]{1,0:T(8,128)S(1)}, f32[8,896]{1,0:T(8,128)S(1)}, u32[]{:S(2)}, u32[]{:S(2)}) collective-permute-start(f32[8,896]{1,0:T(8,128)S(1)} %add.33), channel_id=1, source_target_pairs={{0,16},{2,18},{16,0},{18,2},{32,48},{34,50},{48,32},{50,34},{64,80... | collective-permute-start | bytes 86024 | tf_op jit(solution)/shard_map/ppermute | solution.py:30
  73.0 1.3 %collective-permute-done.16 = f32[8,896]{1,0:T(8,128)S(1)} collective-permute-done((f32[8,896]{1,0:T(8,128)S(1)}, f32[8,896]{1,0:T(8,128)S(1)}, u32[]{:S(2)}, u32[]{:S(2)}) %collective-permute-start.16) | collective-permute-done | bytes 28704 | tf_op jit(solution)/shard_map/ppermute | solution.py:30
  74.2 4.2 %collective-permute-start.17 = (f32[8,896]{1,0:T(8,128)S(1)}, f32[8,896]{1,0:T(8,128)S(1)}, u32[]{:S(2)}, u32[]{:S(2)}) collective-permute-start(f32[8,896]{1,0:T(8,128)S(1)} %add.34), channel_id=1, source_target_pairs={{0,32},{2,34},{16,48},{18,50},{32,0},{34,2},{48,16},{50,18},{64,96... | collective-permute-start | bytes 86024 | tf_op jit(solution)/shard_map/ppermute | solution.py:30
  78.5 1.3 %collective-permute-done.17 = f32[8,896]{1,0:T(8,128)S(1)} collective-permute-done((f32[8,896]{1,0:T(8,128)S(1)}, f32[8,896]{1,0:T(8,128)S(1)}, u32[]{:S(2)}, u32[]{:S(2)}) %collective-permute-start.17) | collective-permute-done | bytes 28704 | tf_op jit(solution)/shard_map/ppermute | solution.py:30
  79.8 7.0 %collective-permute-done.18 = f32[8,896]{1,0:T(8,128)S(1)} collective-permute-done((f32[8,896]{1,0:T(8,128)S(1)}, f32[8,896]{1,0:T(8,128)S(1)}, u32[]{:S(2)}, u32[]{:S(2)}) %collective-permute-start.18) | collective-permute-done | bytes 28704 | tf_op jit(solution)/shard_map/ppermute | solution.py:30
  86.9 2.4 %collective-permute-start.21 = (f32[8,128]{1,0:T(8,128)S(1)}, f32[8,128]{1,0:T(8,128)S(1)}, u32[]{:S(2)}, u32[]{:S(2)}) collective-permute-start(f32[8,128]{1,0:T(8,128)S(1)} %maximum_reduce_fusion), channel_id=1, source_target_pairs={{0,129},{2,14},{16,145},{18,30},{32,161},{34,46},{48,177},{50,62},... | collective-permute-start | bytes 12296 | tf_op jit(solution)/shard_map/ppermute | solution.py:30
  89.3 1.6 %collective-permute-start.19 = (f32[8,128]{1,0:T(8,128)S(1)}, f32[8,128]{1,0:T(8,128)S(1)}, u32[]{:S(2)}, u32[]{:S(2)}) collective-permute-start(f32[8,128]{1,0:T(8,128)S(1)} %maximum_reduce_fusion), channel_id=1, source_target_pairs={{0,128},{2,10},{16,144},{18,26},{32,160},{34,42},{48,176},{50,58},... | collective-permute-start | bytes 12296 | tf_op jit(solution)/shard_map/ppermute | solution.py:30
  90.9 2.0 %collective-permute-done.20 = f32[8,128]{1,0:T(8,128)S(1)} collective-permute-done((f32[8,128]{1,0:T(8,128)S(1)}, f32[8,128]{1,0:T(8,128)S(1)}, u32[]{:S(2)}, u32[]{:S(2)}) %collective-permute-start.20) | collective-permute-done | bytes 4128 | tf_op jit(solution)/shard_map/ppermute | solution.py:30
  93.3 1.5 %collective-permute-start.23 = (f32[8,128]{1,0:T(8,128)S(1)}, f32[8,128]{1,0:T(8,128)S(1)}, u32[]{:S(2)}, u32[]{:S(2)}) collective-permute-start(f32[8,128]{1,0:T(8,128)S(1)} %add_add_fusion.1), channel_id=1, source_target_pairs={{0,4},{2,3},{16,20},{18,19},{32,36},{34,35},{48,52},{50,51},{64,68... | collective-permute-start | bytes 12296 | tf_op jit(solution)/shard_map/ppermute | solution.py:30
  95.7 1.4 %collective-permute-done.23 = f32[8,128]{1,0:T(8,128)S(1)} collective-permute-done((f32[8,128]{1,0:T(8,128)S(1)}, f32[8,128]{1,0:T(8,128)S(1)}, u32[]{:S(2)}, u32[]{:S(2)}) %collective-permute-start.23) | collective-permute-done | bytes 4128 | tf_op jit(solution)/shard_map/ppermute | solution.py:30
  97.1 1.6 %collective-permute-done.22 = f32[8,128]{1,0:T(8,128)S(1)} collective-permute-done((f32[8,128]{1,0:T(8,128)S(1)}, f32[8,128]{1,0:T(8,128)S(1)}, u32[]{:S(2)}, u32[]{:S(2)}) %collective-permute-start.22) | collective-permute-done | bytes 4128 | tf_op jit(solution)/shard_map/ppermute | solution.py:30
  98.7 6.6 %collective-permute-start.25 = (f32[8,128]{1,0:T(8,128)S(1)}, f32[8,128]{1,0:T(8,128)S(1)}, u32[]{:S(2)}, u32[]{:S(2)}) collective-permute-start(f32[8,128]{1,0:T(8,128)S(1)} %add_add_fusion), channel_id=1, source_target_pairs={{0,2},{2,0},{16,18},{18,16},{32,34},{34,32},{48,50},{50,48},{64,66... | collective-permute-start | bytes 12296 | tf_op jit(solution)/shard_map/ppermute | solution.py:30
  106.7 1.5 %finish.1 = (f32[2,56]{1,0:T(2,128)}, f32[1,1]{1,0:T(1,128)}) custom-call(f32[8,896]{1,0:T(8,128)} %copy-done.3, f32[8,128]{1,0:T(8,128)} %add_multiply_fusion.sums_ref), custom_call_target="tpu_custom_call" | custom-call | tf_op jit(solution)/shard_map/finish/pallas_call | solution.py:171
  (45 shorter events, 7.3 us)
Async XLA Ops:
  0.6 21.7 %copy-start.1 = (bf16[56,1024]{1,0:T(8,128)(2,1)S(1)}, bf16[56,1024]{1,0:T(8,128)(2,1)}, u32[]{:S(2)}) copy-start(bf16[56,1024]{1,0:T(8,128)(2,1)} %param.4) | copy-start | bytes 344068
  0.6 21.7 %copy-start.2 = (bf16[56,1024]{1,0:T(8,128)(2,1)S(1)}, bf16[56,1024]{1,0:T(8,128)(2,1)}, u32[]{:S(2)}) copy-start(bf16[56,1024]{1,0:T(8,128)(2,1)} %param.3) | copy-start | bytes 344068
  1.7 4.4 %collective-permute-start = (bf16[2,56,1024]{2,1,0:T(8,128)(2,1)S(1)}, bf16[2,56,1024]{2,1,0:T(8,128)(2,1)S(1)}, u32[]{:S(2)}, u32[]{:S(2)}) collective-permute-start(bf16[2,56,1024]{2,1,0:T(8,128)(2,1)S(1)} %pad_maximum_fusion.3), channel_id=1, source_target_pairs={{0,2},{2,0},{16,18},{18,16},{32,34},{34,32},{48,50},{50,48},{64,66... | collective-permute-start | bytes 688136 | tf_op jit(solution)/shard_map/ppermute | solution.py:30
  7.1 15.3 %collective-permute-start.1 = (bf16[2,112,1024]{2,1,0:T(8,128)(2,1)S(1)}, bf16[2,112,1024]{2,1,0:T(8,128)(2,1)S(1)}, u32[]{:S(2)}, u32[]{:S(2)}) collective-permute-start(bf16[2,112,1024]{2,1,0:T(8,128)(2,1)S(1)} %pad_maximum_fusion.1.refs_0_), channel_id=1, source_target_pairs={{0,16},{2,114},{16,32},{18,2},{32,48},{34,18},{48,64},{50,34},{64,... | collective-permute-start | bytes 1376264 | tf_op jit(solution)/shard_map/ppermute | solution.py:30
  11.0 5.7 %collective-permute-start.3 = (bf16[2,56,1024]{2,1,0:T(8,128)(2,1)S(1)}, bf16[2,56,1024]{2,1,0:T(8,128)(2,1)S(1)}, u32[]{:S(2)}, u32[]{:S(2)}) collective-permute-start(bf16[2,56,1024]{2,1,0:T(8,128)(2,1)S(1)} %pad_maximum_fusion.3), channel_id=1, source_target_pairs={{0,129},{2,14},{16,145},{18,30},{32,161},{34,46},{48,177},{50,62},... | collective-permute-start | bytes 688136 | tf_op jit(solution)/shard_map/ppermute | solution.py:30
  13.8 8.5 %collective-permute-start.2 = (bf16[2,56,1024]{2,1,0:T(8,128)(2,1)S(1)}, bf16[2,56,1024]{2,1,0:T(8,128)(2,1)S(1)}, u32[]{:S(2)}, u32[]{:S(2)}) collective-permute-start(bf16[2,56,1024]{2,1,0:T(8,128)(2,1)S(1)} %pad_maximum_fusion.3), channel_id=1, source_target_pairs={{0,1},{2,6},{16,17},{18,22},{32,33},{34,38},{48,49},{50,54},{64,65... | collective-permute-start | bytes 688136 | tf_op jit(solution)/shard_map/ppermute | solution.py:30
  13.8 8.5 %collective-permute-start.4 = (bf16[2,56,1024]{2,1,0:T(8,128)(2,1)S(1)}, bf16[2,56,1024]{2,1,0:T(8,128)(2,1)S(1)}, u32[]{:S(2)}, u32[]{:S(2)}) collective-permute-start(bf16[2,56,1024]{2,1,0:T(8,128)(2,1)S(1)} %pad_maximum_fusion.3), channel_id=1, source_target_pairs={{0,128},{2,10},{16,144},{18,26},{32,160},{34,42},{48,176},{50,58},... | collective-permute-start | bytes 688136 | tf_op jit(solution)/shard_map/ppermute | solution.py:30
  22.4 32.2 %copy-start = (s32[2]{0:T(128)S(1)}, s32[2]{0:T(128)}, u32[]{:S(2)}) copy-start(s32[2]{0:T(128)} %spread_ref.1) | copy-start | bytes 28
  22.4 7.7 %collective-permute-start.5 = (bf16[2,112,1024]{2,1,0:T(8,128)(2,1)S(1)}, bf16[2,112,1024]{2,1,0:T(8,128)(2,1)S(1)}, u32[]{:S(2)}, u32[]{:S(2)}) collective-permute-start(bf16[2,112,1024]{2,1,0:T(8,128)(2,1)S(1)} %collective-permute-done.1.refs_1_), channel_id=1, source_target_pairs={{0,16},{2,114},{16,32},{18,2},{32,48},{34,18},{48,64},{50,34},{64,... | collective-permute-start | bytes 1376264 | tf_op jit(solution)/shard_map/ppermute | solution.py:30
  23.5 17.8 %collective-permute-start.9 = (bf16[2,224,1024]{2,1,0:T(8,128)(2,1)S(1)}, bf16[2,224,1024]{2,1,0:T(8,128)(2,1)S(1)}, u32[]{:S(2)}, u32[]{:S(2)}) collective-permute-start(bf16[2,224,1024]{2,1,0:T(8,128)(2,1)S(1)} %pad_maximum_fusion.refs_8_), channel_id=1, source_target_pairs={{0,8},{2,130},{16,24},{18,146},{32,40},{34,162},{48,56},{50,178},{... | collective-permute-start | bytes 2752520 | tf_op jit(solution)/shard_map/ppermute | solution.py:30
  26.0 21.1 %collective-permute-start.8 = (bf16[2,224,1024]{2,1,0:T(8,128)(2,1)S(1)}, bf16[2,224,1024]{2,1,0:T(8,128)(2,1)S(1)}, u32[]{:S(2)}, u32[]{:S(2)}) collective-permute-start(bf16[2,224,1024]{2,1,0:T(8,128)(2,1)S(1)} %pad_maximum_fusion.refs_8_), channel_id=1, source_target_pairs={{0,12},{2,131},{16,28},{18,147},{32,44},{34,163},{48,60},{50,179},... | collective-permute-start | bytes 2752520 | tf_op jit(solution)/shard_map/ppermute | solution.py:30
  26.8 20.3 %collective-permute-start.7 = (bf16[2,224,1024]{2,1,0:T(8,128)(2,1)S(1)}, bf16[2,224,1024]{2,1,0:T(8,128)(2,1)S(1)}, u32[]{:S(2)}, u32[]{:S(2)}) collective-permute-start(bf16[2,224,1024]{2,1,0:T(8,128)(2,1)S(1)} %pad_maximum_fusion.refs_8_), channel_id=1, source_target_pairs={{0,4},{2,3},{16,20},{18,19},{32,36},{34,35},{48,52},{50,51},{64,68... | collective-permute-start | bytes 2752520 | tf_op jit(solution)/shard_map/ppermute | solution.py:30
  30.1 7.7 %collective-permute-start.6 = (bf16[2,112,1024]{2,1,0:T(8,128)(2,1)S(1)}, bf16[2,112,1024]{2,1,0:T(8,128)(2,1)S(1)}, u32[]{:S(2)}, u32[]{:S(2)}) collective-permute-start(bf16[2,112,1024]{2,1,0:T(8,128)(2,1)S(1)} %collective-permute-done.5.refs_2_), channel_id=1, source_target_pairs={{0,16},{2,114},{16,32},{18,2},{32,48},{34,18},{48,64},{50,34},{64,... | collective-permute-start | bytes 1376264 | tf_op jit(solution)/shard_map/ppermute | solution.py:30
  37.8 12.1 %collective-permute-start.13 = (bf16[2,56,1024]{2,1,0:T(8,128)(2,1)S(1)}, bf16[2,56,1024]{2,1,0:T(8,128)(2,1)S(1)}, u32[]{:S(2)}, u32[]{:S(2)}) collective-permute-start(bf16[2,56,1024]{2,1,0:T(8,128)(2,1)S(1)} %slice.19), channel_id=1, source_target_pairs={{0,16},{2,114},{16,32},{18,2},{32,48},{34,18},{48,64},{50,34},{64,... | collective-permute-start | bytes 688136 | tf_op jit(solution)/shard_map/ppermute | solution.py:30
  47.1 7.4 %collective-permute-start.10 = (bf16[2,112,1024]{2,1,0:T(8,128)(2,1)S(1)}, bf16[2,112,1024]{2,1,0:T(8,128)(2,1)S(1)}, u32[]{:S(2)}, u32[]{:S(2)}) collective-permute-start(bf16[2,112,1024]{2,1,0:T(8,128)(2,1)S(1)} %collective-permute-done.1.refs_1_), channel_id=1, source_target_pairs={{0,2},{2,0},{16,18},{18,16},{32,34},{34,32},{48,50},{50,48},{64,66... | collective-permute-start | bytes 1376264 | tf_op jit(solution)/shard_map/ppermute | solution.py:30
  49.4 5.2 %collective-permute-start.11 = (bf16[2,112,1024]{2,1,0:T(8,128)(2,1)S(1)}, bf16[2,112,1024]{2,1,0:T(8,128)(2,1)S(1)}, u32[]{:S(2)}, u32[]{:S(2)}) collective-permute-start(bf16[2,112,1024]{2,1,0:T(8,128)(2,1)S(1)} %collective-permute-done.5.refs_2_), channel_id=1, source_target_pairs={{0,2},{2,0},{16,18},{18,16},{32,34},{34,32},{48,50},{50,48},{64,66... | collective-permute-start | bytes 1376264 | tf_op jit(solution)/shard_map/ppermute | solution.py:30
  49.5 5.1 %collective-permute-start.12 = (bf16[2,112,1024]{2,1,0:T(8,128)(2,1)S(1)}, bf16[2,112,1024]{2,1,0:T(8,128)(2,1)S(1)}, u32[]{:S(2)}, u32[]{:S(2)}) collective-permute-start(bf16[2,112,1024]{2,1,0:T(8,128)(2,1)S(1)} %collective-permute-done.6.refs_3_), channel_id=1, source_target_pairs={{0,2},{2,0},{16,18},{18,16},{32,34},{34,32},{48,50},{50,48},{64,66... | collective-permute-start | bytes 1376264 | tf_op jit(solution)/shard_map/ppermute | solution.py:30
  49.9 4.6 %collective-permute-start.14 = (bf16[2,56,1024]{2,1,0:T(8,128)(2,1)S(1)}, bf16[2,56,1024]{2,1,0:T(8,128)(2,1)S(1)}, u32[]{:S(2)}, u32[]{:S(2)}) collective-permute-start(bf16[2,56,1024]{2,1,0:T(8,128)(2,1)S(1)} %collective-permute-done.13), channel_id=1, source_target_pairs={{0,2},{2,0},{16,18},{18,16},{32,34},{34,32},{48,50},{50,48},{64,66... | collective-permute-start | bytes 688136 | tf_op jit(solution)/shard_map/ppermute | solution.py:30
  63.6 1.3 %collective-permute-start.15 = (f32[8,896]{1,0:T(8,128)S(1)}, f32[8,896]{1,0:T(8,128)S(1)}, u32[]{:S(2)}, u32[]{:S(2)}) collective-permute-start(f32[8,896]{1,0:T(8,128)S(1)} %gram.1), channel_id=1, source_target_pairs={{0,2},{2,0},{16,18},{18,16},{32,34},{34,32},{48,50},{50,48},{64,66... | collective-permute-start | bytes 86024 | tf_op jit(solution)/shard_map/ppermute | solution.py:30
  64.9 9.3 %collective-permute-start.16 = (f32[8,896]{1,0:T(8,128)S(1)}, f32[8,896]{1,0:T(8,128)S(1)}, u32[]{:S(2)}, u32[]{:S(2)}) collective-permute-start(f32[8,896]{1,0:T(8,128)S(1)} %add.33), channel_id=1, source_target_pairs={{0,16},{2,18},{16,0},{18,2},{32,48},{34,50},{48,32},{50,34},{64,80... | collective-permute-start | bytes 86024 | tf_op jit(solution)/shard_map/ppermute | solution.py:30
  74.2 5.5 %collective-permute-start.17 = (f32[8,896]{1,0:T(8,128)S(1)}, f32[8,896]{1,0:T(8,128)S(1)}, u32[]{:S(2)}, u32[]{:S(2)}) collective-permute-start(f32[8,896]{1,0:T(8,128)S(1)} %add.34), channel_id=1, source_target_pairs={{0,32},{2,34},{16,48},{18,50},{32,0},{34,2},{48,16},{50,18},{64,96... | collective-permute-start | bytes 86024 | tf_op jit(solution)/shard_map/ppermute | solution.py:30
  79.8 7.0 %collective-permute-start.18 = (f32[8,896]{1,0:T(8,128)S(1)}, f32[8,896]{1,0:T(8,128)S(1)}, u32[]{:S(2)}, u32[]{:S(2)}) collective-permute-start(f32[8,896]{1,0:T(8,128)S(1)} %add.35), channel_id=1, source_target_pairs={{0,64},{2,66},{16,80},{18,82},{32,96},{34,98},{48,112},{50,114},{6... | collective-permute-start | bytes 86024 | tf_op jit(solution)/shard_map/ppermute | solution.py:30
  86.8 19.9 %copy-start.3 = (f32[8,896]{1,0:T(8,128)}, f32[8,896]{1,0:T(8,128)S(1)}, u32[]{:S(2)}) copy-start(f32[8,896]{1,0:T(8,128)S(1)} %add.36.part_ref) | copy-start | bytes 86020
  86.9 4.0 %collective-permute-start.21 = (f32[8,128]{1,0:T(8,128)S(1)}, f32[8,128]{1,0:T(8,128)S(1)}, u32[]{:S(2)}, u32[]{:S(2)}) collective-permute-start(f32[8,128]{1,0:T(8,128)S(1)} %maximum_reduce_fusion), channel_id=1, source_target_pairs={{0,129},{2,14},{16,145},{18,30},{32,161},{34,46},{48,177},{50,62},... | collective-permute-start | bytes 12296 | tf_op jit(solution)/shard_map/ppermute | solution.py:30
  89.3 3.7 %collective-permute-start.20 = (f32[8,128]{1,0:T(8,128)S(1)}, f32[8,128]{1,0:T(8,128)S(1)}, u32[]{:S(2)}, u32[]{:S(2)}) collective-permute-start(f32[8,128]{1,0:T(8,128)S(1)} %maximum_reduce_fusion), channel_id=1, source_target_pairs={{0,1},{2,6},{16,17},{18,22},{32,33},{34,38},{48,49},{50,54},{64,65... | collective-permute-start | bytes 12296 | tf_op jit(solution)/shard_map/ppermute | solution.py:30
  89.3 4.0 %collective-permute-start.19 = (f32[8,128]{1,0:T(8,128)S(1)}, f32[8,128]{1,0:T(8,128)S(1)}, u32[]{:S(2)}, u32[]{:S(2)}) collective-permute-start(f32[8,128]{1,0:T(8,128)S(1)} %maximum_reduce_fusion), channel_id=1, source_target_pairs={{0,128},{2,10},{16,144},{18,26},{32,160},{34,42},{48,176},{50,58},... | collective-permute-start | bytes 12296 | tf_op jit(solution)/shard_map/ppermute | solution.py:30
  93.2 2.5 %collective-permute-start.24 = (f32[8,128]{1,0:T(8,128)S(1)}, f32[8,128]{1,0:T(8,128)S(1)}, u32[]{:S(2)}, u32[]{:S(2)}) collective-permute-start(f32[8,128]{1,0:T(8,128)S(1)} %add_add_fusion.1), channel_id=1, source_target_pairs={{0,12},{2,131},{16,28},{18,147},{32,44},{34,163},{48,60},{50,179},... | collective-permute-start | bytes 12296 | tf_op jit(solution)/shard_map/ppermute | solution.py:30
  93.3 3.8 %collective-permute-start.23 = (f32[8,128]{1,0:T(8,128)S(1)}, f32[8,128]{1,0:T(8,128)S(1)}, u32[]{:S(2)}, u32[]{:S(2)}) collective-permute-start(f32[8,128]{1,0:T(8,128)S(1)} %add_add_fusion.1), channel_id=1, source_target_pairs={{0,4},{2,3},{16,20},{18,19},{32,36},{34,35},{48,52},{50,51},{64,68... | collective-permute-start | bytes 12296 | tf_op jit(solution)/shard_map/ppermute | solution.py:30
  94.7 4.0 %collective-permute-start.22 = (f32[8,128]{1,0:T(8,128)S(1)}, f32[8,128]{1,0:T(8,128)S(1)}, u32[]{:S(2)}, u32[]{:S(2)}) collective-permute-start(f32[8,128]{1,0:T(8,128)S(1)} %add_add_fusion.1), channel_id=1, source_target_pairs={{0,8},{2,130},{16,24},{18,146},{32,40},{34,162},{48,56},{50,178},{... | collective-permute-start | bytes 12296 | tf_op jit(solution)/shard_map/ppermute | solution.py:30
  98.7 7.4 %collective-permute-start.25 = (f32[8,128]{1,0:T(8,128)S(1)}, f32[8,128]{1,0:T(8,128)S(1)}, u32[]{:S(2)}, u32[]{:S(2)}) collective-permute-start(f32[8,128]{1,0:T(8,128)S(1)} %add_add_fusion), channel_id=1, source_target_pairs={{0,2},{2,0},{16,18},{18,16},{32,34},{34,32},{48,50},{50,48},{64,66... | collective-permute-start | bytes 12296 | tf_op jit(solution)/shard_map/ppermute | solution.py:30

commit v4 on v3

--- a/solution.py
+++ b/solution.py
@@ -65,12 +65,11 @@
 
 
 def gram_body(n_line, spread_ref, *refs):
-    line, pieces = refs[:n_line], refs[n_line:-3]
-    out_ref, z_ref, norm_ref = refs[-3:]
+    line, pieces = refs[:n_line], refs[n_line:-4]
+    out_ref, z_ref, w_ref, norm_ref = refs[-4:]
     width = z_ref.shape[1]
     tall = pieces[0].shape[1]
-    lanes = 128
-    scales = [jnp.full((1, lanes), spread_ref[layer].astype(jnp.float32), jnp.float32) for layer in range(2)]
+    scales = [jnp.full((1, 128), spread_ref[layer].astype(jnp.float32), jnp.float32) for layer in range(2)]
     factors = [LOG2E / scale for scale in scales]
     offsets = [jnp.exp(-D / scale) for scale in scales]
     at = 0
@@ -78,28 +77,39 @@
         z_ref[:, at : at + ref.shape[1], :] = ref[...]
         at += ref.shape[1]
     for index, piece in enumerate(pieces):
+        rows = slice(index * tall, (index + 1) * tall)
         for layer in range(2):
-            norms = jnp.sum(fold_squares(piece[layer]), axis=1, keepdims=True)
-            rows = slice(index * tall, (index + 1) * tall)
-            norm_ref[layer, rows, :] = jnp.broadcast_to(norms, (tall, lanes)) * (0.5 * factors[layer])
+            block = piece[layer]
+            w_ref[layer, rows, :] = block
+            norms = jnp.sum(fold_squares(block), axis=1, keepdims=True)
+            norm_ref[layer, rows, :] = jnp.broadcast_to(norms, (tall, 128)) * (0.5 * factors[layer])
     columns = []
-    for start in range(0, width, lanes):
-        z = [z_ref[layer, start : start + lanes, :] for layer in range(2)]
-        z_norms = [
-            jnp.sum(fold_squares(z[layer]).T, axis=0, keepdims=True) * (0.5 * factors[layer]) for layer in range(2)
-        ]
+    height = w_ref.shape[1] // 2
+    for start in range(0, width, 256):
+        spans = range(start, min(start + 256, width), 128)
+        wide = lambda row: jnp.concatenate([row] * len(spans), axis=1)
+        z_norms = []
+        for layer in range(2):
+            norms = [
+                jnp.sum(fold_squares(z_ref[layer, span : span + 128, :]).T, axis=0, keepdims=True) for span in spans
+            ]
+            z_norms.append(jnp.concatenate(norms, axis=1) * (0.5 * wide(factors[layer])))
+        lanes = 128 * len(spans)
         sums = [jnp.zeros((8, lanes), jnp.float32) for _ in range(5)]
-        for index, piece in enumerate(pieces):
+        for top in range(0, w_ref.shape[1], height):
             kernels = []
             for layer in range(2):
                 inner = lax.dot_general(
-                    piece[layer], z[layer], (((1,), (1,)), ((), ())), preferred_element_type=jnp.float32
+                    w_ref[layer, top : top + height, :],
+                    z_ref[layer, start : start + lanes, :],
+                    (((1,), (1,)), ((), ())),
+                    preferred_element_type=jnp.float32,
                 )
-                norms = norm_ref[layer, index * tall : (index + 1) * tall, :]
-                kernels.append(jnp.exp2(inner * factors[layer] - norms - z_norms[layer]) - offsets[layer])
+                power = inner * wide(factors[layer]) - wide(norm_ref[layer, top : top + height, :]) - z_norms[layer]
+                kernels.append(jnp.exp2(power) - wide(offsets[layer]))
             one, two = kernels
             for row, term in enumerate((one, two, one * two, one * one, two * two)):
-                sums[row] = sums[row] + jnp.sum(term.reshape(tall // 8, 8, lanes), axis=0)
+                sums[row] = sums[row] + jnp.sum(term.reshape(height // 8, 8, lanes), axis=0)
         rows = [jnp.sum(term, axis=0, keepdims=True) for term in sums]
         columns.append(jnp.concatenate(rows + [jnp.zeros((3, lanes), jnp.float32)], axis=0))
     local = jnp.concatenate(columns, axis=1)
@@ -121,7 +131,11 @@
         out_shape=jax.ShapeDtypeStruct((8, width), jnp.float32),
         in_specs=[pl.BlockSpec(memory_space=pltpu.SMEM)] + [vmem] * (len(line) + len(pieces)),
         out_specs=vmem,
-        scratch_shapes=[pltpu.VMEM((2, width, D), jnp.bfloat16), pltpu.VMEM((2, rows, 128), jnp.float32)],
+        scratch_shapes=[
+            pltpu.VMEM((2, width, D), jnp.bfloat16),
+            pltpu.VMEM((2, rows, D), jnp.bfloat16),
+            pltpu.VMEM((2, rows, 128), jnp.float32),
+        ],
         compiler_params=pltpu.CompilerParams(vmem_limit_bytes=24 << 20),
         cost_estimate=pl.CostEstimate(
             flops=4 * rows * width * D, bytes_accessed=4 * (rows + width) * D, transcendentals=2 * rows * width
@@ -178,20 +192,20 @@
 
 
 def shards(layer_one, layer_two, spread):
-    own = jnp.stack([layer_one, layer_two])
+    own = lax.optimization_barrier(jnp.stack([layer_one, layer_two]))
     count = own.shape[1]
+    near = [shift(own, step, 0) for step in (1, -1, 2)]
     chip = jnp.concatenate([own, swap(own)], axis=1)
-    near = [shift(own, step, 0) for step in (1, -1, 2)]
     strip = jnp.concatenate([own] + near, axis=1)
     first, strip = lax.optimization_barrier((around(chip), strip))
     pieces = [strip] + [shift(strip, 0, step) for step in (1, -1, 2)]
     ring = [first]
     for _ in range(2):
         ring.append(around(ring[-1]))
-    last = around(ring[-1][:, :count])
-    pieces, late = lax.optimization_barrier((pieces, ring))
-    ends = jnp.concatenate([last, swap(last)], axis=1)
-    line = [chip] + ring + [swap(block) for block in late] + [ends]
+    last = around(ring[2][:, :count])
+    pieces, late = lax.optimization_barrier((pieces, last))
+    ends = jnp.concatenate([last, swap(late)], axis=1)
+    line = [chip] + ring + [swap(block) for block in ring] + [ends]
     part = line_sum(gram(spread, line, pieces))
     r_one, r_two = part[0], part[1]
     sums = jnp.stack([r_one, r_two, part[2], part[3], part[4], r_one * r_two, r_one * r_one, r_two * r_two])

time: 108 us -> 90.8 us (0.84)
  the two profiles are of different devices: /device:TPU:1 before, /device:TPU:6 now
where the time goes in v4:
time: 90.8 us; the launch traced here: 89.9 us
  starting transfers between devices  39.7 us (44%)
  waiting for transfers between devices  39.5 us (44%)
  Pallas kernels  8.04 us (9%)
  other arithmetic  1.78 us (2%)
    ppermute x26, starting transfers between devices, move(): return lax.ppermute(array, AXES, pairs)  39.7 us
    ppermute x26, waiting for transfers between devices, move(): return lax.ppermute(array, AXES, pairs)  39.5 us
    pallas_call x1, Pallas kernels, gram(): pl.pallas_call(functools.partial(gram_body, len(line)), out_shape=jax.Sha...  6.57 us
  transfers between devices with their start and end apart: 26, of which 16 were waited for; matrix products, arithmetic and copies ran while one was open for 0% of the time, Pallas kernels for 0%

profile of v4, /device:TPU:6, one launch (start us, length us, event | category | flops | bytes accessed | tf_op | source)
XLA Modules:
  0.0 89.9 jit_solution(1132350590284365682)
XLA Ops:
  1.7 1.5 %collective-permute-done = bf16[2,56,1024]{2,1,0:T(8,128)(2,1)S(1)} collective-permute-done((bf16[2,56,1024]{2,1,0:T(8,128)(2,1)S(1)}, bf16[2,56,1024]{2,1,0:T(8,128)(2,1)S(1)}, u32[]{:S(2)}, u32[]{:S(2)}) %collective-permute-start) | collective-permute-done | bytes 229408 | tf_op jit(solution)/shard_map/ppermute | solution.py:30
  3.2 2.0 %collective-permute-start.1 = (bf16[2,112,1024]{2,1,0:T(8,128)(2,1)S(1)}, bf16[2,112,1024]{2,1,0:T(8,128)(2,1)S(1)}, u32[]{:S(2)}, u32[]{:S(2)}) collective-permute-start(bf16[2,112,1024]{2,1,0:T(8,128)(2,1)S(1)} %pad_maximum_fusion.1.refs_0_), channel_id=1, source_target_pairs={{0,16},{2,114},{16,32},{18,2},{32,48},{34,18},{48,64},{50,34},{64,... | collective-permute-start | bytes 1376264 | tf_op jit(solution)/shard_map/ppermute | solution.py:30
  5.7 1.5 %collective-permute-start.3 = (bf16[2,56,1024]{2,1,0:T(8,128)(2,1)S(1)}, bf16[2,56,1024]{2,1,0:T(8,128)(2,1)S(1)}, u32[]{:S(2)}, u32[]{:S(2)}) collective-permute-start(bf16[2,56,1024]{2,1,0:T(8,128)(2,1)S(1)} %pad_maximum_fusion.3), channel_id=1, source_target_pairs={{0,129},{2,14},{16,145},{18,30},{32,161},{34,46},{48,177},{50,62},... | collective-permute-start | bytes 688136 | tf_op jit(solution)/shard_map/ppermute | solution.py:30
  7.2 1.4 %collective-permute-start.4 = (bf16[2,56,1024]{2,1,0:T(8,128)(2,1)S(1)}, bf16[2,56,1024]{2,1,0:T(8,128)(2,1)S(1)}, u32[]{:S(2)}, u32[]{:S(2)}) collective-permute-start(bf16[2,56,1024]{2,1,0:T(8,128)(2,1)S(1)} %pad_maximum_fusion.3), channel_id=1, source_target_pairs={{0,128},{2,10},{16,144},{18,26},{32,160},{34,42},{48,176},{50,58},... | collective-permute-start | bytes 688136 | tf_op jit(solution)/shard_map/ppermute | solution.py:30
  8.6 2.6 %collective-permute-done.2 = bf16[2,56,1024]{2,1,0:T(8,128)(2,1)S(1)} collective-permute-done((bf16[2,56,1024]{2,1,0:T(8,128)(2,1)S(1)}, bf16[2,56,1024]{2,1,0:T(8,128)(2,1)S(1)}, u32[]{:S(2)}, u32[]{:S(2)}) %collective-permute-start.2) | collective-permute-done | bytes 229408 | tf_op jit(solution)/shard_map/ppermute | solution.py:30
  11.2 4.1 %collective-permute-done.3 = bf16[2,56,1024]{2,1,0:T(8,128)(2,1)S(1)} collective-permute-done((bf16[2,56,1024]{2,1,0:T(8,128)(2,1)S(1)}, bf16[2,56,1024]{2,1,0:T(8,128)(2,1)S(1)}, u32[]{:S(2)}, u32[]{:S(2)}) %collective-permute-start.3) | collective-permute-done | bytes 229408 | tf_op jit(solution)/shard_map/ppermute | solution.py:30
  15.6 1.9 %collective-permute-start.5 = (bf16[2,112,1024]{2,1,0:T(8,128)(2,1)S(1)}, bf16[2,112,1024]{2,1,0:T(8,128)(2,1)S(1)}, u32[]{:S(2)}, u32[]{:S(2)}) collective-permute-start(bf16[2,112,1024]{2,1,0:T(8,128)(2,1)S(1)} %collective-permute-done.1.refs_1_), channel_id=1, source_target_pairs={{0,16},{2,114},{16,32},{18,2},{32,48},{34,18},{48,64},{50,34},{64,... | collective-permute-start | bytes 1376264 | tf_op jit(solution)/shard_map/ppermute | solution.py:30
  17.5 1.6 %collective-permute-start.11 = (bf16[2,224,1024]{2,1,0:T(8,128)(2,1)S(1)}, bf16[2,224,1024]{2,1,0:T(8,128)(2,1)S(1)}, u32[]{:S(2)}, u32[]{:S(2)}) collective-permute-start(bf16[2,224,1024]{2,1,0:T(8,128)(2,1)S(1)} %pad_maximum_fusion.refs_8_), channel_id=1, source_target_pairs={{0,4},{2,3},{16,20},{18,19},{32,36},{34,35},{48,52},{50,51},{64,68... | collective-permute-start | bytes 2752520 | tf_op jit(solution)/shard_map/ppermute | solution.py:30
  19.1 1.7 %collective-permute-start.12 = (bf16[2,224,1024]{2,1,0:T(8,128)(2,1)S(1)}, bf16[2,224,1024]{2,1,0:T(8,128)(2,1)S(1)}, u32[]{:S(2)}, u32[]{:S(2)}) collective-permute-start(bf16[2,224,1024]{2,1,0:T(8,128)(2,1)S(1)} %pad_maximum_fusion.refs_8_), channel_id=1, source_target_pairs={{0,12},{2,131},{16,28},{18,147},{32,44},{34,163},{48,60},{50,179},... | collective-permute-start | bytes 2752520 | tf_op jit(solution)/shard_map/ppermute | solution.py:30
  20.7 2.0 %collective-permute-start.13 = (bf16[2,224,1024]{2,1,0:T(8,128)(2,1)S(1)}, bf16[2,224,1024]{2,1,0:T(8,128)(2,1)S(1)}, u32[]{:S(2)}, u32[]{:S(2)}) collective-permute-start(bf16[2,224,1024]{2,1,0:T(8,128)(2,1)S(1)} %pad_maximum_fusion.refs_8_), channel_id=1, source_target_pairs={{0,8},{2,130},{16,24},{18,146},{32,40},{34,162},{48,56},{50,178},{... | collective-permute-start | bytes 2752520 | tf_op jit(solution)/shard_map/ppermute | solution.py:30
  22.7 3.3 %collective-permute-done.5.refs_2_ = bf16[2,112,1024]{2,1,0:T(8,128)(2,1)S(1)} collective-permute-done((bf16[2,112,1024]{2,1,0:T(8,128)(2,1)S(1)}, bf16[2,112,1024]{2,1,0:T(8,128)(2,1)S(1)}, u32[]{:S(2)}, u32[]{:S(2)}) %collective-permute-start.5) | collective-permute-done | bytes 458784 | tf_op jit(solution)/shard_map/ppermute | solution.py:30
  26.0 9.7 %collective-permute-done.6.refs_3_ = bf16[2,112,1024]{2,1,0:T(8,128)(2,1)S(1)} collective-permute-done((bf16[2,112,1024]{2,1,0:T(8,128)(2,1)S(1)}, bf16[2,112,1024]{2,1,0:T(8,128)(2,1)S(1)}, u32[]{:S(2)}, u32[]{:S(2)}) %collective-permute-start.6) | collective-permute-done | bytes 458784 | tf_op jit(solution)/shard_map/ppermute | solution.py:30
  35.8 1.6 %collective-permute-start.7 = (bf16[2,112,1024]{2,1,0:T(8,128)(2,1)S(1)}, bf16[2,112,1024]{2,1,0:T(8,128)(2,1)S(1)}, u32[]{:S(2)}, u32[]{:S(2)}) collective-permute-start(bf16[2,112,1024]{2,1,0:T(8,128)(2,1)S(1)} %collective-permute-done.1.refs_1_), channel_id=1, source_target_pairs={{0,2},{2,0},{16,18},{18,16},{32,34},{34,32},{48,50},{50,48},{64,66... | collective-permute-start | bytes 1376264 | tf_op jit(solution)/shard_map/ppermute | solution.py:30
  37.5 6.0 %collective-permute-start.9 = (bf16[2,112,1024]{2,1,0:T(8,128)(2,1)S(1)}, bf16[2,112,1024]{2,1,0:T(8,128)(2,1)S(1)}, u32[]{:S(2)}, u32[]{:S(2)}) collective-permute-start(bf16[2,112,1024]{2,1,0:T(8,128)(2,1)S(1)} %collective-permute-done.6.refs_3_), channel_id=1, source_target_pairs={{0,2},{2,0},{16,18},{18,16},{32,34},{34,32},{48,50},{50,48},{64,66... | collective-permute-start | bytes 1376264 | tf_op jit(solution)/shard_map/ppermute | solution.py:30
  43.7 1.5 %collective-permute-done.14 = bf16[2,56,1024]{2,1,0:T(8,128)(2,1)S(1)} collective-permute-done((bf16[2,56,1024]{2,1,0:T(8,128)(2,1)S(1)}, bf16[2,56,1024]{2,1,0:T(8,128)(2,1)S(1)}, u32[]{:S(2)}, u32[]{:S(2)}) %collective-permute-start.14) | collective-permute-done | bytes 229408 | tf_op jit(solution)/shard_map/ppermute | solution.py:30
  45.3 6.6 %gram.1 = f32[8,896]{1,0:T(8,128)S(1)} custom-call(s32[2]{0:T(128)S(1)} %copy-done, bf16[2,112,1024]{2,1,0:T(8,128)(2,1)S(1)} %pad_maximum_fusion.1.refs_0_, bf16[2,112,1024]{2,1,0:T(8,128)(2,1)S(1)} %collective-permute-done.1.refs_1_, bf16[2,112,1024]{2,1,0:T(8,128)(2,1)S(1)} %collective-permute-done.5.refs_2_, ...), custom_call_target="tpu_custom_call" | custom-call | flops 3288334336 | bytes 7340032 | tf_op jit(solution)/shard_map/gram/pallas_call | solution.py:129
  53.2 1.3 %collective-permute-start.16 = (f32[8,896]{1,0:T(8,128)S(1)}, f32[8,896]{1,0:T(8,128)S(1)}, u32[]{:S(2)}, u32[]{:S(2)}) collective-permute-start(f32[8,896]{1,0:T(8,128)S(1)} %add.33), channel_id=1, source_target_pairs={{0,16},{2,18},{16,0},{18,2},{32,48},{34,50},{48,32},{50,34},{64,80... | collective-permute-start | bytes 86024 | tf_op jit(solution)/shard_map/ppermute | solution.py:30
  54.5 2.6 %collective-permute-done.16 = f32[8,896]{1,0:T(8,128)S(1)} collective-permute-done((f32[8,896]{1,0:T(8,128)S(1)}, f32[8,896]{1,0:T(8,128)S(1)}, u32[]{:S(2)}, u32[]{:S(2)}) %collective-permute-start.16) | collective-permute-done | bytes 28704 | tf_op jit(solution)/shard_map/ppermute | solution.py:30
  57.1 3.9 %collective-permute-start.17 = (f32[8,896]{1,0:T(8,128)S(1)}, f32[8,896]{1,0:T(8,128)S(1)}, u32[]{:S(2)}, u32[]{:S(2)}) collective-permute-start(f32[8,896]{1,0:T(8,128)S(1)} %add.34), channel_id=1, source_target_pairs={{0,32},{2,34},{16,48},{18,50},{32,0},{34,2},{48,16},{50,18},{64,96... | collective-permute-start | bytes 86024 | tf_op jit(solution)/shard_map/ppermute | solution.py:30
  61.0 1.8 %collective-permute-done.17 = f32[8,896]{1,0:T(8,128)S(1)} collective-permute-done((f32[8,896]{1,0:T(8,128)S(1)}, f32[8,896]{1,0:T(8,128)S(1)}, u32[]{:S(2)}, u32[]{:S(2)}) %collective-permute-start.17) | collective-permute-done | bytes 28704 | tf_op jit(solution)/shard_map/ppermute | solution.py:30
  62.8 3.8 %collective-permute-start.18 = (f32[8,896]{1,0:T(8,128)S(1)}, f32[8,896]{1,0:T(8,128)S(1)}, u32[]{:S(2)}, u32[]{:S(2)}) collective-permute-start(f32[8,896]{1,0:T(8,128)S(1)} %add.35), channel_id=1, source_target_pairs={{0,64},{2,66},{16,80},{18,82},{32,96},{34,98},{48,112},{50,114},{6... | collective-permute-start | bytes 86024 | tf_op jit(solution)/shard_map/ppermute | solution.py:30
  66.6 3.9 %collective-permute-done.18 = f32[8,896]{1,0:T(8,128)S(1)} collective-permute-done((f32[8,896]{1,0:T(8,128)S(1)}, f32[8,896]{1,0:T(8,128)S(1)}, u32[]{:S(2)}, u32[]{:S(2)}) %collective-permute-start.18) | collective-permute-done | bytes 28704 | tf_op jit(solution)/shard_map/ppermute | solution.py:30
  70.7 2.0 %collective-permute-start.19 = (f32[8,128]{1,0:T(8,128)S(1)}, f32[8,128]{1,0:T(8,128)S(1)}, u32[]{:S(2)}, u32[]{:S(2)}) collective-permute-start(f32[8,128]{1,0:T(8,128)S(1)} %maximum_reduce_fusion), channel_id=1, source_target_pairs={{0,128},{2,10},{16,144},{18,26},{32,160},{34,42},{48,176},{50,58},... | collective-permute-start | bytes 12296 | tf_op jit(solution)/shard_map/ppermute | solution.py:30
  72.7 1.9 %collective-permute-start.20 = (f32[8,128]{1,0:T(8,128)S(1)}, f32[8,128]{1,0:T(8,128)S(1)}, u32[]{:S(2)}, u32[]{:S(2)}) collective-permute-start(f32[8,128]{1,0:T(8,128)S(1)} %maximum_reduce_fusion), channel_id=1, source_target_pairs={{0,1},{2,6},{16,17},{18,22},{32,33},{34,38},{48,49},{50,54},{64,65... | collective-permute-start | bytes 12296 | tf_op jit(solution)/shard_map/ppermute | solution.py:30
  74.7 1.2 %collective-permute-done.19 = f32[8,128]{1,0:T(8,128)S(1)} collective-permute-done((f32[8,128]{1,0:T(8,128)S(1)}, f32[8,128]{1,0:T(8,128)S(1)}, u32[]{:S(2)}, u32[]{:S(2)}) %collective-permute-start.19) | collective-permute-done | bytes 4128 | tf_op jit(solution)/shard_map/ppermute | solution.py:30
  76.3 3.1 %collective-permute-done.21 = f32[8,128]{1,0:T(8,128)S(1)} collective-permute-done((f32[8,128]{1,0:T(8,128)S(1)}, f32[8,128]{1,0:T(8,128)S(1)}, u32[]{:S(2)}, u32[]{:S(2)}) %collective-permute-start.21) | collective-permute-done | bytes 4128 | tf_op jit(solution)/shard_map/ppermute | solution.py:30
  79.4 2.3 %collective-permute-start.22 = (f32[8,128]{1,0:T(8,128)S(1)}, f32[8,128]{1,0:T(8,128)S(1)}, u32[]{:S(2)}, u32[]{:S(2)}) collective-permute-start(f32[8,128]{1,0:T(8,128)S(1)} %add_add_fusion.1), channel_id=1, source_target_pairs={{0,8},{2,130},{16,24},{18,146},{32,40},{34,162},{48,56},{50,178},{... | collective-permute-start | bytes 12296 | tf_op jit(solution)/shard_map/ppermute | solution.py:30
  81.7 1.0 %collective-permute-start.23 = (f32[8,128]{1,0:T(8,128)S(1)}, f32[8,128]{1,0:T(8,128)S(1)}, u32[]{:S(2)}, u32[]{:S(2)}) collective-permute-start(f32[8,128]{1,0:T(8,128)S(1)} %add_add_fusion.1), channel_id=1, source_target_pairs={{0,4},{2,3},{16,20},{18,19},{32,36},{34,35},{48,52},{50,51},{64,68... | collective-permute-start | bytes 12296 | tf_op jit(solution)/shard_map/ppermute | solution.py:30
  82.7 2.2 %collective-permute-start.24 = (f32[8,128]{1,0:T(8,128)S(1)}, f32[8,128]{1,0:T(8,128)S(1)}, u32[]{:S(2)}, u32[]{:S(2)}) collective-permute-start(f32[8,128]{1,0:T(8,128)S(1)} %add_add_fusion.1), channel_id=1, source_target_pairs={{0,12},{2,131},{16,28},{18,147},{32,44},{34,163},{48,60},{50,179},... | collective-permute-start | bytes 12296 | tf_op jit(solution)/shard_map/ppermute | solution.py:30
  85.0 1.6 %collective-permute-done.23 = f32[8,128]{1,0:T(8,128)S(1)} collective-permute-done((f32[8,128]{1,0:T(8,128)S(1)}, f32[8,128]{1,0:T(8,128)S(1)}, u32[]{:S(2)}, u32[]{:S(2)}) %collective-permute-start.23) | collective-permute-done | bytes 4128 | tf_op jit(solution)/shard_map/ppermute | solution.py:30
  86.7 1.2 %collective-permute-done.25 = f32[8,128]{1,0:T(8,128)S(1)} collective-permute-done((f32[8,128]{1,0:T(8,128)S(1)}, f32[8,128]{1,0:T(8,128)S(1)}, u32[]{:S(2)}, u32[]{:S(2)}) %collective-permute-start.25) | collective-permute-done | bytes 4128 | tf_op jit(solution)/shard_map/ppermute | solution.py:30
  88.4 1.5 %finish.1 = (f32[2,56]{1,0:T(2,128)}, f32[1,1]{1,0:T(1,128)}) custom-call(f32[8,896]{1,0:T(8,128)} %copy-done.1, f32[8,128]{1,0:T(8,128)} %add_multiply_fusion.sums_ref), custom_call_target="tpu_custom_call" | custom-call | tf_op jit(solution)/shard_map/finish/pallas_call | solution.py:185
  (41 shorter events, 4.9 us)
Async XLA Ops:
  1.6 1.6 %collective-permute-start = (bf16[2,56,1024]{2,1,0:T(8,128)(2,1)S(1)}, bf16[2,56,1024]{2,1,0:T(8,128)(2,1)S(1)}, u32[]{:S(2)}, u32[]{:S(2)}) collective-permute-start(bf16[2,56,1024]{2,1,0:T(8,128)(2,1)S(1)} %pad_maximum_fusion.3), channel_id=1, source_target_pairs={{0,2},{2,0},{16,18},{18,16},{32,34},{34,32},{48,50},{50,48},{64,66... | collective-permute-start | bytes 688136 | tf_op jit(solution)/shard_map/ppermute | solution.py:30
  3.2 12.4 %collective-permute-start.1 = (bf16[2,112,1024]{2,1,0:T(8,128)(2,1)S(1)}, bf16[2,112,1024]{2,1,0:T(8,128)(2,1)S(1)}, u32[]{:S(2)}, u32[]{:S(2)}) collective-permute-start(bf16[2,112,1024]{2,1,0:T(8,128)(2,1)S(1)} %pad_maximum_fusion.1.refs_0_), channel_id=1, source_target_pairs={{0,16},{2,114},{16,32},{18,2},{32,48},{34,18},{48,64},{50,34},{64,... | collective-permute-start | bytes 1376264 | tf_op jit(solution)/shard_map/ppermute | solution.py:30
  5.2 6.0 %collective-permute-start.2 = (bf16[2,56,1024]{2,1,0:T(8,128)(2,1)S(1)}, bf16[2,56,1024]{2,1,0:T(8,128)(2,1)S(1)}, u32[]{:S(2)}, u32[]{:S(2)}) collective-permute-start(bf16[2,56,1024]{2,1,0:T(8,128)(2,1)S(1)} %pad_maximum_fusion.3), channel_id=1, source_target_pairs={{0,1},{2,6},{16,17},{18,22},{32,33},{34,38},{48,49},{50,54},{64,65... | collective-permute-start | bytes 688136 | tf_op jit(solution)/shard_map/ppermute | solution.py:30
  5.7 9.7 %collective-permute-start.3 = (bf16[2,56,1024]{2,1,0:T(8,128)(2,1)S(1)}, bf16[2,56,1024]{2,1,0:T(8,128)(2,1)S(1)}, u32[]{:S(2)}, u32[]{:S(2)}) collective-permute-start(bf16[2,56,1024]{2,1,0:T(8,128)(2,1)S(1)} %pad_maximum_fusion.3), channel_id=1, source_target_pairs={{0,129},{2,14},{16,145},{18,30},{32,161},{34,46},{48,177},{50,62},... | collective-permute-start | bytes 688136 | tf_op jit(solution)/shard_map/ppermute | solution.py:30
  7.2 8.1 %collective-permute-start.4 = (bf16[2,56,1024]{2,1,0:T(8,128)(2,1)S(1)}, bf16[2,56,1024]{2,1,0:T(8,128)(2,1)S(1)}, u32[]{:S(2)}, u32[]{:S(2)}) collective-permute-start(bf16[2,56,1024]{2,1,0:T(8,128)(2,1)S(1)} %pad_maximum_fusion.3), channel_id=1, source_target_pairs={{0,128},{2,10},{16,144},{18,26},{32,160},{34,42},{48,176},{50,58},... | collective-permute-start | bytes 688136 | tf_op jit(solution)/shard_map/ppermute | solution.py:30
  15.5 29.9 %copy-start = (s32[2]{0:T(128)S(1)}, s32[2]{0:T(128)}, u32[]{:S(2)}) copy-start(s32[2]{0:T(128)} %spread_ref.1) | copy-start | bytes 28
  15.6 10.4 %collective-permute-start.5 = (bf16[2,112,1024]{2,1,0:T(8,128)(2,1)S(1)}, bf16[2,112,1024]{2,1,0:T(8,128)(2,1)S(1)}, u32[]{:S(2)}, u32[]{:S(2)}) collective-permute-start(bf16[2,112,1024]{2,1,0:T(8,128)(2,1)S(1)} %collective-permute-done.1.refs_1_), channel_id=1, source_target_pairs={{0,16},{2,114},{16,32},{18,2},{32,48},{34,18},{48,64},{50,34},{64,... | collective-permute-start | bytes 1376264 | tf_op jit(solution)/shard_map/ppermute | solution.py:30
  17.5 20.0 %collective-permute-start.11 = (bf16[2,224,1024]{2,1,0:T(8,128)(2,1)S(1)}, bf16[2,224,1024]{2,1,0:T(8,128)(2,1)S(1)}, u32[]{:S(2)}, u32[]{:S(2)}) collective-permute-start(bf16[2,224,1024]{2,1,0:T(8,128)(2,1)S(1)} %pad_maximum_fusion.refs_8_), channel_id=1, source_target_pairs={{0,4},{2,3},{16,20},{18,19},{32,36},{34,35},{48,52},{50,51},{64,68... | collective-permute-start | bytes 2752520 | tf_op jit(solution)/shard_map/ppermute | solution.py:30
  19.1 18.4 %collective-permute-start.12 = (bf16[2,224,1024]{2,1,0:T(8,128)(2,1)S(1)}, bf16[2,224,1024]{2,1,0:T(8,128)(2,1)S(1)}, u32[]{:S(2)}, u32[]{:S(2)}) collective-permute-start(bf16[2,224,1024]{2,1,0:T(8,128)(2,1)S(1)} %pad_maximum_fusion.refs_8_), channel_id=1, source_target_pairs={{0,12},{2,131},{16,28},{18,147},{32,44},{34,163},{48,60},{50,179},... | collective-permute-start | bytes 2752520 | tf_op jit(solution)/shard_map/ppermute | solution.py:30
  20.7 22.8 %collective-permute-start.13 = (bf16[2,224,1024]{2,1,0:T(8,128)(2,1)S(1)}, bf16[2,224,1024]{2,1,0:T(8,128)(2,1)S(1)}, u32[]{:S(2)}, u32[]{:S(2)}) collective-permute-start(bf16[2,224,1024]{2,1,0:T(8,128)(2,1)S(1)} %pad_maximum_fusion.refs_8_), channel_id=1, source_target_pairs={{0,8},{2,130},{16,24},{18,146},{32,40},{34,162},{48,56},{50,178},{... | collective-permute-start | bytes 2752520 | tf_op jit(solution)/shard_map/ppermute | solution.py:30
  26.0 9.7 %collective-permute-start.6 = (bf16[2,112,1024]{2,1,0:T(8,128)(2,1)S(1)}, bf16[2,112,1024]{2,1,0:T(8,128)(2,1)S(1)}, u32[]{:S(2)}, u32[]{:S(2)}) collective-permute-start(bf16[2,112,1024]{2,1,0:T(8,128)(2,1)S(1)} %collective-permute-done.5.refs_2_), channel_id=1, source_target_pairs={{0,16},{2,114},{16,32},{18,2},{32,48},{34,18},{48,64},{50,34},{64,... | collective-permute-start | bytes 1376264 | tf_op jit(solution)/shard_map/ppermute | solution.py:30
  35.8 7.7 %collective-permute-start.10 = (bf16[2,56,1024]{2,1,0:T(8,128)(2,1)S(1)}, bf16[2,56,1024]{2,1,0:T(8,128)(2,1)S(1)}, u32[]{:S(2)}, u32[]{:S(2)}) collective-permute-start(bf16[2,56,1024]{2,1,0:T(8,128)(2,1)S(1)} %slice.19), channel_id=1, source_target_pairs={{0,16},{2,114},{16,32},{18,2},{32,48},{34,18},{48,64},{50,34},{64,... | collective-permute-start | bytes 688136 | tf_op jit(solution)/shard_map/ppermute | solution.py:30
  35.8 9.4 %collective-permute-start.7 = (bf16[2,112,1024]{2,1,0:T(8,128)(2,1)S(1)}, bf16[2,112,1024]{2,1,0:T(8,128)(2,1)S(1)}, u32[]{:S(2)}, u32[]{:S(2)}) collective-permute-start(bf16[2,112,1024]{2,1,0:T(8,128)(2,1)S(1)} %collective-permute-done.1.refs_1_), channel_id=1, source_target_pairs={{0,2},{2,0},{16,18},{18,16},{32,34},{34,32},{48,50},{50,48},{64,66... | collective-permute-start | bytes 1376264 | tf_op jit(solution)/shard_map/ppermute | solution.py:30
  37.5 7.8 %collective-permute-start.8 = (bf16[2,112,1024]{2,1,0:T(8,128)(2,1)S(1)}, bf16[2,112,1024]{2,1,0:T(8,128)(2,1)S(1)}, u32[]{:S(2)}, u32[]{:S(2)}) collective-permute-start(bf16[2,112,1024]{2,1,0:T(8,128)(2,1)S(1)} %collective-permute-done.5.refs_2_), channel_id=1, source_target_pairs={{0,2},{2,0},{16,18},{18,16},{32,34},{34,32},{48,50},{50,48},{64,66... | collective-permute-start | bytes 1376264 | tf_op jit(solution)/shard_map/ppermute | solution.py:30
  37.5 7.8 %collective-permute-start.9 = (bf16[2,112,1024]{2,1,0:T(8,128)(2,1)S(1)}, bf16[2,112,1024]{2,1,0:T(8,128)(2,1)S(1)}, u32[]{:S(2)}, u32[]{:S(2)}) collective-permute-start(bf16[2,112,1024]{2,1,0:T(8,128)(2,1)S(1)} %collective-permute-done.6.refs_3_), channel_id=1, source_target_pairs={{0,2},{2,0},{16,18},{18,16},{32,34},{34,32},{48,50},{50,48},{64,66... | collective-permute-start | bytes 1376264 | tf_op jit(solution)/shard_map/ppermute | solution.py:30
  43.5 1.8 %collective-permute-start.14 = (bf16[2,56,1024]{2,1,0:T(8,128)(2,1)S(1)}, bf16[2,56,1024]{2,1,0:T(8,128)(2,1)S(1)}, u32[]{:S(2)}, u32[]{:S(2)}) collective-permute-start(bf16[2,56,1024]{2,1,0:T(8,128)(2,1)S(1)} %collective-permute-done.10), channel_id=1, source_target_pairs={{0,2},{2,0},{16,18},{18,16},{32,34},{34,32},{48,50},{50,48},{64,66... | collective-permute-start | bytes 688136 | tf_op jit(solution)/shard_map/ppermute | solution.py:30
  51.9 1.3 %collective-permute-start.15 = (f32[8,896]{1,0:T(8,128)S(1)}, f32[8,896]{1,0:T(8,128)S(1)}, u32[]{:S(2)}, u32[]{:S(2)}) collective-permute-start(f32[8,896]{1,0:T(8,128)S(1)} %gram.1), channel_id=1, source_target_pairs={{0,2},{2,0},{16,18},{18,16},{32,34},{34,32},{48,50},{50,48},{64,66... | collective-permute-start | bytes 86024 | tf_op jit(solution)/shard_map/ppermute | solution.py:30
  53.2 3.9 %collective-permute-start.16 = (f32[8,896]{1,0:T(8,128)S(1)}, f32[8,896]{1,0:T(8,128)S(1)}, u32[]{:S(2)}, u32[]{:S(2)}) collective-permute-start(f32[8,896]{1,0:T(8,128)S(1)} %add.33), channel_id=1, source_target_pairs={{0,16},{2,18},{16,0},{18,2},{32,48},{34,50},{48,32},{50,34},{64,80... | collective-permute-start | bytes 86024 | tf_op jit(solution)/shard_map/ppermute | solution.py:30
  57.1 5.7 %collective-permute-start.17 = (f32[8,896]{1,0:T(8,128)S(1)}, f32[8,896]{1,0:T(8,128)S(1)}, u32[]{:S(2)}, u32[]{:S(2)}) collective-permute-start(f32[8,896]{1,0:T(8,128)S(1)} %add.34), channel_id=1, source_target_pairs={{0,32},{2,34},{16,48},{18,50},{32,0},{34,2},{48,16},{50,18},{64,96... | collective-permute-start | bytes 86024 | tf_op jit(solution)/shard_map/ppermute | solution.py:30
  62.8 7.8 %collective-permute-start.18 = (f32[8,896]{1,0:T(8,128)S(1)}, f32[8,896]{1,0:T(8,128)S(1)}, u32[]{:S(2)}, u32[]{:S(2)}) collective-permute-start(f32[8,896]{1,0:T(8,128)S(1)} %add.35), channel_id=1, source_target_pairs={{0,64},{2,66},{16,80},{18,82},{32,96},{34,98},{48,112},{50,114},{6... | collective-permute-start | bytes 86024 | tf_op jit(solution)/shard_map/ppermute | solution.py:30
  70.6 17.8 %copy-start.1 = (f32[8,896]{1,0:T(8,128)}, f32[8,896]{1,0:T(8,128)S(1)}, u32[]{:S(2)}) copy-start(f32[8,896]{1,0:T(8,128)S(1)} %add.36.part_ref) | copy-start | bytes 86020
  70.7 5.2 %collective-permute-start.19 = (f32[8,128]{1,0:T(8,128)S(1)}, f32[8,128]{1,0:T(8,128)S(1)}, u32[]{:S(2)}, u32[]{:S(2)}) collective-permute-start(f32[8,128]{1,0:T(8,128)S(1)} %maximum_reduce_fusion), channel_id=1, source_target_pairs={{0,128},{2,10},{16,144},{18,26},{32,160},{34,42},{48,176},{50,58},... | collective-permute-start | bytes 12296 | tf_op jit(solution)/shard_map/ppermute | solution.py:30
  72.7 3.6 %collective-permute-start.20 = (f32[8,128]{1,0:T(8,128)S(1)}, f32[8,128]{1,0:T(8,128)S(1)}, u32[]{:S(2)}, u32[]{:S(2)}) collective-permute-start(f32[8,128]{1,0:T(8,128)S(1)} %maximum_reduce_fusion), channel_id=1, source_target_pairs={{0,1},{2,6},{16,17},{18,22},{32,33},{34,38},{48,49},{50,54},{64,65... | collective-permute-start | bytes 12296 | tf_op jit(solution)/shard_map/ppermute | solution.py:30
  74.6 4.8 %collective-permute-start.21 = (f32[8,128]{1,0:T(8,128)S(1)}, f32[8,128]{1,0:T(8,128)S(1)}, u32[]{:S(2)}, u32[]{:S(2)}) collective-permute-start(f32[8,128]{1,0:T(8,128)S(1)} %maximum_reduce_fusion), channel_id=1, source_target_pairs={{0,129},{2,14},{16,145},{18,30},{32,161},{34,46},{48,177},{50,62},... | collective-permute-start | bytes 12296 | tf_op jit(solution)/shard_map/ppermute | solution.py:30
  79.4 5.6 %collective-permute-start.22 = (f32[8,128]{1,0:T(8,128)S(1)}, f32[8,128]{1,0:T(8,128)S(1)}, u32[]{:S(2)}, u32[]{:S(2)}) collective-permute-start(f32[8,128]{1,0:T(8,128)S(1)} %add_add_fusion.1), channel_id=1, source_target_pairs={{0,8},{2,130},{16,24},{18,146},{32,40},{34,162},{48,56},{50,178},{... | collective-permute-start | bytes 12296 | tf_op jit(solution)/shard_map/ppermute | solution.py:30
  81.7 4.8 %collective-permute-start.23 = (f32[8,128]{1,0:T(8,128)S(1)}, f32[8,128]{1,0:T(8,128)S(1)}, u32[]{:S(2)}, u32[]{:S(2)}) collective-permute-start(f32[8,128]{1,0:T(8,128)S(1)} %add_add_fusion.1), channel_id=1, source_target_pairs={{0,4},{2,3},{16,20},{18,19},{32,36},{34,35},{48,52},{50,51},{64,68... | collective-permute-start | bytes 12296 | tf_op jit(solution)/shard_map/ppermute | solution.py:30
  82.7 3.8 %collective-permute-start.24 = (f32[8,128]{1,0:T(8,128)S(1)}, f32[8,128]{1,0:T(8,128)S(1)}, u32[]{:S(2)}, u32[]{:S(2)}) collective-permute-start(f32[8,128]{1,0:T(8,128)S(1)} %add_add_fusion.1), channel_id=1, source_target_pairs={{0,12},{2,131},{16,28},{18,147},{32,44},{34,163},{48,60},{50,179},... | collective-permute-start | bytes 12296 | tf_op jit(solution)/shard_map/ppermute | solution.py:30
  86.6 1.3 %collective-permute-start.25 = (f32[8,128]{1,0:T(8,128)S(1)}, f32[8,128]{1,0:T(8,128)S(1)}, u32[]{:S(2)}, u32[]{:S(2)}) collective-permute-start(f32[8,128]{1,0:T(8,128)S(1)} %add_add_fusion), channel_id=1, source_target_pairs={{0,2},{2,0},{16,18},{18,16},{32,34},{34,32},{48,50},{50,48},{64,66... | collective-permute-start | bytes 12296 | tf_op jit(solution)/shard_map/ppermute | solution.py:30

commit v5 on v4

--- a/solution.py
+++ b/solution.py
@@ -154,20 +154,25 @@
 
 def line_sum(array):
     array = array + swap(array)
-    for bit in (1, 2, 4):
-        array = array + move(array, lambda x, y, z, core: (x, y, z ^ bit, core))
-    return array
-
-
-def plane_sum(array):
-    for stage in range(2):
-        parts = [shift(array, *((step, 0) if stage == 0 else (0, step))) for step in (1, -1, 2)]
-        array = (array + parts[2]) + (parts[0] + parts[1])
-    return 0.5 * (array + swap(array))
-
-
-def finish_body(total, count, part_ref, sums_ref, profiles_ref, alignment_ref):
-    sums = jnp.sum(sums_ref[...], axis=1, keepdims=True)
+    array = array + move(array, lambda x, y, z, core: (x, y, z ^ 1, core))
+    parts = [move(array, lambda x, y, z, core: (x, y, z + step, core)) for step in (2, -2, 4)]
+    return ring_sum(array, parts)
+
+
+def ring_parts(array, axis):
+    return [
+        move(array, lambda x, y, z, core: (x + step, y, z, core) if axis == "x" else (x, y + step, z, core))
+        for step in (1, -1, 2)
+    ]
+
+
+def ring_sum(array, parts):
+    return (array + parts[2]) + (parts[0] + parts[1])
+
+
+def finish_body(total, count, part_ref, sums_ref, *refs):
+    parts, (profiles_ref, alignment_ref) = refs[:3], refs[3:]
+    sums = jnp.sum(ring_sum(sums_ref[...], [part[...] for part in parts]), axis=1, keepdims=True)
     sum_one, sum_two, f_cross, f_one, f_two, c_cross, c_one, c_two = (sums[at : at + 1, :] for at in range(8))
     h_cross = f_cross - 2.0 * c_cross / total + sum_one * sum_two / (total * total)
     h_one = f_one - 2.0 * c_one / total + sum_one * sum_one / (total * total)
@@ -180,15 +185,16 @@
     profiles_ref[...] = rows[:2, :count] / roots
 
 
-def finish(part, sums, total, count):
+def finish(part, sums, parts, total, count):
     vmem = pl.BlockSpec(memory_space=pltpu.VMEM)
     return pl.pallas_call(
         functools.partial(finish_body, float(total), count),
         out_shape=(jax.ShapeDtypeStruct((2, count), jnp.float32), jax.ShapeDtypeStruct((1, 1), jnp.float32)),
-        in_specs=[vmem, vmem],
+        in_specs=[vmem] * 5,
         out_specs=(vmem, vmem),
+        compiler_params=pltpu.CompilerParams(vmem_limit_bytes=2 << 20),
         name="finish",
-    )(part, sums)
+    )(part, sums, *parts)
 
 
 def shards(layer_one, layer_two, spread):
@@ -209,8 +215,9 @@
     part = line_sum(gram(spread, line, pieces))
     r_one, r_two = part[0], part[1]
     sums = jnp.stack([r_one, r_two, part[2], part[3], part[4], r_one * r_two, r_one * r_one, r_two * r_two])
-    sums = plane_sum(jnp.sum(sums.reshape(8, part.shape[1] // 128, 128), axis=1))
-    profiles, alignment = finish(part, sums, count * lax.axis_size(AXES), count)
+    sums = jnp.sum(sums.reshape(8, part.shape[1] // 128, 128), axis=1)
+    sums = ring_sum(sums, ring_parts(sums, "x"))
+    profiles, alignment = finish(part, sums, ring_parts(sums, "y"), count * lax.axis_size(AXES), count)
     return (profiles, alignment.reshape(()))
 
 

time: 90.8 us -> 85.1 us (0.937)
  waiting for transfers between devices: 39.5 us -> 35.1 us
    ppermute x26, waiting for transfers between devices: 39.5 us -> 35.1 us  [move(): return lax.ppermute(array, AXES, pairs)]
  transfers between devices with their start and end apart: 26 -> 26, of which waited for: 16 -> 14; matrix products, arithmetic and copies ran while one was open for 0% -> 0% of each run, Pallas kernels for 0% -> 0%
where the time goes in v5:
time: 85.1 us; the launch traced here: 85 us
  starting transfers between devices  40.6 us (48%)
  waiting for transfers between devices  35.1 us (41%)
  Pallas kernels  7.31 us (9%)
  other arithmetic  1.18 us (1%)
    ppermute x26, starting transfers between devices, move(): return lax.ppermute(array, AXES, pairs)  40.6 us
    ppermute x26, waiting for transfers between devices, move(): return lax.ppermute(array, AXES, pairs)  35.1 us
    pallas_call x1, Pallas kernels, gram(): pl.pallas_call(functools.partial(gram_body, len(line)), out_shape=jax.Sha...  6.57 us
  transfers between devices with their start and end apart: 26, of which 14 were waited for; matrix products, arithmetic and copies ran while one was open for 0% of the time, Pallas kernels for 0%

profile of v5, /device:TPU:6, one launch (start us, length us, event | category | flops | bytes accessed | tf_op | source)
XLA Modules:
  0.0 85.0 jit_solution(16193098315482005832)
XLA Ops:
  0.6 1.0 %pad_maximum_fusion.3 = bf16[2,56,1024]{2,1,0:T(8,128)(2,1)S(1)} fusion(bf16[1,56,1024]{2,1,0:T(8,128)(2,1)} %bitcast.8, bf16[1,56,1024]{2,1,0:T(8,128)(2,1)} %bitcast.9), kind=kLoop, calls=%fused_computation.3 | loop fusion | flops 114688 | bytes 458752 | tf_op jit(solution)/shard_map/stack | solution.py:201
  1.7 1.5 %collective-permute-done = bf16[2,56,1024]{2,1,0:T(8,128)(2,1)S(1)} collective-permute-done((bf16[2,56,1024]{2,1,0:T(8,128)(2,1)S(1)}, bf16[2,56,1024]{2,1,0:T(8,128)(2,1)S(1)}, u32[]{:S(2)}, u32[]{:S(2)}) %collective-permute-start) | collective-permute-done | bytes 229408 | tf_op jit(solution)/shard_map/ppermute | solution.py:30
  3.2 2.0 %collective-permute-start.1 = (bf16[2,112,1024]{2,1,0:T(8,128)(2,1)S(1)}, bf16[2,112,1024]{2,1,0:T(8,128)(2,1)S(1)}, u32[]{:S(2)}, u32[]{:S(2)}) collective-permute-start(bf16[2,112,1024]{2,1,0:T(8,128)(2,1)S(1)} %pad_maximum_fusion.1.refs_0_), channel_id=1, source_target_pairs={{0,16},{2,114},{16,32},{18,2},{32,48},{34,18},{48,64},{50,34},{64,... | collective-permute-start | bytes 1376264 | tf_op jit(solution)/shard_map/ppermute | solution.py:30
  5.7 1.5 %collective-permute-start.3 = (bf16[2,56,1024]{2,1,0:T(8,128)(2,1)S(1)}, bf16[2,56,1024]{2,1,0:T(8,128)(2,1)S(1)}, u32[]{:S(2)}, u32[]{:S(2)}) collective-permute-start(bf16[2,56,1024]{2,1,0:T(8,128)(2,1)S(1)} %pad_maximum_fusion.3), channel_id=1, source_target_pairs={{0,129},{2,14},{16,145},{18,30},{32,161},{34,46},{48,177},{50,62},... | collective-permute-start | bytes 688136 | tf_op jit(solution)/shard_map/ppermute | solution.py:30
  7.2 1.4 %collective-permute-start.4 = (bf16[2,56,1024]{2,1,0:T(8,128)(2,1)S(1)}, bf16[2,56,1024]{2,1,0:T(8,128)(2,1)S(1)}, u32[]{:S(2)}, u32[]{:S(2)}) collective-permute-start(bf16[2,56,1024]{2,1,0:T(8,128)(2,1)S(1)} %pad_maximum_fusion.3), channel_id=1, source_target_pairs={{0,128},{2,10},{16,144},{18,26},{32,160},{34,42},{48,176},{50,58},... | collective-permute-start | bytes 688136 | tf_op jit(solution)/shard_map/ppermute | solution.py:30
  8.6 2.6 %collective-permute-done.2 = bf16[2,56,1024]{2,1,0:T(8,128)(2,1)S(1)} collective-permute-done((bf16[2,56,1024]{2,1,0:T(8,128)(2,1)S(1)}, bf16[2,56,1024]{2,1,0:T(8,128)(2,1)S(1)}, u32[]{:S(2)}, u32[]{:S(2)}) %collective-permute-start.2) | collective-permute-done | bytes 229408 | tf_op jit(solution)/shard_map/ppermute | solution.py:30
  11.2 4.1 %collective-permute-done.3 = bf16[2,56,1024]{2,1,0:T(8,128)(2,1)S(1)} collective-permute-done((bf16[2,56,1024]{2,1,0:T(8,128)(2,1)S(1)}, bf16[2,56,1024]{2,1,0:T(8,128)(2,1)S(1)}, u32[]{:S(2)}, u32[]{:S(2)}) %collective-permute-start.3) | collective-permute-done | bytes 229408 | tf_op jit(solution)/shard_map/ppermute | solution.py:30
  15.6 1.9 %collective-permute-start.5 = (bf16[2,112,1024]{2,1,0:T(8,128)(2,1)S(1)}, bf16[2,112,1024]{2,1,0:T(8,128)(2,1)S(1)}, u32[]{:S(2)}, u32[]{:S(2)}) collective-permute-start(bf16[2,112,1024]{2,1,0:T(8,128)(2,1)S(1)} %collective-permute-done.1.refs_1_), channel_id=1, source_target_pairs={{0,16},{2,114},{16,32},{18,2},{32,48},{34,18},{48,64},{50,34},{64,... | collective-permute-start | bytes 1376264 | tf_op jit(solution)/shard_map/ppermute | solution.py:30
  17.5 1.6 %collective-permute-start.11 = (bf16[2,224,1024]{2,1,0:T(8,128)(2,1)S(1)}, bf16[2,224,1024]{2,1,0:T(8,128)(2,1)S(1)}, u32[]{:S(2)}, u32[]{:S(2)}) collective-permute-start(bf16[2,224,1024]{2,1,0:T(8,128)(2,1)S(1)} %pad_maximum_fusion.refs_8_), channel_id=1, source_target_pairs={{0,4},{2,3},{16,20},{18,19},{32,36},{34,35},{48,52},{50,51},{64,68... | collective-permute-start | bytes 2752520 | tf_op jit(solution)/shard_map/ppermute | solution.py:30
  19.1 1.7 %collective-permute-start.12 = (bf16[2,224,1024]{2,1,0:T(8,128)(2,1)S(1)}, bf16[2,224,1024]{2,1,0:T(8,128)(2,1)S(1)}, u32[]{:S(2)}, u32[]{:S(2)}) collective-permute-start(bf16[2,224,1024]{2,1,0:T(8,128)(2,1)S(1)} %pad_maximum_fusion.refs_8_), channel_id=1, source_target_pairs={{0,12},{2,131},{16,28},{18,147},{32,44},{34,163},{48,60},{50,179},... | collective-permute-start | bytes 2752520 | tf_op jit(solution)/shard_map/ppermute | solution.py:30
  20.7 2.0 %collective-permute-start.13 = (bf16[2,224,1024]{2,1,0:T(8,128)(2,1)S(1)}, bf16[2,224,1024]{2,1,0:T(8,128)(2,1)S(1)}, u32[]{:S(2)}, u32[]{:S(2)}) collective-permute-start(bf16[2,224,1024]{2,1,0:T(8,128)(2,1)S(1)} %pad_maximum_fusion.refs_8_), channel_id=1, source_target_pairs={{0,8},{2,130},{16,24},{18,146},{32,40},{34,162},{48,56},{50,178},{... | collective-permute-start | bytes 2752520 | tf_op jit(solution)/shard_map/ppermute | solution.py:30
  22.7 3.3 %collective-permute-done.5.refs_2_ = bf16[2,112,1024]{2,1,0:T(8,128)(2,1)S(1)} collective-permute-done((bf16[2,112,1024]{2,1,0:T(8,128)(2,1)S(1)}, bf16[2,112,1024]{2,1,0:T(8,128)(2,1)S(1)}, u32[]{:S(2)}, u32[]{:S(2)}) %collective-permute-start.5) | collective-permute-done | bytes 458784 | tf_op jit(solution)/shard_map/ppermute | solution.py:30
  26.0 9.7 %collective-permute-done.6.refs_3_ = bf16[2,112,1024]{2,1,0:T(8,128)(2,1)S(1)} collective-permute-done((bf16[2,112,1024]{2,1,0:T(8,128)(2,1)S(1)}, bf16[2,112,1024]{2,1,0:T(8,128)(2,1)S(1)}, u32[]{:S(2)}, u32[]{:S(2)}) %collective-permute-start.6) | collective-permute-done | bytes 458784 | tf_op jit(solution)/shard_map/ppermute | solution.py:30
  35.8 1.6 %collective-permute-start.7 = (bf16[2,112,1024]{2,1,0:T(8,128)(2,1)S(1)}, bf16[2,112,1024]{2,1,0:T(8,128)(2,1)S(1)}, u32[]{:S(2)}, u32[]{:S(2)}) collective-permute-start(bf16[2,112,1024]{2,1,0:T(8,128)(2,1)S(1)} %collective-permute-done.1.refs_1_), channel_id=1, source_target_pairs={{0,2},{2,0},{16,18},{18,16},{32,34},{34,32},{48,50},{50,48},{64,66... | collective-permute-start | bytes 1376264 | tf_op jit(solution)/shard_map/ppermute | solution.py:30
  37.5 6.0 %collective-permute-start.9 = (bf16[2,112,1024]{2,1,0:T(8,128)(2,1)S(1)}, bf16[2,112,1024]{2,1,0:T(8,128)(2,1)S(1)}, u32[]{:S(2)}, u32[]{:S(2)}) collective-permute-start(bf16[2,112,1024]{2,1,0:T(8,128)(2,1)S(1)} %collective-permute-done.6.refs_3_), channel_id=1, source_target_pairs={{0,2},{2,0},{16,18},{18,16},{32,34},{34,32},{48,50},{50,48},{64,66... | collective-permute-start | bytes 1376264 | tf_op jit(solution)/shard_map/ppermute | solution.py:30
  43.7 1.5 %collective-permute-done.14 = bf16[2,56,1024]{2,1,0:T(8,128)(2,1)S(1)} collective-permute-done((bf16[2,56,1024]{2,1,0:T(8,128)(2,1)S(1)}, bf16[2,56,1024]{2,1,0:T(8,128)(2,1)S(1)}, u32[]{:S(2)}, u32[]{:S(2)}) %collective-permute-start.14) | collective-permute-done | bytes 229408 | tf_op jit(solution)/shard_map/ppermute | solution.py:30
  45.3 6.6 %gram.1 = f32[8,896]{1,0:T(8,128)S(1)} custom-call(s32[2]{0:T(128)S(1)} %copy-done, bf16[2,112,1024]{2,1,0:T(8,128)(2,1)S(1)} %pad_maximum_fusion.1.refs_0_, bf16[2,112,1024]{2,1,0:T(8,128)(2,1)S(1)} %collective-permute-done.1.refs_1_, bf16[2,112,1024]{2,1,0:T(8,128)(2,1)S(1)} %collective-permute-done.5.refs_2_, ...), custom_call_target="tpu_custom_call" | custom-call | flops 3288334336 | bytes 7340032 | tf_op jit(solution)/shard_map/gram/pallas_call | solution.py:129
  52.4 0.9 %collective-permute-done.15 = f32[8,896]{1,0:T(8,128)S(1)} collective-permute-done((f32[8,896]{1,0:T(8,128)S(1)}, f32[8,896]{1,0:T(8,128)S(1)}, u32[]{:S(2)}, u32[]{:S(2)}) %collective-permute-start.15) | collective-permute-done | bytes 28704 | tf_op jit(solution)/shard_map/ppermute | solution.py:30
  53.2 1.3 %collective-permute-start.16 = (f32[8,896]{1,0:T(8,128)S(1)}, f32[8,896]{1,0:T(8,128)S(1)}, u32[]{:S(2)}, u32[]{:S(2)}) collective-permute-start(f32[8,896]{1,0:T(8,128)S(1)} %add.24), channel_id=1, source_target_pairs={{0,16},{2,18},{16,0},{18,2},{32,48},{34,50},{48,32},{50,34},{64,80... | collective-permute-start | bytes 86024 | tf_op jit(solution)/shard_map/ppermute | solution.py:30
  54.5 2.6 %collective-permute-done.16 = f32[8,896]{1,0:T(8,128)S(1)} collective-permute-done((f32[8,896]{1,0:T(8,128)S(1)}, f32[8,896]{1,0:T(8,128)S(1)}, u32[]{:S(2)}, u32[]{:S(2)}) %collective-permute-start.16) | collective-permute-done | bytes 28704 | tf_op jit(solution)/shard_map/ppermute | solution.py:30
  57.1 4.8 %collective-permute-start.17 = (f32[8,896]{1,0:T(8,128)S(1)}, f32[8,896]{1,0:T(8,128)S(1)}, u32[]{:S(2)}, u32[]{:S(2)}) collective-permute-start(f32[8,896]{1,0:T(8,128)S(1)} %add.25), channel_id=1, source_target_pairs={{0,64},{2,66},{16,80},{18,82},{32,96},{34,98},{48,112},{50,114},{6... | collective-permute-start | bytes 86024 | tf_op jit(solution)/shard_map/ppermute | solution.py:30
  62.4 3.6 %collective-permute-start.19 = (f32[8,896]{1,0:T(8,128)S(1)}, f32[8,896]{1,0:T(8,128)S(1)}, u32[]{:S(2)}, u32[]{:S(2)}) collective-permute-start(f32[8,896]{1,0:T(8,128)S(1)} %add.25), channel_id=1, source_target_pairs={{0,96},{2,98},{16,112},{18,114},{32,0},{34,2},{48,16},{50,18},{64,... | collective-permute-start | bytes 86024 | tf_op jit(solution)/shard_map/ppermute | solution.py:30
  66.0 1.8 %collective-permute-done.18 = f32[8,896]{1,0:T(8,128)S(1)} collective-permute-done((f32[8,896]{1,0:T(8,128)S(1)}, f32[8,896]{1,0:T(8,128)S(1)}, u32[]{:S(2)}, u32[]{:S(2)}) %collective-permute-start.18) | collective-permute-done | bytes 28704 | tf_op jit(solution)/shard_map/ppermute | solution.py:30
  67.9 1.9 %collective-permute-start.20 = (f32[8,128]{1,0:T(8,128)S(1)}, f32[8,128]{1,0:T(8,128)S(1)}, u32[]{:S(2)}, u32[]{:S(2)}) collective-permute-start(f32[8,128]{1,0:T(8,128)S(1)} %maximum_reduce_fusion), channel_id=1, source_target_pairs={{0,128},{2,130},{16,144},{18,146},{32,160},{34,162},{48,176},{50,1... | collective-permute-start | bytes 12296 | tf_op jit(solution)/shard_map/ppermute | solution.py:30
  69.9 1.1 %collective-permute-start.21 = (f32[8,128]{1,0:T(8,128)S(1)}, f32[8,128]{1,0:T(8,128)S(1)}, u32[]{:S(2)}, u32[]{:S(2)}) collective-permute-start(f32[8,128]{1,0:T(8,128)S(1)} %maximum_reduce_fusion), channel_id=1, source_target_pairs={{0,1},{2,3},{16,17},{18,19},{32,33},{34,35},{48,49},{50,51},{64,65... | collective-permute-start | bytes 12296 | tf_op jit(solution)/shard_map/ppermute | solution.py:30
  70.9 1.0 %collective-permute-start.22 = (f32[8,128]{1,0:T(8,128)S(1)}, f32[8,128]{1,0:T(8,128)S(1)}, u32[]{:S(2)}, u32[]{:S(2)}) collective-permute-start(f32[8,128]{1,0:T(8,128)S(1)} %maximum_reduce_fusion), channel_id=1, source_target_pairs={{0,129},{2,131},{16,145},{18,147},{32,161},{34,163},{48,177},{50,1... | collective-permute-start | bytes 12296 | tf_op jit(solution)/shard_map/ppermute | solution.py:30
  71.9 1.2 %collective-permute-done.20 = f32[8,128]{1,0:T(8,128)S(1)} collective-permute-done((f32[8,128]{1,0:T(8,128)S(1)}, f32[8,128]{1,0:T(8,128)S(1)}, u32[]{:S(2)}, u32[]{:S(2)}) %collective-permute-start.20) | collective-permute-done | bytes 4128 | tf_op jit(solution)/shard_map/ppermute | solution.py:30
  73.5 2.3 %collective-permute-done.22 = f32[8,128]{1,0:T(8,128)S(1)} collective-permute-done((f32[8,128]{1,0:T(8,128)S(1)}, f32[8,128]{1,0:T(8,128)S(1)}, u32[]{:S(2)}, u32[]{:S(2)}) %collective-permute-start.22) | collective-permute-done | bytes 4128 | tf_op jit(solution)/shard_map/ppermute | solution.py:30
  75.7 1.6 %collective-permute-start.23 = (f32[8,128]{1,0:T(8,128)S(1)}, f32[8,128]{1,0:T(8,128)S(1)}, u32[]{:S(2)}, u32[]{:S(2)}) collective-permute-start(f32[8,128]{1,0:T(8,128)S(1)} %add_add_fusion.1.sums_ref), channel_id=1, source_target_pairs={{0,4},{2,6},{16,20},{18,22},{32,36},{34,38},{48,52},{50,54},{64,68... | collective-permute-start | bytes 12296 | tf_op jit(solution)/shard_map/ppermute | solution.py:30
  77.3 1.8 %collective-permute-start.24 = (f32[8,128]{1,0:T(8,128)S(1)}, f32[8,128]{1,0:T(8,128)S(1)}, u32[]{:S(2)}, u32[]{:S(2)}) collective-permute-start(f32[8,128]{1,0:T(8,128)S(1)} %add_add_fusion.1.sums_ref), channel_id=1, source_target_pairs={{0,12},{2,14},{16,28},{18,30},{32,44},{34,46},{48,60},{50,62},{64,... | collective-permute-start | bytes 12296 | tf_op jit(solution)/shard_map/ppermute | solution.py:30
  79.1 2.0 %collective-permute-start.25 = (f32[8,128]{1,0:T(8,128)S(1)}, f32[8,128]{1,0:T(8,128)S(1)}, u32[]{:S(2)}, u32[]{:S(2)}) collective-permute-start(f32[8,128]{1,0:T(8,128)S(1)} %add_add_fusion.1.sums_ref), channel_id=1, source_target_pairs={{0,8},{2,10},{16,24},{18,26},{32,40},{34,42},{48,56},{50,58},{64,7... | collective-permute-start | bytes 12296 | tf_op jit(solution)/shard_map/ppermute | solution.py:30
  81.2 3.1 %collective-permute-done.25.refs_2_ = f32[8,128]{1,0:T(8,128)S(1)} collective-permute-done((f32[8,128]{1,0:T(8,128)S(1)}, f32[8,128]{1,0:T(8,128)S(1)}, u32[]{:S(2)}, u32[]{:S(2)}) %collective-permute-start.25) | collective-permute-done | bytes 4128 | tf_op jit(solution)/shard_map/ppermute | solution.py:30
  (36 shorter events, 3.4 us)
Async XLA Ops:
  1.6 1.6 %collective-permute-start = (bf16[2,56,1024]{2,1,0:T(8,128)(2,1)S(1)}, bf16[2,56,1024]{2,1,0:T(8,128)(2,1)S(1)}, u32[]{:S(2)}, u32[]{:S(2)}) collective-permute-start(bf16[2,56,1024]{2,1,0:T(8,128)(2,1)S(1)} %pad_maximum_fusion.3), channel_id=1, source_target_pairs={{0,2},{2,0},{16,18},{18,16},{32,34},{34,32},{48,50},{50,48},{64,66... | collective-permute-start | bytes 688136 | tf_op jit(solution)/shard_map/ppermute | solution.py:30
  3.2 12.4 %collective-permute-start.1 = (bf16[2,112,1024]{2,1,0:T(8,128)(2,1)S(1)}, bf16[2,112,1024]{2,1,0:T(8,128)(2,1)S(1)}, u32[]{:S(2)}, u32[]{:S(2)}) collective-permute-start(bf16[2,112,1024]{2,1,0:T(8,128)(2,1)S(1)} %pad_maximum_fusion.1.refs_0_), channel_id=1, source_target_pairs={{0,16},{2,114},{16,32},{18,2},{32,48},{34,18},{48,64},{50,34},{64,... | collective-permute-start | bytes 1376264 | tf_op jit(solution)/shard_map/ppermute | solution.py:30
  5.2 6.0 %collective-permute-start.2 = (bf16[2,56,1024]{2,1,0:T(8,128)(2,1)S(1)}, bf16[2,56,1024]{2,1,0:T(8,128)(2,1)S(1)}, u32[]{:S(2)}, u32[]{:S(2)}) collective-permute-start(bf16[2,56,1024]{2,1,0:T(8,128)(2,1)S(1)} %pad_maximum_fusion.3), channel_id=1, source_target_pairs={{0,1},{2,6},{16,17},{18,22},{32,33},{34,38},{48,49},{50,54},{64,65... | collective-permute-start | bytes 688136 | tf_op jit(solution)/shard_map/ppermute | solution.py:30
  5.7 9.7 %collective-permute-start.3 = (bf16[2,56,1024]{2,1,0:T(8,128)(2,1)S(1)}, bf16[2,56,1024]{2,1,0:T(8,128)(2,1)S(1)}, u32[]{:S(2)}, u32[]{:S(2)}) collective-permute-start(bf16[2,56,1024]{2,1,0:T(8,128)(2,1)S(1)} %pad_maximum_fusion.3), channel_id=1, source_target_pairs={{0,129},{2,14},{16,145},{18,30},{32,161},{34,46},{48,177},{50,62},... | collective-permute-start | bytes 688136 | tf_op jit(solution)/shard_map/ppermute | solution.py:30
  7.2 8.1 %collective-permute-start.4 = (bf16[2,56,1024]{2,1,0:T(8,128)(2,1)S(1)}, bf16[2,56,1024]{2,1,0:T(8,128)(2,1)S(1)}, u32[]{:S(2)}, u32[]{:S(2)}) collective-permute-start(bf16[2,56,1024]{2,1,0:T(8,128)(2,1)S(1)} %pad_maximum_fusion.3), channel_id=1, source_target_pairs={{0,128},{2,10},{16,144},{18,26},{32,160},{34,42},{48,176},{50,58},... | collective-permute-start | bytes 688136 | tf_op jit(solution)/shard_map/ppermute | solution.py:30
  15.5 29.9 %copy-start = (s32[2]{0:T(128)S(1)}, s32[2]{0:T(128)}, u32[]{:S(2)}) copy-start(s32[2]{0:T(128)} %spread_ref.1) | copy-start | bytes 28
  15.6 10.4 %collective-permute-start.5 = (bf16[2,112,1024]{2,1,0:T(8,128)(2,1)S(1)}, bf16[2,112,1024]{2,1,0:T(8,128)(2,1)S(1)}, u32[]{:S(2)}, u32[]{:S(2)}) collective-permute-start(bf16[2,112,1024]{2,1,0:T(8,128)(2,1)S(1)} %collective-permute-done.1.refs_1_), channel_id=1, source_target_pairs={{0,16},{2,114},{16,32},{18,2},{32,48},{34,18},{48,64},{50,34},{64,... | collective-permute-start | bytes 1376264 | tf_op jit(solution)/shard_map/ppermute | solution.py:30
  17.5 20.0 %collective-permute-start.11 = (bf16[2,224,1024]{2,1,0:T(8,128)(2,1)S(1)}, bf16[2,224,1024]{2,1,0:T(8,128)(2,1)S(1)}, u32[]{:S(2)}, u32[]{:S(2)}) collective-permute-start(bf16[2,224,1024]{2,1,0:T(8,128)(2,1)S(1)} %pad_maximum_fusion.refs_8_), channel_id=1, source_target_pairs={{0,4},{2,3},{16,20},{18,19},{32,36},{34,35},{48,52},{50,51},{64,68... | collective-permute-start | bytes 2752520 | tf_op jit(solution)/shard_map/ppermute | solution.py:30
  19.1 18.4 %collective-permute-start.12 = (bf16[2,224,1024]{2,1,0:T(8,128)(2,1)S(1)}, bf16[2,224,1024]{2,1,0:T(8,128)(2,1)S(1)}, u32[]{:S(2)}, u32[]{:S(2)}) collective-permute-start(bf16[2,224,1024]{2,1,0:T(8,128)(2,1)S(1)} %pad_maximum_fusion.refs_8_), channel_id=1, source_target_pairs={{0,12},{2,131},{16,28},{18,147},{32,44},{34,163},{48,60},{50,179},... | collective-permute-start | bytes 2752520 | tf_op jit(solution)/shard_map/ppermute | solution.py:30
  20.7 22.8 %collective-permute-start.13 = (bf16[2,224,1024]{2,1,0:T(8,128)(2,1)S(1)}, bf16[2,224,1024]{2,1,0:T(8,128)(2,1)S(1)}, u32[]{:S(2)}, u32[]{:S(2)}) collective-permute-start(bf16[2,224,1024]{2,1,0:T(8,128)(2,1)S(1)} %pad_maximum_fusion.refs_8_), channel_id=1, source_target_pairs={{0,8},{2,130},{16,24},{18,146},{32,40},{34,162},{48,56},{50,178},{... | collective-permute-start | bytes 2752520 | tf_op jit(solution)/shard_map/ppermute | solution.py:30
  26.0 9.7 %collective-permute-start.6 = (bf16[2,112,1024]{2,1,0:T(8,128)(2,1)S(1)}, bf16[2,112,1024]{2,1,0:T(8,128)(2,1)S(1)}, u32[]{:S(2)}, u32[]{:S(2)}) collective-permute-start(bf16[2,112,1024]{2,1,0:T(8,128)(2,1)S(1)} %collective-permute-done.5.refs_2_), channel_id=1, source_target_pairs={{0,16},{2,114},{16,32},{18,2},{32,48},{34,18},{48,64},{50,34},{64,... | collective-permute-start | bytes 1376264 | tf_op jit(solution)/shard_map/ppermute | solution.py:30
  35.8 7.7 %collective-permute-start.10 = (bf16[2,56,1024]{2,1,0:T(8,128)(2,1)S(1)}, bf16[2,56,1024]{2,1,0:T(8,128)(2,1)S(1)}, u32[]{:S(2)}, u32[]{:S(2)}) collective-permute-start(bf16[2,56,1024]{2,1,0:T(8,128)(2,1)S(1)} %slice.19), channel_id=1, source_target_pairs={{0,16},{2,114},{16,32},{18,2},{32,48},{34,18},{48,64},{50,34},{64,... | collective-permute-start | bytes 688136 | tf_op jit(solution)/shard_map/ppermute | solution.py:30
  35.8 9.4 %collective-permute-start.7 = (bf16[2,112,1024]{2,1,0:T(8,128)(2,1)S(1)}, bf16[2,112,1024]{2,1,0:T(8,128)(2,1)S(1)}, u32[]{:S(2)}, u32[]{:S(2)}) collective-permute-start(bf16[2,112,1024]{2,1,0:T(8,128)(2,1)S(1)} %collective-permute-done.1.refs_1_), channel_id=1, source_target_pairs={{0,2},{2,0},{16,18},{18,16},{32,34},{34,32},{48,50},{50,48},{64,66... | collective-permute-start | bytes 1376264 | tf_op jit(solution)/shard_map/ppermute | solution.py:30
  37.5 7.8 %collective-permute-start.8 = (bf16[2,112,1024]{2,1,0:T(8,128)(2,1)S(1)}, bf16[2,112,1024]{2,1,0:T(8,128)(2,1)S(1)}, u32[]{:S(2)}, u32[]{:S(2)}) collective-permute-start(bf16[2,112,1024]{2,1,0:T(8,128)(2,1)S(1)} %collective-permute-done.5.refs_2_), channel_id=1, source_target_pairs={{0,2},{2,0},{16,18},{18,16},{32,34},{34,32},{48,50},{50,48},{64,66... | collective-permute-start | bytes 1376264 | tf_op jit(solution)/shard_map/ppermute | solution.py:30
  37.5 7.8 %collective-permute-start.9 = (bf16[2,112,1024]{2,1,0:T(8,128)(2,1)S(1)}, bf16[2,112,1024]{2,1,0:T(8,128)(2,1)S(1)}, u32[]{:S(2)}, u32[]{:S(2)}) collective-permute-start(bf16[2,112,1024]{2,1,0:T(8,128)(2,1)S(1)} %collective-permute-done.6.refs_3_), channel_id=1, source_target_pairs={{0,2},{2,0},{16,18},{18,16},{32,34},{34,32},{48,50},{50,48},{64,66... | collective-permute-start | bytes 1376264 | tf_op jit(solution)/shard_map/ppermute | solution.py:30
  43.5 1.8 %collective-permute-start.14 = (bf16[2,56,1024]{2,1,0:T(8,128)(2,1)S(1)}, bf16[2,56,1024]{2,1,0:T(8,128)(2,1)S(1)}, u32[]{:S(2)}, u32[]{:S(2)}) collective-permute-start(bf16[2,56,1024]{2,1,0:T(8,128)(2,1)S(1)} %collective-permute-done.10), channel_id=1, source_target_pairs={{0,2},{2,0},{16,18},{18,16},{32,34},{34,32},{48,50},{50,48},{64,66... | collective-permute-start | bytes 688136 | tf_op jit(solution)/shard_map/ppermute | solution.py:30
  51.9 1.3 %collective-permute-start.15 = (f32[8,896]{1,0:T(8,128)S(1)}, f32[8,896]{1,0:T(8,128)S(1)}, u32[]{:S(2)}, u32[]{:S(2)}) collective-permute-start(f32[8,896]{1,0:T(8,128)S(1)} %gram.1), channel_id=1, source_target_pairs={{0,2},{2,0},{16,18},{18,16},{32,34},{34,32},{48,50},{50,48},{64,66... | collective-permute-start | bytes 86024 | tf_op jit(solution)/shard_map/ppermute | solution.py:30
  53.2 3.9 %collective-permute-start.16 = (f32[8,896]{1,0:T(8,128)S(1)}, f32[8,896]{1,0:T(8,128)S(1)}, u32[]{:S(2)}, u32[]{:S(2)}) collective-permute-start(f32[8,896]{1,0:T(8,128)S(1)} %add.24), channel_id=1, source_target_pairs={{0,16},{2,18},{16,0},{18,2},{32,48},{34,50},{48,32},{50,34},{64,80... | collective-permute-start | bytes 86024 | tf_op jit(solution)/shard_map/ppermute | solution.py:30
  57.1 8.9 %collective-permute-start.17 = (f32[8,896]{1,0:T(8,128)S(1)}, f32[8,896]{1,0:T(8,128)S(1)}, u32[]{:S(2)}, u32[]{:S(2)}) collective-permute-start(f32[8,896]{1,0:T(8,128)S(1)} %add.25), channel_id=1, source_target_pairs={{0,64},{2,66},{16,80},{18,82},{32,96},{34,98},{48,112},{50,114},{6... | collective-permute-start | bytes 86024 | tf_op jit(solution)/shard_map/ppermute | solution.py:30
  61.9 6.0 %collective-permute-start.18 = (f32[8,896]{1,0:T(8,128)S(1)}, f32[8,896]{1,0:T(8,128)S(1)}, u32[]{:S(2)}, u32[]{:S(2)}) collective-permute-start(f32[8,896]{1,0:T(8,128)S(1)} %add.25), channel_id=1, source_target_pairs={{0,32},{2,34},{16,48},{18,50},{32,64},{34,66},{48,80},{50,82},{64,... | collective-permute-start | bytes 86024 | tf_op jit(solution)/shard_map/ppermute | solution.py:30
  62.4 5.5 %collective-permute-start.19 = (f32[8,896]{1,0:T(8,128)S(1)}, f32[8,896]{1,0:T(8,128)S(1)}, u32[]{:S(2)}, u32[]{:S(2)}) collective-permute-start(f32[8,896]{1,0:T(8,128)S(1)} %add.25), channel_id=1, source_target_pairs={{0,96},{2,98},{16,112},{18,114},{32,0},{34,2},{48,16},{50,18},{64,... | collective-permute-start | bytes 86024 | tf_op jit(solution)/shard_map/ppermute | solution.py:30
  67.9 5.2 %collective-permute-start.20 = (f32[8,128]{1,0:T(8,128)S(1)}, f32[8,128]{1,0:T(8,128)S(1)}, u32[]{:S(2)}, u32[]{:S(2)}) collective-permute-start(f32[8,128]{1,0:T(8,128)S(1)} %maximum_reduce_fusion), channel_id=1, source_target_pairs={{0,128},{2,130},{16,144},{18,146},{32,160},{34,162},{48,176},{50,1... | collective-permute-start | bytes 12296 | tf_op jit(solution)/shard_map/ppermute | solution.py:30
  69.9 3.6 %collective-permute-start.21 = (f32[8,128]{1,0:T(8,128)S(1)}, f32[8,128]{1,0:T(8,128)S(1)}, u32[]{:S(2)}, u32[]{:S(2)}) collective-permute-start(f32[8,128]{1,0:T(8,128)S(1)} %maximum_reduce_fusion), channel_id=1, source_target_pairs={{0,1},{2,3},{16,17},{18,19},{32,33},{34,35},{48,49},{50,51},{64,65... | collective-permute-start | bytes 12296 | tf_op jit(solution)/shard_map/ppermute | solution.py:30
  70.9 4.8 %collective-permute-start.22 = (f32[8,128]{1,0:T(8,128)S(1)}, f32[8,128]{1,0:T(8,128)S(1)}, u32[]{:S(2)}, u32[]{:S(2)}) collective-permute-start(f32[8,128]{1,0:T(8,128)S(1)} %maximum_reduce_fusion), channel_id=1, source_target_pairs={{0,129},{2,131},{16,145},{18,147},{32,161},{34,163},{48,177},{50,1... | collective-permute-start | bytes 12296 | tf_op jit(solution)/shard_map/ppermute | solution.py:30
  75.7 5.4 %collective-permute-start.23 = (f32[8,128]{1,0:T(8,128)S(1)}, f32[8,128]{1,0:T(8,128)S(1)}, u32[]{:S(2)}, u32[]{:S(2)}) collective-permute-start(f32[8,128]{1,0:T(8,128)S(1)} %add_add_fusion.1.sums_ref), channel_id=1, source_target_pairs={{0,4},{2,6},{16,20},{18,22},{32,36},{34,38},{48,52},{50,54},{64,68... | collective-permute-start | bytes 12296 | tf_op jit(solution)/shard_map/ppermute | solution.py:30
  77.3 3.8 %collective-permute-start.24 = (f32[8,128]{1,0:T(8,128)S(1)}, f32[8,128]{1,0:T(8,128)S(1)}, u32[]{:S(2)}, u32[]{:S(2)}) collective-permute-start(f32[8,128]{1,0:T(8,128)S(1)} %add_add_fusion.1.sums_ref), channel_id=1, source_target_pairs={{0,12},{2,14},{16,28},{18,30},{32,44},{34,46},{48,60},{50,62},{64,... | collective-permute-start | bytes 12296 | tf_op jit(solution)/shard_map/ppermute | solution.py:30
  79.1 5.1 %collective-permute-start.25 = (f32[8,128]{1,0:T(8,128)S(1)}, f32[8,128]{1,0:T(8,128)S(1)}, u32[]{:S(2)}, u32[]{:S(2)}) collective-permute-start(f32[8,128]{1,0:T(8,128)S(1)} %add_add_fusion.1.sums_ref), channel_id=1, source_target_pairs={{0,8},{2,10},{16,24},{18,26},{32,40},{34,42},{48,56},{50,58},{64,7... | collective-permute-start | bytes 12296 | tf_op jit(solution)/shard_map/ppermute | solution.py:30

commit v6 on v5

--- a/solution.py
+++ b/solution.py
@@ -64,11 +64,39 @@
     return result
 
 
-def gram_body(n_line, spread_ref, *refs):
-    line, pieces = refs[:n_line], refs[n_line:-4]
-    out_ref, z_ref, w_ref, norm_ref = refs[-4:]
+def plane_body(spread_ref, *refs):
+    pieces, (w_ref, norm_ref) = refs[:-2], refs[-2:]
+    tall = pieces[0].shape[1]
+    for layer in range(2):
+        factor = LOG2E / jnp.full((1, 128), spread_ref[layer].astype(jnp.float32), jnp.float32)
+        for index, piece in enumerate(pieces):
+            rows = slice(index * tall, (index + 1) * tall)
+            block = piece[layer]
+            w_ref[layer, rows, :] = block
+            norms = jnp.sum(fold_squares(block), axis=1, keepdims=True)
+            norm_ref[layer, rows, :] = jnp.broadcast_to(norms, (tall, 128)) * (0.5 * factor)
+
+
+def plane_rows(spread, pieces):
+    vmem = pl.BlockSpec(memory_space=pltpu.VMEM)
+    rows = sum(piece.shape[1] for piece in pieces)
+    return pl.pallas_call(
+        plane_body,
+        out_shape=(
+            jax.ShapeDtypeStruct((2, rows, D), jnp.bfloat16),
+            jax.ShapeDtypeStruct((2, rows, 128), jnp.float32),
+        ),
+        in_specs=[pl.BlockSpec(memory_space=pltpu.SMEM)] + [vmem] * len(pieces),
+        out_specs=(vmem, vmem),
+        compiler_params=pltpu.CompilerParams(vmem_limit_bytes=16 << 20),
+        cost_estimate=pl.CostEstimate(flops=4 * rows * D, bytes_accessed=8 * rows * D, transcendentals=0),
+        name="plane_rows",
+    )(spread, *pieces)
+
+
+def gram_body(spread_ref, w_ref, norm_ref, *refs):
+    line, (out_ref, z_ref) = refs[:-2], refs[-2:]
     width = z_ref.shape[1]
-    tall = pieces[0].shape[1]
     scales = [jnp.full((1, 128), spread_ref[layer].astype(jnp.float32), jnp.float32) for layer in range(2)]
     factors = [LOG2E / scale for scale in scales]
     offsets = [jnp.exp(-D / scale) for scale in scales]
@@ -76,13 +104,6 @@
     for ref in line:
         z_ref[:, at : at + ref.shape[1], :] = ref[...]
         at += ref.shape[1]
-    for index, piece in enumerate(pieces):
-        rows = slice(index * tall, (index + 1) * tall)
-        for layer in range(2):
-            block = piece[layer]
-            w_ref[layer, rows, :] = block
-            norms = jnp.sum(fold_squares(block), axis=1, keepdims=True)
-            norm_ref[layer, rows, :] = jnp.broadcast_to(norms, (tall, 128)) * (0.5 * factors[layer])
     columns = []
     height = w_ref.shape[1] // 2
     for start in range(0, width, 256):
@@ -119,29 +140,34 @@
     other.update({place: place - 6 for place in range(8, 14)})
     local = jnp.where(lax.axis_index("core") == 0, local, shuffled(local, other, count))
     near = {0: 0, 1: 1, 2: 14, 3: 15, 4: 12, 5: 13, 6: 10, 7: 11, 8: 3, 9: 2, 10: 5, 11: 4, 12: 7, 13: 6, 14: 8, 15: 9}
-    out_ref[...] = pltpu.roll(shuffled(local, near, count), lax.axis_index("z") * (NC * count), 1)
-
-
-def gram(spread, line, pieces):
+    local = pltpu.roll(shuffled(local, near, count), lax.axis_index("z") * (NC * count), 1)
+    parts = [local[:, start : start + 128] for start in range(0, width, 128)]
+    folded = functools.reduce(lambda total, part: total + part, parts)
+    for index, part in enumerate(parts):
+        out_ref[index : index + 1, :] = part[0:1]
+        out_ref[8 + index : 9 + index, :] = part[1:2]
+    out_ref[7:8, :] = folded[2:3]
+    halves = folded + pltpu.roll(folded, 64, 1)
+    left = lax.broadcasted_iota(jnp.int32, (1, 128), 1) < 64
+    out_ref[15:16, :] = jnp.where(left, halves[3:4], halves[4:5])
+
+
+def gram(spread, columns, norms, line):
     vmem = pl.BlockSpec(memory_space=pltpu.VMEM)
-    rows = sum(piece.shape[1] for piece in pieces)
+    rows = columns.shape[1]
     width = sum(part.shape[1] for part in line)
     return pl.pallas_call(
-        functools.partial(gram_body, len(line)),
-        out_shape=jax.ShapeDtypeStruct((8, width), jnp.float32),
-        in_specs=[pl.BlockSpec(memory_space=pltpu.SMEM)] + [vmem] * (len(line) + len(pieces)),
+        gram_body,
+        out_shape=jax.ShapeDtypeStruct((16, 128), jnp.float32),
+        in_specs=[pl.BlockSpec(memory_space=pltpu.SMEM)] + [vmem] * (2 + len(line)),
         out_specs=vmem,
-        scratch_shapes=[
-            pltpu.VMEM((2, width, D), jnp.bfloat16),
-            pltpu.VMEM((2, rows, D), jnp.bfloat16),
-            pltpu.VMEM((2, rows, 128), jnp.float32),
-        ],
-        compiler_params=pltpu.CompilerParams(vmem_limit_bytes=24 << 20),
+        scratch_shapes=[pltpu.VMEM((2, width, D), jnp.bfloat16)],
+        compiler_params=pltpu.CompilerParams(vmem_limit_bytes=20 << 20),
         cost_estimate=pl.CostEstimate(
             flops=4 * rows * width * D, bytes_accessed=4 * (rows + width) * D, transcendentals=2 * rows * width
         ),
         name="gram",
-    )(spread, *line, *pieces)
+    )(spread, columns, norms, *line)
 
 
 def swap(array):
@@ -172,17 +198,22 @@
 
 def finish_body(total, count, part_ref, sums_ref, *refs):
     parts, (profiles_ref, alignment_ref) = refs[:3], refs[3:]
-    sums = jnp.sum(ring_sum(sums_ref[...], [part[...] for part in parts]), axis=1, keepdims=True)
-    sum_one, sum_two, f_cross, f_one, f_two, c_cross, c_one, c_two = (sums[at : at + 1, :] for at in range(8))
+    lanes = ring_sum(sums_ref[...], [part[...] for part in parts])
+    sums = jnp.sum(lanes, axis=1, keepdims=True)
+    sum_one, sum_two, f_cross, _, c_cross, c_one, c_two = (sums[at : at + 1, :] for at in range(7))
+    left = lax.broadcasted_iota(jnp.int32, (1, 128), 1) < 64
+    f_one = jnp.sum(jnp.where(left, lanes[3:4], 0.0), axis=1, keepdims=True)
+    f_two = jnp.sum(jnp.where(left, 0.0, lanes[3:4]), axis=1, keepdims=True)
     h_cross = f_cross - 2.0 * c_cross / total + sum_one * sum_two / (total * total)
     h_one = f_one - 2.0 * c_one / total + sum_one * sum_one / (total * total)
     h_two = f_two - 2.0 * c_two / total + sum_two * sum_two / (total * total)
     alignment_ref[...] = h_cross / jnp.sqrt(h_one * h_two)
-    width = part_ref.shape[1]
+    width = NZ * NC * count
     first = (lax.axis_index("z") * NC + lax.axis_index("core")) * count
-    rows = pltpu.roll(part_ref[...], lax.rem(width - first, width), 1)
-    roots = jnp.sqrt(jnp.concatenate([c_one, c_two], axis=0) / total)
-    profiles_ref[...] = rows[:2, :count] / roots
+    for layer, c_sum in enumerate((c_one, c_two)):
+        rows = jnp.concatenate([part_ref[8 * layer + at : 8 * layer + at + 1, :] for at in range(7)], axis=1)
+        rows = pltpu.roll(jnp.broadcast_to(rows, (8, width)), lax.rem(width - first, width), 1)
+        profiles_ref[layer : layer + 1, :] = rows[:1, :count] / jnp.sqrt(c_sum / total)
 
 
 def finish(part, sums, parts, total, count):
@@ -209,13 +240,12 @@
     for _ in range(2):
         ring.append(around(ring[-1]))
     last = around(ring[2][:, :count])
-    pieces, late = lax.optimization_barrier((pieces, last))
-    ends = jnp.concatenate([last, swap(late)], axis=1)
+    ends = jnp.concatenate([last, swap(last)], axis=1)
     line = [chip] + ring + [swap(block) for block in ring] + [ends]
-    part = line_sum(gram(spread, line, pieces))
-    r_one, r_two = part[0], part[1]
-    sums = jnp.stack([r_one, r_two, part[2], part[3], part[4], r_one * r_two, r_one * r_one, r_two * r_two])
-    sums = jnp.sum(sums.reshape(8, part.shape[1] // 128, 128), axis=1)
+    part = line_sum(gram(spread, *plane_rows(spread, pieces), line))
+    r_one, r_two = part[0:7], part[8:15]
+    terms = [r_one, r_two, part[7:8], part[15:16], r_one * r_two, r_one * r_one, r_two * r_two]
+    sums = jnp.stack([jnp.sum(term, axis=0) for term in terms] + [jnp.zeros((128,), jnp.float32)])
     sums = ring_sum(sums, ring_parts(sums, "x"))
     profiles, alignment = finish(part, sums, ring_parts(sums, "y"), count * lax.axis_size(AXES), count)
     return (profiles, alignment.reshape(()))

time: 85.1 us -> 84 us (0.987)
  waiting for transfers between devices: 35.1 us -> 33.5 us
  Pallas kernels: 7.31 us -> 8.22 us
    ppermute x26, waiting for transfers between devices: 35.1 us -> 33.5 us  [move(): return lax.ppermute(array, AXES, pairs)]
    pallas_call x1 -> x2, Pallas kernels: 6.57 us -> 7.55 us  [the longest x1 6.17 us: gram(): pl.pallas_call(gram_body, out_shape=jax.ShapeDtypeStruct((16, 128), jnp.f...]
  transfers between devices with their start and end apart: 26 -> 26, of which waited for: 14 -> 14; matrix products, arithmetic and copies ran while one was open for 0% -> 0% of each run, Pallas kernels for 0% -> 2%
where the time goes in v6:
time: 84 us; the launch traced here: 83.9 us
  starting transfers between devices  40.3 us (48%)
  waiting for transfers between devices  33.5 us (40%)
  Pallas kernels  8.22 us (10%)
  other arithmetic  1.15 us (1%)
    ppermute x26, starting transfers between devices, move(): return lax.ppermute(array, AXES, pairs)  40.3 us
    ppermute x26, waiting for transfers between devices, move(): return lax.ppermute(array, AXES, pairs)  33.5 us
    pallas_call x1, Pallas kernels, gram(): pl.pallas_call(gram_body, out_shape=jax.ShapeDtypeStruct((16, 128), jnp.f...  6.17 us
  transfers between devices with their start and end apart: 26, of which 14 were waited for; matrix products, arithmetic and copies ran while one was open for 0% of the time, Pallas kernels for 2%

profile of v6, /device:TPU:6, one launch (start us, length us, event | category | flops | bytes accessed | tf_op | source)
XLA Modules:
  0.0 83.9 jit_solution(14740064531638715167)
XLA Ops:
  0.6 1.0 %pad_maximum_fusion.3 = bf16[2,56,1024]{2,1,0:T(8,128)(2,1)S(1)} fusion(bf16[1,56,1024]{2,1,0:T(8,128)(2,1)} %bitcast.8, bf16[1,56,1024]{2,1,0:T(8,128)(2,1)} %bitcast.9), kind=kLoop, calls=%fused_computation.3 | loop fusion | flops 114688 | bytes 458752 | tf_op jit(solution)/shard_map/stack | solution.py:232
  1.7 1.5 %collective-permute-done = bf16[2,56,1024]{2,1,0:T(8,128)(2,1)S(1)} collective-permute-done((bf16[2,56,1024]{2,1,0:T(8,128)(2,1)S(1)}, bf16[2,56,1024]{2,1,0:T(8,128)(2,1)S(1)}, u32[]{:S(2)}, u32[]{:S(2)}) %collective-permute-start) | collective-permute-done | bytes 229408 | tf_op jit(solution)/shard_map/ppermute | solution.py:30
  3.2 2.0 %collective-permute-start.1 = (bf16[2,112,1024]{2,1,0:T(8,128)(2,1)S(1)}, bf16[2,112,1024]{2,1,0:T(8,128)(2,1)S(1)}, u32[]{:S(2)}, u32[]{:S(2)}) collective-permute-start(bf16[2,112,1024]{2,1,0:T(8,128)(2,1)S(1)} %pad_maximum_fusion.1.refs_0_), channel_id=1, source_target_pairs={{0,16},{2,114},{16,32},{18,2},{32,48},{34,18},{48,64},{50,34},{64,... | collective-permute-start | bytes 1376264 | tf_op jit(solution)/shard_map/ppermute | solution.py:30
  5.7 1.5 %collective-permute-start.3 = (bf16[2,56,1024]{2,1,0:T(8,128)(2,1)S(1)}, bf16[2,56,1024]{2,1,0:T(8,128)(2,1)S(1)}, u32[]{:S(2)}, u32[]{:S(2)}) collective-permute-start(bf16[2,56,1024]{2,1,0:T(8,128)(2,1)S(1)} %pad_maximum_fusion.3), channel_id=1, source_target_pairs={{0,129},{2,14},{16,145},{18,30},{32,161},{34,46},{48,177},{50,62},... | collective-permute-start | bytes 688136 | tf_op jit(solution)/shard_map/ppermute | solution.py:30
  7.3 1.4 %collective-permute-start.4 = (bf16[2,56,1024]{2,1,0:T(8,128)(2,1)S(1)}, bf16[2,56,1024]{2,1,0:T(8,128)(2,1)S(1)}, u32[]{:S(2)}, u32[]{:S(2)}) collective-permute-start(bf16[2,56,1024]{2,1,0:T(8,128)(2,1)S(1)} %pad_maximum_fusion.3), channel_id=1, source_target_pairs={{0,128},{2,10},{16,144},{18,26},{32,160},{34,42},{48,176},{50,58},... | collective-permute-start | bytes 688136 | tf_op jit(solution)/shard_map/ppermute | solution.py:30
  8.7 2.6 %collective-permute-done.2 = bf16[2,56,1024]{2,1,0:T(8,128)(2,1)S(1)} collective-permute-done((bf16[2,56,1024]{2,1,0:T(8,128)(2,1)S(1)}, bf16[2,56,1024]{2,1,0:T(8,128)(2,1)S(1)}, u32[]{:S(2)}, u32[]{:S(2)}) %collective-permute-start.2) | collective-permute-done | bytes 229408 | tf_op jit(solution)/shard_map/ppermute | solution.py:30
  11.3 4.1 %collective-permute-done.3 = bf16[2,56,1024]{2,1,0:T(8,128)(2,1)S(1)} collective-permute-done((bf16[2,56,1024]{2,1,0:T(8,128)(2,1)S(1)}, bf16[2,56,1024]{2,1,0:T(8,128)(2,1)S(1)}, u32[]{:S(2)}, u32[]{:S(2)}) %collective-permute-start.3) | collective-permute-done | bytes 229408 | tf_op jit(solution)/shard_map/ppermute | solution.py:30
  15.6 1.9 %collective-permute-start.8 = (bf16[2,112,1024]{2,1,0:T(8,128)(2,1)S(1)}, bf16[2,112,1024]{2,1,0:T(8,128)(2,1)S(1)}, u32[]{:S(2)}, u32[]{:S(2)}) collective-permute-start(bf16[2,112,1024]{2,1,0:T(8,128)(2,1)S(1)} %collective-permute-done.1.refs_1_), channel_id=1, source_target_pairs={{0,16},{2,114},{16,32},{18,2},{32,48},{34,18},{48,64},{50,34},{64,... | collective-permute-start | bytes 1376264 | tf_op jit(solution)/shard_map/ppermute | solution.py:30
  17.5 1.6 %collective-permute-start.5 = (bf16[2,224,1024]{2,1,0:T(8,128)(2,1)S(1)}, bf16[2,224,1024]{2,1,0:T(8,128)(2,1)S(1)}, u32[]{:S(2)}, u32[]{:S(2)}) collective-permute-start(bf16[2,224,1024]{2,1,0:T(8,128)(2,1)S(1)} %pad_maximum_fusion.refs_0_), channel_id=1, source_target_pairs={{0,4},{2,3},{16,20},{18,19},{32,36},{34,35},{48,52},{50,51},{64,68... | collective-permute-start | bytes 2752520 | tf_op jit(solution)/shard_map/ppermute | solution.py:30
  19.1 1.7 %collective-permute-start.6 = (bf16[2,224,1024]{2,1,0:T(8,128)(2,1)S(1)}, bf16[2,224,1024]{2,1,0:T(8,128)(2,1)S(1)}, u32[]{:S(2)}, u32[]{:S(2)}) collective-permute-start(bf16[2,224,1024]{2,1,0:T(8,128)(2,1)S(1)} %pad_maximum_fusion.refs_0_), channel_id=1, source_target_pairs={{0,12},{2,131},{16,28},{18,147},{32,44},{34,163},{48,60},{50,179},... | collective-permute-start | bytes 2752520 | tf_op jit(solution)/shard_map/ppermute | solution.py:30
  20.7 2.0 %collective-permute-start.7 = (bf16[2,224,1024]{2,1,0:T(8,128)(2,1)S(1)}, bf16[2,224,1024]{2,1,0:T(8,128)(2,1)S(1)}, u32[]{:S(2)}, u32[]{:S(2)}) collective-permute-start(bf16[2,224,1024]{2,1,0:T(8,128)(2,1)S(1)} %pad_maximum_fusion.refs_0_), channel_id=1, source_target_pairs={{0,8},{2,130},{16,24},{18,146},{32,40},{34,162},{48,56},{50,178},{... | collective-permute-start | bytes 2752520 | tf_op jit(solution)/shard_map/ppermute | solution.py:30
  22.7 3.3 %collective-permute-done.8.refs_2_ = bf16[2,112,1024]{2,1,0:T(8,128)(2,1)S(1)} collective-permute-done((bf16[2,112,1024]{2,1,0:T(8,128)(2,1)S(1)}, bf16[2,112,1024]{2,1,0:T(8,128)(2,1)S(1)}, u32[]{:S(2)}, u32[]{:S(2)}) %collective-permute-start.8) | collective-permute-done | bytes 458784 | tf_op jit(solution)/shard_map/ppermute | solution.py:30
  26.1 9.7 %collective-permute-done.9.refs_3_ = bf16[2,112,1024]{2,1,0:T(8,128)(2,1)S(1)} collective-permute-done((bf16[2,112,1024]{2,1,0:T(8,128)(2,1)S(1)}, bf16[2,112,1024]{2,1,0:T(8,128)(2,1)S(1)}, u32[]{:S(2)}, u32[]{:S(2)}) %collective-permute-start.9) | collective-permute-done | bytes 458784 | tf_op jit(solution)/shard_map/ppermute | solution.py:30
  35.8 1.6 %collective-permute-start.10 = (bf16[2,112,1024]{2,1,0:T(8,128)(2,1)S(1)}, bf16[2,112,1024]{2,1,0:T(8,128)(2,1)S(1)}, u32[]{:S(2)}, u32[]{:S(2)}) collective-permute-start(bf16[2,112,1024]{2,1,0:T(8,128)(2,1)S(1)} %collective-permute-done.1.refs_1_), channel_id=1, source_target_pairs={{0,2},{2,0},{16,18},{18,16},{32,34},{34,32},{48,50},{50,48},{64,66... | collective-permute-start | bytes 1376264 | tf_op jit(solution)/shard_map/ppermute | solution.py:30
  37.5 6.0 %collective-permute-start.12 = (bf16[2,112,1024]{2,1,0:T(8,128)(2,1)S(1)}, bf16[2,112,1024]{2,1,0:T(8,128)(2,1)S(1)}, u32[]{:S(2)}, u32[]{:S(2)}) collective-permute-start(bf16[2,112,1024]{2,1,0:T(8,128)(2,1)S(1)} %collective-permute-done.9.refs_3_), channel_id=1, source_target_pairs={{0,2},{2,0},{16,18},{18,16},{32,34},{34,32},{48,50},{50,48},{64,66... | collective-permute-start | bytes 1376264 | tf_op jit(solution)/shard_map/ppermute | solution.py:30
  43.5 1.4 %plane_rows.1 = (bf16[2,896,1024]{2,1,0:T(8,128)(2,1)S(1)}, f32[2,896,128]{2,1,0:T(8,128)S(1)}) custom-call(s32[2]{0:T(128)S(1)} %copy-done, bf16[2,224,1024]{2,1,0:T(8,128)(2,1)S(1)} %pad_maximum_fusion.refs_0_, bf16[2,224,1024]{2,1,0:T(8,128)(2,1)S(1)} %collective-permute-done.5.refs_1_, bf16[2,224,1024]{2,1,0:T(8,128)(2,1)S(1)} %collective-permute-done.6.refs_2_, ...), custom_call_target="tpu_custom_call" | custom-call | flops 3670016 | bytes 7340032 | tf_op jit(solution)/shard_map/plane_rows/pallas_call | solution.py:83
  45.3 6.2 %gram.1 = f32[16,128]{1,0:T(8,128)S(1)} custom-call(s32[2]{0:T(128)S(1)} %copy-done, bf16[2,896,1024]{2,1,0:T(8,128)(2,1)S(1)} %get-tuple-element.9.w_ref, f32[2,896,128]{2,1,0:T(8,128)S(1)} %get-tuple-element.10.norm_ref, bf16[2,112,1024]{2,1,0:T(8,128)(2,1)S(1)} %pad_maximum_fusion.1.refs_0_, bf16[2,112,1024]{2,1,0:T(8,128)(2,1)S(1)} %collective-permute-done.1.refs_1_, ...), custom_call_target="tpu_custom_call" | custom-call | flops 3288334336 | bytes 7340032 | tf_op jit(solution)/shard_map/gram/pallas_call | solution.py:159
  51.9 0.8 collective-permute-done.15
  52.7 1.2 %collective-permute-start.16 = (f32[16,128]{1,0:T(8,128)S(1)}, f32[16,128]{1,0:T(8,128)S(1)}, u32[]{:S(2)}, u32[]{:S(2)}) collective-permute-start(f32[16,128]{1,0:T(8,128)S(1)} %add.24), channel_id=1, source_target_pairs={{0,16},{2,18},{16,0},{18,2},{32,48},{34,50},{48,32},{50,34},{64,80... | collective-permute-start | bytes 24584 | tf_op jit(solution)/shard_map/ppermute | solution.py:30
  53.9 2.5 %collective-permute-done.16 = f32[16,128]{1,0:T(8,128)S(1)} collective-permute-done((f32[16,128]{1,0:T(8,128)S(1)}, f32[16,128]{1,0:T(8,128)S(1)}, u32[]{:S(2)}, u32[]{:S(2)}) %collective-permute-start.16) | collective-permute-done | bytes 8224 | tf_op jit(solution)/shard_map/ppermute | solution.py:30
  56.4 4.8 %collective-permute-start.17 = (f32[16,128]{1,0:T(8,128)S(1)}, f32[16,128]{1,0:T(8,128)S(1)}, u32[]{:S(2)}, u32[]{:S(2)}) collective-permute-start(f32[16,128]{1,0:T(8,128)S(1)} %add.25), channel_id=1, source_target_pairs={{0,64},{2,66},{16,80},{18,82},{32,96},{34,98},{48,112},{50,114},{6... | collective-permute-start | bytes 24584 | tf_op jit(solution)/shard_map/ppermute | solution.py:30
  61.6 3.8 %collective-permute-start.19 = (f32[16,128]{1,0:T(8,128)S(1)}, f32[16,128]{1,0:T(8,128)S(1)}, u32[]{:S(2)}, u32[]{:S(2)}) collective-permute-start(f32[16,128]{1,0:T(8,128)S(1)} %add.25), channel_id=1, source_target_pairs={{0,96},{2,98},{16,112},{18,114},{32,0},{34,2},{48,16},{50,18},{64,... | collective-permute-start | bytes 24584 | tf_op jit(solution)/shard_map/ppermute | solution.py:30
  65.4 1.6 %collective-permute-done.18 = f32[16,128]{1,0:T(8,128)S(1)} collective-permute-done((f32[16,128]{1,0:T(8,128)S(1)}, f32[16,128]{1,0:T(8,128)S(1)}, u32[]{:S(2)}, u32[]{:S(2)}) %collective-permute-start.18) | collective-permute-done | bytes 8224 | tf_op jit(solution)/shard_map/ppermute | solution.py:30
  67.1 1.9 %collective-permute-start.20 = (f32[8,128]{1,0:T(8,128)S(1)}, f32[8,128]{1,0:T(8,128)S(1)}, u32[]{:S(2)}, u32[]{:S(2)}) collective-permute-start(f32[8,128]{1,0:T(8,128)S(1)} %stack.37), channel_id=1, source_target_pairs={{0,128},{2,130},{16,144},{18,146},{32,160},{34,162},{48,176},{50,1... | collective-permute-start | bytes 12296 | tf_op jit(solution)/shard_map/ppermute | solution.py:30
  69.0 1.1 %collective-permute-start.21 = (f32[8,128]{1,0:T(8,128)S(1)}, f32[8,128]{1,0:T(8,128)S(1)}, u32[]{:S(2)}, u32[]{:S(2)}) collective-permute-start(f32[8,128]{1,0:T(8,128)S(1)} %stack.37), channel_id=1, source_target_pairs={{0,1},{2,3},{16,17},{18,19},{32,33},{34,35},{48,49},{50,51},{64,65... | collective-permute-start | bytes 12296 | tf_op jit(solution)/shard_map/ppermute | solution.py:30
  70.0 1.0 %collective-permute-start.22 = (f32[8,128]{1,0:T(8,128)S(1)}, f32[8,128]{1,0:T(8,128)S(1)}, u32[]{:S(2)}, u32[]{:S(2)}) collective-permute-start(f32[8,128]{1,0:T(8,128)S(1)} %stack.37), channel_id=1, source_target_pairs={{0,129},{2,131},{16,145},{18,147},{32,161},{34,163},{48,177},{50,1... | collective-permute-start | bytes 12296 | tf_op jit(solution)/shard_map/ppermute | solution.py:30
  71.0 1.3 %collective-permute-done.20 = f32[8,128]{1,0:T(8,128)S(1)} collective-permute-done((f32[8,128]{1,0:T(8,128)S(1)}, f32[8,128]{1,0:T(8,128)S(1)}, u32[]{:S(2)}, u32[]{:S(2)}) %collective-permute-start.20) | collective-permute-done | bytes 4128 | tf_op jit(solution)/shard_map/ppermute | solution.py:30
  72.6 2.3 %collective-permute-done.22 = f32[8,128]{1,0:T(8,128)S(1)} collective-permute-done((f32[8,128]{1,0:T(8,128)S(1)}, f32[8,128]{1,0:T(8,128)S(1)}, u32[]{:S(2)}, u32[]{:S(2)}) %collective-permute-start.22) | collective-permute-done | bytes 4128 | tf_op jit(solution)/shard_map/ppermute | solution.py:30
  74.9 1.6 %collective-permute-start.23 = (f32[8,128]{1,0:T(8,128)S(1)}, f32[8,128]{1,0:T(8,128)S(1)}, u32[]{:S(2)}, u32[]{:S(2)}) collective-permute-start(f32[8,128]{1,0:T(8,128)S(1)} %add_add_fusion.1.sums_ref), channel_id=1, source_target_pairs={{0,4},{2,6},{16,20},{18,22},{32,36},{34,38},{48,52},{50,54},{64,68... | collective-permute-start | bytes 12296 | tf_op jit(solution)/shard_map/ppermute | solution.py:30
  76.4 1.7 %collective-permute-start.24 = (f32[8,128]{1,0:T(8,128)S(1)}, f32[8,128]{1,0:T(8,128)S(1)}, u32[]{:S(2)}, u32[]{:S(2)}) collective-permute-start(f32[8,128]{1,0:T(8,128)S(1)} %add_add_fusion.1.sums_ref), channel_id=1, source_target_pairs={{0,12},{2,14},{16,28},{18,30},{32,44},{34,46},{48,60},{50,62},{64,... | collective-permute-start | bytes 12296 | tf_op jit(solution)/shard_map/ppermute | solution.py:30
  78.1 2.2 %collective-permute-start.25 = (f32[8,128]{1,0:T(8,128)S(1)}, f32[8,128]{1,0:T(8,128)S(1)}, u32[]{:S(2)}, u32[]{:S(2)}) collective-permute-start(f32[8,128]{1,0:T(8,128)S(1)} %add_add_fusion.1.sums_ref), channel_id=1, source_target_pairs={{0,8},{2,10},{16,24},{18,26},{32,40},{34,42},{48,56},{50,58},{64,7... | collective-permute-start | bytes 12296 | tf_op jit(solution)/shard_map/ppermute | solution.py:30
  80.3 2.9 %collective-permute-done.25.refs_2_ = f32[8,128]{1,0:T(8,128)S(1)} collective-permute-done((f32[8,128]{1,0:T(8,128)S(1)}, f32[8,128]{1,0:T(8,128)S(1)}, u32[]{:S(2)}, u32[]{:S(2)}) %collective-permute-start.25) | collective-permute-done | bytes 4128 | tf_op jit(solution)/shard_map/ppermute | solution.py:30
  (38 shorter events, 3.2 us)
Async XLA Ops:
  0.6 42.9 %copy-start = (s32[2]{0:T(128)S(1)}, s32[2]{0:T(128)}, u32[]{:S(2)}) copy-start(s32[2]{0:T(128)} %spread_ref.3) | copy-start | bytes 28
  1.6 1.6 %collective-permute-start = (bf16[2,56,1024]{2,1,0:T(8,128)(2,1)S(1)}, bf16[2,56,1024]{2,1,0:T(8,128)(2,1)S(1)}, u32[]{:S(2)}, u32[]{:S(2)}) collective-permute-start(bf16[2,56,1024]{2,1,0:T(8,128)(2,1)S(1)} %pad_maximum_fusion.3), channel_id=1, source_target_pairs={{0,2},{2,0},{16,18},{18,16},{32,34},{34,32},{48,50},{50,48},{64,66... | collective-permute-start | bytes 688136 | tf_op jit(solution)/shard_map/ppermute | solution.py:30
  3.2 12.4 %collective-permute-start.1 = (bf16[2,112,1024]{2,1,0:T(8,128)(2,1)S(1)}, bf16[2,112,1024]{2,1,0:T(8,128)(2,1)S(1)}, u32[]{:S(2)}, u32[]{:S(2)}) collective-permute-start(bf16[2,112,1024]{2,1,0:T(8,128)(2,1)S(1)} %pad_maximum_fusion.1.refs_0_), channel_id=1, source_target_pairs={{0,16},{2,114},{16,32},{18,2},{32,48},{34,18},{48,64},{50,34},{64,... | collective-permute-start | bytes 1376264 | tf_op jit(solution)/shard_map/ppermute | solution.py:30
  5.2 6.0 %collective-permute-start.2 = (bf16[2,56,1024]{2,1,0:T(8,128)(2,1)S(1)}, bf16[2,56,1024]{2,1,0:T(8,128)(2,1)S(1)}, u32[]{:S(2)}, u32[]{:S(2)}) collective-permute-start(bf16[2,56,1024]{2,1,0:T(8,128)(2,1)S(1)} %pad_maximum_fusion.3), channel_id=1, source_target_pairs={{0,1},{2,6},{16,17},{18,22},{32,33},{34,38},{48,49},{50,54},{64,65... | collective-permute-start | bytes 688136 | tf_op jit(solution)/shard_map/ppermute | solution.py:30
  5.7 9.7 %collective-permute-start.3 = (bf16[2,56,1024]{2,1,0:T(8,128)(2,1)S(1)}, bf16[2,56,1024]{2,1,0:T(8,128)(2,1)S(1)}, u32[]{:S(2)}, u32[]{:S(2)}) collective-permute-start(bf16[2,56,1024]{2,1,0:T(8,128)(2,1)S(1)} %pad_maximum_fusion.3), channel_id=1, source_target_pairs={{0,129},{2,14},{16,145},{18,30},{32,161},{34,46},{48,177},{50,62},... | collective-permute-start | bytes 688136 | tf_op jit(solution)/shard_map/ppermute | solution.py:30
  7.3 8.1 %collective-permute-start.4 = (bf16[2,56,1024]{2,1,0:T(8,128)(2,1)S(1)}, bf16[2,56,1024]{2,1,0:T(8,128)(2,1)S(1)}, u32[]{:S(2)}, u32[]{:S(2)}) collective-permute-start(bf16[2,56,1024]{2,1,0:T(8,128)(2,1)S(1)} %pad_maximum_fusion.3), channel_id=1, source_target_pairs={{0,128},{2,10},{16,144},{18,26},{32,160},{34,42},{48,176},{50,58},... | collective-permute-start | bytes 688136 | tf_op jit(solution)/shard_map/ppermute | solution.py:30
  15.6 10.4 %collective-permute-start.8 = (bf16[2,112,1024]{2,1,0:T(8,128)(2,1)S(1)}, bf16[2,112,1024]{2,1,0:T(8,128)(2,1)S(1)}, u32[]{:S(2)}, u32[]{:S(2)}) collective-permute-start(bf16[2,112,1024]{2,1,0:T(8,128)(2,1)S(1)} %collective-permute-done.1.refs_1_), channel_id=1, source_target_pairs={{0,16},{2,114},{16,32},{18,2},{32,48},{34,18},{48,64},{50,34},{64,... | collective-permute-start | bytes 1376264 | tf_op jit(solution)/shard_map/ppermute | solution.py:30
  17.5 20.0 %collective-permute-start.5 = (bf16[2,224,1024]{2,1,0:T(8,128)(2,1)S(1)}, bf16[2,224,1024]{2,1,0:T(8,128)(2,1)S(1)}, u32[]{:S(2)}, u32[]{:S(2)}) collective-permute-start(bf16[2,224,1024]{2,1,0:T(8,128)(2,1)S(1)} %pad_maximum_fusion.refs_0_), channel_id=1, source_target_pairs={{0,4},{2,3},{16,20},{18,19},{32,36},{34,35},{48,52},{50,51},{64,68... | collective-permute-start | bytes 2752520 | tf_op jit(solution)/shard_map/ppermute | solution.py:30
  19.1 18.4 %collective-permute-start.6 = (bf16[2,224,1024]{2,1,0:T(8,128)(2,1)S(1)}, bf16[2,224,1024]{2,1,0:T(8,128)(2,1)S(1)}, u32[]{:S(2)}, u32[]{:S(2)}) collective-permute-start(bf16[2,224,1024]{2,1,0:T(8,128)(2,1)S(1)} %pad_maximum_fusion.refs_0_), channel_id=1, source_target_pairs={{0,12},{2,131},{16,28},{18,147},{32,44},{34,163},{48,60},{50,179},... | collective-permute-start | bytes 2752520 | tf_op jit(solution)/shard_map/ppermute | solution.py:30
  20.7 22.8 %collective-permute-start.7 = (bf16[2,224,1024]{2,1,0:T(8,128)(2,1)S(1)}, bf16[2,224,1024]{2,1,0:T(8,128)(2,1)S(1)}, u32[]{:S(2)}, u32[]{:S(2)}) collective-permute-start(bf16[2,224,1024]{2,1,0:T(8,128)(2,1)S(1)} %pad_maximum_fusion.refs_0_), channel_id=1, source_target_pairs={{0,8},{2,130},{16,24},{18,146},{32,40},{34,162},{48,56},{50,178},{... | collective-permute-start | bytes 2752520 | tf_op jit(solution)/shard_map/ppermute | solution.py:30
  26.0 9.7 %collective-permute-start.9 = (bf16[2,112,1024]{2,1,0:T(8,128)(2,1)S(1)}, bf16[2,112,1024]{2,1,0:T(8,128)(2,1)S(1)}, u32[]{:S(2)}, u32[]{:S(2)}) collective-permute-start(bf16[2,112,1024]{2,1,0:T(8,128)(2,1)S(1)} %collective-permute-done.8.refs_2_), channel_id=1, source_target_pairs={{0,16},{2,114},{16,32},{18,2},{32,48},{34,18},{48,64},{50,34},{64,... | collective-permute-start | bytes 1376264 | tf_op jit(solution)/shard_map/ppermute | solution.py:30
  35.8 7.7 %collective-permute-start.13 = (bf16[2,56,1024]{2,1,0:T(8,128)(2,1)S(1)}, bf16[2,56,1024]{2,1,0:T(8,128)(2,1)S(1)}, u32[]{:S(2)}, u32[]{:S(2)}) collective-permute-start(bf16[2,56,1024]{2,1,0:T(8,128)(2,1)S(1)} %slice.20), channel_id=1, source_target_pairs={{0,16},{2,114},{16,32},{18,2},{32,48},{34,18},{48,64},{50,34},{64,... | collective-permute-start | bytes 688136 | tf_op jit(solution)/shard_map/ppermute | solution.py:30
  35.8 9.4 %collective-permute-start.10 = (bf16[2,112,1024]{2,1,0:T(8,128)(2,1)S(1)}, bf16[2,112,1024]{2,1,0:T(8,128)(2,1)S(1)}, u32[]{:S(2)}, u32[]{:S(2)}) collective-permute-start(bf16[2,112,1024]{2,1,0:T(8,128)(2,1)S(1)} %collective-permute-done.1.refs_1_), channel_id=1, source_target_pairs={{0,2},{2,0},{16,18},{18,16},{32,34},{34,32},{48,50},{50,48},{64,66... | collective-permute-start | bytes 1376264 | tf_op jit(solution)/shard_map/ppermute | solution.py:30
  37.5 7.8 %collective-permute-start.11 = (bf16[2,112,1024]{2,1,0:T(8,128)(2,1)S(1)}, bf16[2,112,1024]{2,1,0:T(8,128)(2,1)S(1)}, u32[]{:S(2)}, u32[]{:S(2)}) collective-permute-start(bf16[2,112,1024]{2,1,0:T(8,128)(2,1)S(1)} %collective-permute-done.8.refs_2_), channel_id=1, source_target_pairs={{0,2},{2,0},{16,18},{18,16},{32,34},{34,32},{48,50},{50,48},{64,66... | collective-permute-start | bytes 1376264 | tf_op jit(solution)/shard_map/ppermute | solution.py:30
  37.5 7.8 %collective-permute-start.12 = (bf16[2,112,1024]{2,1,0:T(8,128)(2,1)S(1)}, bf16[2,112,1024]{2,1,0:T(8,128)(2,1)S(1)}, u32[]{:S(2)}, u32[]{:S(2)}) collective-permute-start(bf16[2,112,1024]{2,1,0:T(8,128)(2,1)S(1)} %collective-permute-done.9.refs_3_), channel_id=1, source_target_pairs={{0,2},{2,0},{16,18},{18,16},{32,34},{34,32},{48,50},{50,48},{64,66... | collective-permute-start | bytes 1376264 | tf_op jit(solution)/shard_map/ppermute | solution.py:30
  43.5 1.8 %collective-permute-start.14 = (bf16[2,56,1024]{2,1,0:T(8,128)(2,1)S(1)}, bf16[2,56,1024]{2,1,0:T(8,128)(2,1)S(1)}, u32[]{:S(2)}, u32[]{:S(2)}) collective-permute-start(bf16[2,56,1024]{2,1,0:T(8,128)(2,1)S(1)} %collective-permute-done.13), channel_id=1, source_target_pairs={{0,2},{2,0},{16,18},{18,16},{32,34},{34,32},{48,50},{50,48},{64,66... | collective-permute-start | bytes 688136 | tf_op jit(solution)/shard_map/ppermute | solution.py:30
  51.5 1.2 %collective-permute-start.15 = (f32[16,128]{1,0:T(8,128)S(1)}, f32[16,128]{1,0:T(8,128)S(1)}, u32[]{:S(2)}, u32[]{:S(2)}) collective-permute-start(f32[16,128]{1,0:T(8,128)S(1)} %gram.1), channel_id=1, source_target_pairs={{0,2},{2,0},{16,18},{18,16},{32,34},{34,32},{48,50},{50,48},{64,66... | collective-permute-start | bytes 24584 | tf_op jit(solution)/shard_map/ppermute | solution.py:30
  52.7 3.7 %collective-permute-start.16 = (f32[16,128]{1,0:T(8,128)S(1)}, f32[16,128]{1,0:T(8,128)S(1)}, u32[]{:S(2)}, u32[]{:S(2)}) collective-permute-start(f32[16,128]{1,0:T(8,128)S(1)} %add.24), channel_id=1, source_target_pairs={{0,16},{2,18},{16,0},{18,2},{32,48},{34,50},{48,32},{50,34},{64,80... | collective-permute-start | bytes 24584 | tf_op jit(solution)/shard_map/ppermute | solution.py:30
  56.4 9.0 %collective-permute-start.17 = (f32[16,128]{1,0:T(8,128)S(1)}, f32[16,128]{1,0:T(8,128)S(1)}, u32[]{:S(2)}, u32[]{:S(2)}) collective-permute-start(f32[16,128]{1,0:T(8,128)S(1)} %add.25), channel_id=1, source_target_pairs={{0,64},{2,66},{16,80},{18,82},{32,96},{34,98},{48,112},{50,114},{6... | collective-permute-start | bytes 24584 | tf_op jit(solution)/shard_map/ppermute | solution.py:30
  61.2 5.8 %collective-permute-start.18 = (f32[16,128]{1,0:T(8,128)S(1)}, f32[16,128]{1,0:T(8,128)S(1)}, u32[]{:S(2)}, u32[]{:S(2)}) collective-permute-start(f32[16,128]{1,0:T(8,128)S(1)} %add.25), channel_id=1, source_target_pairs={{0,32},{2,34},{16,48},{18,50},{32,64},{34,66},{48,80},{50,82},{64,... | collective-permute-start | bytes 24584 | tf_op jit(solution)/shard_map/ppermute | solution.py:30
  61.6 5.4 %collective-permute-start.19 = (f32[16,128]{1,0:T(8,128)S(1)}, f32[16,128]{1,0:T(8,128)S(1)}, u32[]{:S(2)}, u32[]{:S(2)}) collective-permute-start(f32[16,128]{1,0:T(8,128)S(1)} %add.25), channel_id=1, source_target_pairs={{0,96},{2,98},{16,112},{18,114},{32,0},{34,2},{48,16},{50,18},{64,... | collective-permute-start | bytes 24584 | tf_op jit(solution)/shard_map/ppermute | solution.py:30
  67.1 5.2 %collective-permute-start.20 = (f32[8,128]{1,0:T(8,128)S(1)}, f32[8,128]{1,0:T(8,128)S(1)}, u32[]{:S(2)}, u32[]{:S(2)}) collective-permute-start(f32[8,128]{1,0:T(8,128)S(1)} %stack.37), channel_id=1, source_target_pairs={{0,128},{2,130},{16,144},{18,146},{32,160},{34,162},{48,176},{50,1... | collective-permute-start | bytes 12296 | tf_op jit(solution)/shard_map/ppermute | solution.py:30
  69.0 3.6 %collective-permute-start.21 = (f32[8,128]{1,0:T(8,128)S(1)}, f32[8,128]{1,0:T(8,128)S(1)}, u32[]{:S(2)}, u32[]{:S(2)}) collective-permute-start(f32[8,128]{1,0:T(8,128)S(1)} %stack.37), channel_id=1, source_target_pairs={{0,1},{2,3},{16,17},{18,19},{32,33},{34,35},{48,49},{50,51},{64,65... | collective-permute-start | bytes 12296 | tf_op jit(solution)/shard_map/ppermute | solution.py:30
  70.0 4.8 %collective-permute-start.22 = (f32[8,128]{1,0:T(8,128)S(1)}, f32[8,128]{1,0:T(8,128)S(1)}, u32[]{:S(2)}, u32[]{:S(2)}) collective-permute-start(f32[8,128]{1,0:T(8,128)S(1)} %stack.37), channel_id=1, source_target_pairs={{0,129},{2,131},{16,145},{18,147},{32,161},{34,163},{48,177},{50,1... | collective-permute-start | bytes 12296 | tf_op jit(solution)/shard_map/ppermute | solution.py:30
  74.9 5.4 %collective-permute-start.23 = (f32[8,128]{1,0:T(8,128)S(1)}, f32[8,128]{1,0:T(8,128)S(1)}, u32[]{:S(2)}, u32[]{:S(2)}) collective-permute-start(f32[8,128]{1,0:T(8,128)S(1)} %add_add_fusion.1.sums_ref), channel_id=1, source_target_pairs={{0,4},{2,6},{16,20},{18,22},{32,36},{34,38},{48,52},{50,54},{64,68... | collective-permute-start | bytes 12296 | tf_op jit(solution)/shard_map/ppermute | solution.py:30
  76.4 3.9 %collective-permute-start.24 = (f32[8,128]{1,0:T(8,128)S(1)}, f32[8,128]{1,0:T(8,128)S(1)}, u32[]{:S(2)}, u32[]{:S(2)}) collective-permute-start(f32[8,128]{1,0:T(8,128)S(1)} %add_add_fusion.1.sums_ref), channel_id=1, source_target_pairs={{0,12},{2,14},{16,28},{18,30},{32,44},{34,46},{48,60},{50,62},{64,... | collective-permute-start | bytes 12296 | tf_op jit(solution)/shard_map/ppermute | solution.py:30
  78.1 5.1 %collective-permute-start.25 = (f32[8,128]{1,0:T(8,128)S(1)}, f32[8,128]{1,0:T(8,128)S(1)}, u32[]{:S(2)}, u32[]{:S(2)}) collective-permute-start(f32[8,128]{1,0:T(8,128)S(1)} %add_add_fusion.1.sums_ref), channel_id=1, source_target_pairs={{0,8},{2,10},{16,24},{18,26},{32,40},{34,42},{48,56},{50,58},{64,7... | collective-permute-start | bytes 12296 | tf_op jit(solution)/shard_map/ppermute | solution.py:30

commit v7 on v6

--- a/solution.py
+++ b/solution.py
@@ -179,8 +179,9 @@
 
 
 def line_sum(array):
-    array = array + swap(array)
-    array = array + move(array, lambda x, y, z, core: (x, y, z ^ 1, core))
+    other = swap(array)
+    beside = [move(array, lambda x, y, z, core: (x, y, z ^ 1, core ^ flip)) for flip in range(2)]
+    array = (array + other) + (beside[0] + beside[1])
     parts = [move(array, lambda x, y, z, core: (x, y, z + step, core)) for step in (2, -2, 4)]
     return ring_sum(array, parts)
 
@@ -198,7 +199,8 @@
 
 def finish_body(total, count, part_ref, sums_ref, *refs):
     parts, (profiles_ref, alignment_ref) = refs[:3], refs[3:]
-    lanes = ring_sum(sums_ref[...], [part[...] for part in parts])
+    far, ahead, behind = (part[...] for part in parts)
+    lanes = ring_sum(sums_ref[...], [ahead, behind, far])
     sums = jnp.sum(lanes, axis=1, keepdims=True)
     sum_one, sum_two, f_cross, _, c_cross, c_one, c_two = (sums[at : at + 1, :] for at in range(7))
     left = lax.broadcasted_iota(jnp.int32, (1, 128), 1) < 64
@@ -247,7 +249,8 @@
     terms = [r_one, r_two, part[7:8], part[15:16], r_one * r_two, r_one * r_one, r_two * r_two]
     sums = jnp.stack([jnp.sum(term, axis=0) for term in terms] + [jnp.zeros((128,), jnp.float32)])
     sums = ring_sum(sums, ring_parts(sums, "x"))
-    profiles, alignment = finish(part, sums, ring_parts(sums, "y"), count * lax.axis_size(AXES), count)
+    ahead, behind, far = ring_parts(sums, "y")
+    profiles, alignment = finish(part, sums, (far, ahead, behind), count * lax.axis_size(AXES), count)
     return (profiles, alignment.reshape(()))
 
 

time: 84 us -> 83.4 us (level)
  waiting for transfers between devices: 33.5 us -> 31.5 us
  starting transfers between devices: 40.3 us -> 41.5 us
    ppermute x26 -> x27, waiting for transfers between devices: 33.5 us -> 31.5 us  [move(): return lax.ppermute(array, AXES, pairs)]
    ppermute x26 -> x27, starting transfers between devices: 40.3 us -> 41.5 us  [move(): return lax.ppermute(array, AXES, pairs)]
  transfers between devices with their start and end apart: 26 -> 27, of which waited for: 14 -> 14; matrix products, arithmetic and copies ran while one was open for 0% -> 0% of each run, Pallas kernels for 2% -> 2%
where the time goes in v7:
time: 83.4 us; the launch traced here: 83.1 us
  starting transfers between devices  41.5 us (50%)
  waiting for transfers between devices  31.5 us (38%)
  Pallas kernels  8.22 us (10%)
  other arithmetic  1.14 us (1%)
    ppermute x27, starting transfers between devices, move(): return lax.ppermute(array, AXES, pairs)  41.5 us
    ppermute x27, waiting for transfers between devices, move(): return lax.ppermute(array, AXES, pairs)  31.5 us
    pallas_call x1, Pallas kernels, gram(): pl.pallas_call(gram_body, out_shape=jax.ShapeDtypeStruct((16, 128), jnp.f...  6.17 us
  transfers between devices with their start and end apart: 27, of which 14 were waited for; matrix products, arithmetic and copies ran while one was open for 0% of the time, Pallas kernels for 2%

profile of v7, /device:TPU:6, one launch (start us, length us, event | category | flops | bytes accessed | tf_op | source)
XLA Modules:
  0.0 83.1 jit_solution(2724167403651381479)
XLA Ops:
  0.6 1.0 %pad_maximum_fusion.3 = bf16[2,56,1024]{2,1,0:T(8,128)(2,1)S(1)} fusion(bf16[1,56,1024]{2,1,0:T(8,128)(2,1)} %bitcast.8, bf16[1,56,1024]{2,1,0:T(8,128)(2,1)} %bitcast.9), kind=kLoop, calls=%fused_computation.3 | loop fusion | flops 114688 | bytes 458752 | tf_op jit(solution)/shard_map/stack | solution.py:234
  1.7 1.5 %collective-permute-done = bf16[2,56,1024]{2,1,0:T(8,128)(2,1)S(1)} collective-permute-done((bf16[2,56,1024]{2,1,0:T(8,128)(2,1)S(1)}, bf16[2,56,1024]{2,1,0:T(8,128)(2,1)S(1)}, u32[]{:S(2)}, u32[]{:S(2)}) %collective-permute-start) | collective-permute-done | bytes 229408 | tf_op jit(solution)/shard_map/ppermute | solution.py:30
  3.2 2.0 %collective-permute-start.1 = (bf16[2,112,1024]{2,1,0:T(8,128)(2,1)S(1)}, bf16[2,112,1024]{2,1,0:T(8,128)(2,1)S(1)}, u32[]{:S(2)}, u32[]{:S(2)}) collective-permute-start(bf16[2,112,1024]{2,1,0:T(8,128)(2,1)S(1)} %pad_maximum_fusion.1.refs_0_), channel_id=1, source_target_pairs={{0,16},{2,114},{16,32},{18,2},{32,48},{34,18},{48,64},{50,34},{64,... | collective-permute-start | bytes 1376264 | tf_op jit(solution)/shard_map/ppermute | solution.py:30
  5.2 0.5 collective-permute-start.2
  5.7 1.5 %collective-permute-start.3 = (bf16[2,56,1024]{2,1,0:T(8,128)(2,1)S(1)}, bf16[2,56,1024]{2,1,0:T(8,128)(2,1)S(1)}, u32[]{:S(2)}, u32[]{:S(2)}) collective-permute-start(bf16[2,56,1024]{2,1,0:T(8,128)(2,1)S(1)} %pad_maximum_fusion.3), channel_id=1, source_target_pairs={{0,129},{2,14},{16,145},{18,30},{32,161},{34,46},{48,177},{50,62},... | collective-permute-start | bytes 688136 | tf_op jit(solution)/shard_map/ppermute | solution.py:30
  7.3 1.4 %collective-permute-start.4 = (bf16[2,56,1024]{2,1,0:T(8,128)(2,1)S(1)}, bf16[2,56,1024]{2,1,0:T(8,128)(2,1)S(1)}, u32[]{:S(2)}, u32[]{:S(2)}) collective-permute-start(bf16[2,56,1024]{2,1,0:T(8,128)(2,1)S(1)} %pad_maximum_fusion.3), channel_id=1, source_target_pairs={{0,128},{2,10},{16,144},{18,26},{32,160},{34,42},{48,176},{50,58},... | collective-permute-start | bytes 688136 | tf_op jit(solution)/shard_map/ppermute | solution.py:30
  8.7 2.6 %collective-permute-done.2 = bf16[2,56,1024]{2,1,0:T(8,128)(2,1)S(1)} collective-permute-done((bf16[2,56,1024]{2,1,0:T(8,128)(2,1)S(1)}, bf16[2,56,1024]{2,1,0:T(8,128)(2,1)S(1)}, u32[]{:S(2)}, u32[]{:S(2)}) %collective-permute-start.2) | collective-permute-done | bytes 229408 | tf_op jit(solution)/shard_map/ppermute | solution.py:30
  11.3 4.1 %collective-permute-done.3 = bf16[2,56,1024]{2,1,0:T(8,128)(2,1)S(1)} collective-permute-done((bf16[2,56,1024]{2,1,0:T(8,128)(2,1)S(1)}, bf16[2,56,1024]{2,1,0:T(8,128)(2,1)S(1)}, u32[]{:S(2)}, u32[]{:S(2)}) %collective-permute-start.3) | collective-permute-done | bytes 229408 | tf_op jit(solution)/shard_map/ppermute | solution.py:30
  15.6 1.9 %collective-permute-start.8 = (bf16[2,112,1024]{2,1,0:T(8,128)(2,1)S(1)}, bf16[2,112,1024]{2,1,0:T(8,128)(2,1)S(1)}, u32[]{:S(2)}, u32[]{:S(2)}) collective-permute-start(bf16[2,112,1024]{2,1,0:T(8,128)(2,1)S(1)} %collective-permute-done.1.refs_1_), channel_id=1, source_target_pairs={{0,16},{2,114},{16,32},{18,2},{32,48},{34,18},{48,64},{50,34},{64,... | collective-permute-start | bytes 1376264 | tf_op jit(solution)/shard_map/ppermute | solution.py:30
  17.5 1.6 %collective-permute-start.5 = (bf16[2,224,1024]{2,1,0:T(8,128)(2,1)S(1)}, bf16[2,224,1024]{2,1,0:T(8,128)(2,1)S(1)}, u32[]{:S(2)}, u32[]{:S(2)}) collective-permute-start(bf16[2,224,1024]{2,1,0:T(8,128)(2,1)S(1)} %pad_maximum_fusion.refs_0_), channel_id=1, source_target_pairs={{0,4},{2,3},{16,20},{18,19},{32,36},{34,35},{48,52},{50,51},{64,68... | collective-permute-start | bytes 2752520 | tf_op jit(solution)/shard_map/ppermute | solution.py:30
  19.1 1.7 %collective-permute-start.6 = (bf16[2,224,1024]{2,1,0:T(8,128)(2,1)S(1)}, bf16[2,224,1024]{2,1,0:T(8,128)(2,1)S(1)}, u32[]{:S(2)}, u32[]{:S(2)}) collective-permute-start(bf16[2,224,1024]{2,1,0:T(8,128)(2,1)S(1)} %pad_maximum_fusion.refs_0_), channel_id=1, source_target_pairs={{0,12},{2,131},{16,28},{18,147},{32,44},{34,163},{48,60},{50,179},... | collective-permute-start | bytes 2752520 | tf_op jit(solution)/shard_map/ppermute | solution.py:30
  20.7 2.0 %collective-permute-start.7 = (bf16[2,224,1024]{2,1,0:T(8,128)(2,1)S(1)}, bf16[2,224,1024]{2,1,0:T(8,128)(2,1)S(1)}, u32[]{:S(2)}, u32[]{:S(2)}) collective-permute-start(bf16[2,224,1024]{2,1,0:T(8,128)(2,1)S(1)} %pad_maximum_fusion.refs_0_), channel_id=1, source_target_pairs={{0,8},{2,130},{16,24},{18,146},{32,40},{34,162},{48,56},{50,178},{... | collective-permute-start | bytes 2752520 | tf_op jit(solution)/shard_map/ppermute | solution.py:30
  22.7 3.3 %collective-permute-done.8.refs_2_ = bf16[2,112,1024]{2,1,0:T(8,128)(2,1)S(1)} collective-permute-done((bf16[2,112,1024]{2,1,0:T(8,128)(2,1)S(1)}, bf16[2,112,1024]{2,1,0:T(8,128)(2,1)S(1)}, u32[]{:S(2)}, u32[]{:S(2)}) %collective-permute-start.8) | collective-permute-done | bytes 458784 | tf_op jit(solution)/shard_map/ppermute | solution.py:30
  26.1 9.7 %collective-permute-done.9.refs_3_ = bf16[2,112,1024]{2,1,0:T(8,128)(2,1)S(1)} collective-permute-done((bf16[2,112,1024]{2,1,0:T(8,128)(2,1)S(1)}, bf16[2,112,1024]{2,1,0:T(8,128)(2,1)S(1)}, u32[]{:S(2)}, u32[]{:S(2)}) %collective-permute-start.9) | collective-permute-done | bytes 458784 | tf_op jit(solution)/shard_map/ppermute | solution.py:30
  35.8 1.6 %collective-permute-start.10 = (bf16[2,112,1024]{2,1,0:T(8,128)(2,1)S(1)}, bf16[2,112,1024]{2,1,0:T(8,128)(2,1)S(1)}, u32[]{:S(2)}, u32[]{:S(2)}) collective-permute-start(bf16[2,112,1024]{2,1,0:T(8,128)(2,1)S(1)} %collective-permute-done.1.refs_1_), channel_id=1, source_target_pairs={{0,2},{2,0},{16,18},{18,16},{32,34},{34,32},{48,50},{50,48},{64,66... | collective-permute-start | bytes 1376264 | tf_op jit(solution)/shard_map/ppermute | solution.py:30
  37.5 6.0 %collective-permute-start.12 = (bf16[2,112,1024]{2,1,0:T(8,128)(2,1)S(1)}, bf16[2,112,1024]{2,1,0:T(8,128)(2,1)S(1)}, u32[]{:S(2)}, u32[]{:S(2)}) collective-permute-start(bf16[2,112,1024]{2,1,0:T(8,128)(2,1)S(1)} %collective-permute-done.9.refs_3_), channel_id=1, source_target_pairs={{0,2},{2,0},{16,18},{18,16},{32,34},{34,32},{48,50},{50,48},{64,66... | collective-permute-start | bytes 1376264 | tf_op jit(solution)/shard_map/ppermute | solution.py:30
  43.5 1.4 %plane_rows.1 = (bf16[2,896,1024]{2,1,0:T(8,128)(2,1)S(1)}, f32[2,896,128]{2,1,0:T(8,128)S(1)}) custom-call(s32[2]{0:T(128)S(1)} %copy-done, bf16[2,224,1024]{2,1,0:T(8,128)(2,1)S(1)} %pad_maximum_fusion.refs_0_, bf16[2,224,1024]{2,1,0:T(8,128)(2,1)S(1)} %collective-permute-done.5.refs_1_, bf16[2,224,1024]{2,1,0:T(8,128)(2,1)S(1)} %collective-permute-done.6.refs_2_, ...), custom_call_target="tpu_custom_call" | custom-call | flops 3670016 | bytes 7340032 | tf_op jit(solution)/shard_map/plane_rows/pallas_call | solution.py:83
  45.3 6.2 %gram.1 = f32[16,128]{1,0:T(8,128)S(1)} custom-call(s32[2]{0:T(128)S(1)} %copy-done, bf16[2,896,1024]{2,1,0:T(8,128)(2,1)S(1)} %get-tuple-element.9.w_ref, f32[2,896,128]{2,1,0:T(8,128)S(1)} %get-tuple-element.10.norm_ref, bf16[2,112,1024]{2,1,0:T(8,128)(2,1)S(1)} %pad_maximum_fusion.1.refs_0_, bf16[2,112,1024]{2,1,0:T(8,128)(2,1)S(1)} %collective-permute-done.1.refs_1_, ...), custom_call_target="tpu_custom_call" | custom-call | flops 3288334336 | bytes 7340032 | tf_op jit(solution)/shard_map/gram/pallas_call | solution.py:159
  51.9 1.0 %collective-permute-start.16 = (f32[16,128]{1,0:T(8,128)S(1)}, f32[16,128]{1,0:T(8,128)S(1)}, u32[]{:S(2)}, u32[]{:S(2)}) collective-permute-start(f32[16,128]{1,0:T(8,128)S(1)} %gram.1), channel_id=1, source_target_pairs={{0,16},{2,18},{16,0},{18,2},{32,48},{34,50},{48,32},{50,34},{64,80... | collective-permute-start | bytes 24584 | tf_op jit(solution)/shard_map/ppermute | solution.py:30
  53.4 2.2 %collective-permute-done.16 = f32[16,128]{1,0:T(8,128)S(1)} collective-permute-done((f32[16,128]{1,0:T(8,128)S(1)}, f32[16,128]{1,0:T(8,128)S(1)}, u32[]{:S(2)}, u32[]{:S(2)}) %collective-permute-start.16) | collective-permute-done | bytes 8224 | tf_op jit(solution)/shard_map/ppermute | solution.py:30
  56.0 4.6 %collective-permute-start.18 = (f32[16,128]{1,0:T(8,128)S(1)}, f32[16,128]{1,0:T(8,128)S(1)}, u32[]{:S(2)}, u32[]{:S(2)}) collective-permute-start(f32[16,128]{1,0:T(8,128)S(1)} %add_add_fusion.1), channel_id=1, source_target_pairs={{0,64},{2,66},{16,80},{18,82},{32,96},{34,98},{48,112},{50,114},{6... | collective-permute-start | bytes 24584 | tf_op jit(solution)/shard_map/ppermute | solution.py:30
  60.6 4.1 %collective-permute-start.20 = (f32[16,128]{1,0:T(8,128)S(1)}, f32[16,128]{1,0:T(8,128)S(1)}, u32[]{:S(2)}, u32[]{:S(2)}) collective-permute-start(f32[16,128]{1,0:T(8,128)S(1)} %add_add_fusion.1), channel_id=1, source_target_pairs={{0,96},{2,98},{16,112},{18,114},{32,0},{34,2},{48,16},{50,18},{64,... | collective-permute-start | bytes 24584 | tf_op jit(solution)/shard_map/ppermute | solution.py:30
  64.7 1.6 %collective-permute-done.19 = f32[16,128]{1,0:T(8,128)S(1)} collective-permute-done((f32[16,128]{1,0:T(8,128)S(1)}, f32[16,128]{1,0:T(8,128)S(1)}, u32[]{:S(2)}, u32[]{:S(2)}) %collective-permute-start.19) | collective-permute-done | bytes 8224 | tf_op jit(solution)/shard_map/ppermute | solution.py:30
  66.4 1.9 %collective-permute-start.21 = (f32[8,128]{1,0:T(8,128)S(1)}, f32[8,128]{1,0:T(8,128)S(1)}, u32[]{:S(2)}, u32[]{:S(2)}) collective-permute-start(f32[8,128]{1,0:T(8,128)S(1)} %stack.37), channel_id=1, source_target_pairs={{0,128},{2,130},{16,144},{18,146},{32,160},{34,162},{48,176},{50,1... | collective-permute-start | bytes 12296 | tf_op jit(solution)/shard_map/ppermute | solution.py:30
  68.3 1.1 %collective-permute-start.22 = (f32[8,128]{1,0:T(8,128)S(1)}, f32[8,128]{1,0:T(8,128)S(1)}, u32[]{:S(2)}, u32[]{:S(2)}) collective-permute-start(f32[8,128]{1,0:T(8,128)S(1)} %stack.37), channel_id=1, source_target_pairs={{0,1},{2,3},{16,17},{18,19},{32,33},{34,35},{48,49},{50,51},{64,65... | collective-permute-start | bytes 12296 | tf_op jit(solution)/shard_map/ppermute | solution.py:30
  69.4 1.0 %collective-permute-start.23 = (f32[8,128]{1,0:T(8,128)S(1)}, f32[8,128]{1,0:T(8,128)S(1)}, u32[]{:S(2)}, u32[]{:S(2)}) collective-permute-start(f32[8,128]{1,0:T(8,128)S(1)} %stack.37), channel_id=1, source_target_pairs={{0,129},{2,131},{16,145},{18,147},{32,161},{34,163},{48,177},{50,1... | collective-permute-start | bytes 12296 | tf_op jit(solution)/shard_map/ppermute | solution.py:30
  70.4 1.3 %collective-permute-done.21 = f32[8,128]{1,0:T(8,128)S(1)} collective-permute-done((f32[8,128]{1,0:T(8,128)S(1)}, f32[8,128]{1,0:T(8,128)S(1)}, u32[]{:S(2)}, u32[]{:S(2)}) %collective-permute-start.21) | collective-permute-done | bytes 4128 | tf_op jit(solution)/shard_map/ppermute | solution.py:30
  71.9 2.3 %collective-permute-done.23 = f32[8,128]{1,0:T(8,128)S(1)} collective-permute-done((f32[8,128]{1,0:T(8,128)S(1)}, f32[8,128]{1,0:T(8,128)S(1)}, u32[]{:S(2)}, u32[]{:S(2)}) %collective-permute-start.23) | collective-permute-done | bytes 4128 | tf_op jit(solution)/shard_map/ppermute | solution.py:30
  74.2 3.4 %collective-permute-start.24 = (f32[8,128]{1,0:T(8,128)S(1)}, f32[8,128]{1,0:T(8,128)S(1)}, u32[]{:S(2)}, u32[]{:S(2)}) collective-permute-start(f32[8,128]{1,0:T(8,128)S(1)} %add_add_fusion.2.sums_ref), channel_id=1, source_target_pairs={{0,8},{2,10},{16,24},{18,26},{32,40},{34,42},{48,56},{50,58},{64,7... | collective-permute-start | bytes 12296 | tf_op jit(solution)/shard_map/ppermute | solution.py:30
  78.1 2.8 %collective-permute-start.26 = (f32[8,128]{1,0:T(8,128)S(1)}, f32[8,128]{1,0:T(8,128)S(1)}, u32[]{:S(2)}, u32[]{:S(2)}) collective-permute-start(f32[8,128]{1,0:T(8,128)S(1)} %add_add_fusion.2.sums_ref), channel_id=1, source_target_pairs={{0,12},{2,14},{16,28},{18,30},{32,44},{34,46},{48,60},{50,62},{64,... | collective-permute-start | bytes 12296 | tf_op jit(solution)/shard_map/ppermute | solution.py:30
  80.9 1.6 %collective-permute-done.25.refs_1_ = f32[8,128]{1,0:T(8,128)S(1)} collective-permute-done((f32[8,128]{1,0:T(8,128)S(1)}, f32[8,128]{1,0:T(8,128)S(1)}, u32[]{:S(2)}, u32[]{:S(2)}) %collective-permute-start.25) | collective-permute-done | bytes 4128 | tf_op jit(solution)/shard_map/ppermute | solution.py:30
  82.4 0.7 finish.1
  (39 shorter events, 3.1 us)
Async XLA Ops:
  0.6 42.9 %copy-start = (s32[2]{0:T(128)S(1)}, s32[2]{0:T(128)}, u32[]{:S(2)}) copy-start(s32[2]{0:T(128)} %spread_ref.3) | copy-start | bytes 28
  1.6 1.6 %collective-permute-start = (bf16[2,56,1024]{2,1,0:T(8,128)(2,1)S(1)}, bf16[2,56,1024]{2,1,0:T(8,128)(2,1)S(1)}, u32[]{:S(2)}, u32[]{:S(2)}) collective-permute-start(bf16[2,56,1024]{2,1,0:T(8,128)(2,1)S(1)} %pad_maximum_fusion.3), channel_id=1, source_target_pairs={{0,2},{2,0},{16,18},{18,16},{32,34},{34,32},{48,50},{50,48},{64,66... | collective-permute-start | bytes 688136 | tf_op jit(solution)/shard_map/ppermute | solution.py:30
  3.2 12.4 %collective-permute-start.1 = (bf16[2,112,1024]{2,1,0:T(8,128)(2,1)S(1)}, bf16[2,112,1024]{2,1,0:T(8,128)(2,1)S(1)}, u32[]{:S(2)}, u32[]{:S(2)}) collective-permute-start(bf16[2,112,1024]{2,1,0:T(8,128)(2,1)S(1)} %pad_maximum_fusion.1.refs_0_), channel_id=1, source_target_pairs={{0,16},{2,114},{16,32},{18,2},{32,48},{34,18},{48,64},{50,34},{64,... | collective-permute-start | bytes 1376264 | tf_op jit(solution)/shard_map/ppermute | solution.py:30
  5.2 6.0 %collective-permute-start.2 = (bf16[2,56,1024]{2,1,0:T(8,128)(2,1)S(1)}, bf16[2,56,1024]{2,1,0:T(8,128)(2,1)S(1)}, u32[]{:S(2)}, u32[]{:S(2)}) collective-permute-start(bf16[2,56,1024]{2,1,0:T(8,128)(2,1)S(1)} %pad_maximum_fusion.3), channel_id=1, source_target_pairs={{0,1},{2,6},{16,17},{18,22},{32,33},{34,38},{48,49},{50,54},{64,65... | collective-permute-start | bytes 688136 | tf_op jit(solution)/shard_map/ppermute | solution.py:30
  5.7 9.7 %collective-permute-start.3 = (bf16[2,56,1024]{2,1,0:T(8,128)(2,1)S(1)}, bf16[2,56,1024]{2,1,0:T(8,128)(2,1)S(1)}, u32[]{:S(2)}, u32[]{:S(2)}) collective-permute-start(bf16[2,56,1024]{2,1,0:T(8,128)(2,1)S(1)} %pad_maximum_fusion.3), channel_id=1, source_target_pairs={{0,129},{2,14},{16,145},{18,30},{32,161},{34,46},{48,177},{50,62},... | collective-permute-start | bytes 688136 | tf_op jit(solution)/shard_map/ppermute | solution.py:30
  7.3 8.1 %collective-permute-start.4 = (bf16[2,56,1024]{2,1,0:T(8,128)(2,1)S(1)}, bf16[2,56,1024]{2,1,0:T(8,128)(2,1)S(1)}, u32[]{:S(2)}, u32[]{:S(2)}) collective-permute-start(bf16[2,56,1024]{2,1,0:T(8,128)(2,1)S(1)} %pad_maximum_fusion.3), channel_id=1, source_target_pairs={{0,128},{2,10},{16,144},{18,26},{32,160},{34,42},{48,176},{50,58},... | collective-permute-start | bytes 688136 | tf_op jit(solution)/shard_map/ppermute | solution.py:30
  15.6 10.4 %collective-permute-start.8 = (bf16[2,112,1024]{2,1,0:T(8,128)(2,1)S(1)}, bf16[2,112,1024]{2,1,0:T(8,128)(2,1)S(1)}, u32[]{:S(2)}, u32[]{:S(2)}) collective-permute-start(bf16[2,112,1024]{2,1,0:T(8,128)(2,1)S(1)} %collective-permute-done.1.refs_1_), channel_id=1, source_target_pairs={{0,16},{2,114},{16,32},{18,2},{32,48},{34,18},{48,64},{50,34},{64,... | collective-permute-start | bytes 1376264 | tf_op jit(solution)/shard_map/ppermute | solution.py:30
  17.5 20.0 %collective-permute-start.5 = (bf16[2,224,1024]{2,1,0:T(8,128)(2,1)S(1)}, bf16[2,224,1024]{2,1,0:T(8,128)(2,1)S(1)}, u32[]{:S(2)}, u32[]{:S(2)}) collective-permute-start(bf16[2,224,1024]{2,1,0:T(8,128)(2,1)S(1)} %pad_maximum_fusion.refs_0_), channel_id=1, source_target_pairs={{0,4},{2,3},{16,20},{18,19},{32,36},{34,35},{48,52},{50,51},{64,68... | collective-permute-start | bytes 2752520 | tf_op jit(solution)/shard_map/ppermute | solution.py:30
  19.1 18.4 %collective-permute-start.6 = (bf16[2,224,1024]{2,1,0:T(8,128)(2,1)S(1)}, bf16[2,224,1024]{2,1,0:T(8,128)(2,1)S(1)}, u32[]{:S(2)}, u32[]{:S(2)}) collective-permute-start(bf16[2,224,1024]{2,1,0:T(8,128)(2,1)S(1)} %pad_maximum_fusion.refs_0_), channel_id=1, source_target_pairs={{0,12},{2,131},{16,28},{18,147},{32,44},{34,163},{48,60},{50,179},... | collective-permute-start | bytes 2752520 | tf_op jit(solution)/shard_map/ppermute | solution.py:30
  20.7 22.8 %collective-permute-start.7 = (bf16[2,224,1024]{2,1,0:T(8,128)(2,1)S(1)}, bf16[2,224,1024]{2,1,0:T(8,128)(2,1)S(1)}, u32[]{:S(2)}, u32[]{:S(2)}) collective-permute-start(bf16[2,224,1024]{2,1,0:T(8,128)(2,1)S(1)} %pad_maximum_fusion.refs_0_), channel_id=1, source_target_pairs={{0,8},{2,130},{16,24},{18,146},{32,40},{34,162},{48,56},{50,178},{... | collective-permute-start | bytes 2752520 | tf_op jit(solution)/shard_map/ppermute | solution.py:30
  26.0 9.7 %collective-permute-start.9 = (bf16[2,112,1024]{2,1,0:T(8,128)(2,1)S(1)}, bf16[2,112,1024]{2,1,0:T(8,128)(2,1)S(1)}, u32[]{:S(2)}, u32[]{:S(2)}) collective-permute-start(bf16[2,112,1024]{2,1,0:T(8,128)(2,1)S(1)} %collective-permute-done.8.refs_2_), channel_id=1, source_target_pairs={{0,16},{2,114},{16,32},{18,2},{32,48},{34,18},{48,64},{50,34},{64,... | collective-permute-start | bytes 1376264 | tf_op jit(solution)/shard_map/ppermute | solution.py:30
  35.8 7.7 %collective-permute-start.13 = (bf16[2,56,1024]{2,1,0:T(8,128)(2,1)S(1)}, bf16[2,56,1024]{2,1,0:T(8,128)(2,1)S(1)}, u32[]{:S(2)}, u32[]{:S(2)}) collective-permute-start(bf16[2,56,1024]{2,1,0:T(8,128)(2,1)S(1)} %slice.20), channel_id=1, source_target_pairs={{0,16},{2,114},{16,32},{18,2},{32,48},{34,18},{48,64},{50,34},{64,... | collective-permute-start | bytes 688136 | tf_op jit(solution)/shard_map/ppermute | solution.py:30
  35.8 9.4 %collective-permute-start.10 = (bf16[2,112,1024]{2,1,0:T(8,128)(2,1)S(1)}, bf16[2,112,1024]{2,1,0:T(8,128)(2,1)S(1)}, u32[]{:S(2)}, u32[]{:S(2)}) collective-permute-start(bf16[2,112,1024]{2,1,0:T(8,128)(2,1)S(1)} %collective-permute-done.1.refs_1_), channel_id=1, source_target_pairs={{0,2},{2,0},{16,18},{18,16},{32,34},{34,32},{48,50},{50,48},{64,66... | collective-permute-start | bytes 1376264 | tf_op jit(solution)/shard_map/ppermute | solution.py:30
  37.5 7.8 %collective-permute-start.11 = (bf16[2,112,1024]{2,1,0:T(8,128)(2,1)S(1)}, bf16[2,112,1024]{2,1,0:T(8,128)(2,1)S(1)}, u32[]{:S(2)}, u32[]{:S(2)}) collective-permute-start(bf16[2,112,1024]{2,1,0:T(8,128)(2,1)S(1)} %collective-permute-done.8.refs_2_), channel_id=1, source_target_pairs={{0,2},{2,0},{16,18},{18,16},{32,34},{34,32},{48,50},{50,48},{64,66... | collective-permute-start | bytes 1376264 | tf_op jit(solution)/shard_map/ppermute | solution.py:30
  37.5 7.8 %collective-permute-start.12 = (bf16[2,112,1024]{2,1,0:T(8,128)(2,1)S(1)}, bf16[2,112,1024]{2,1,0:T(8,128)(2,1)S(1)}, u32[]{:S(2)}, u32[]{:S(2)}) collective-permute-start(bf16[2,112,1024]{2,1,0:T(8,128)(2,1)S(1)} %collective-permute-done.9.refs_3_), channel_id=1, source_target_pairs={{0,2},{2,0},{16,18},{18,16},{32,34},{34,32},{48,50},{50,48},{64,66... | collective-permute-start | bytes 1376264 | tf_op jit(solution)/shard_map/ppermute | solution.py:30
  43.5 1.8 %collective-permute-start.14 = (bf16[2,56,1024]{2,1,0:T(8,128)(2,1)S(1)}, bf16[2,56,1024]{2,1,0:T(8,128)(2,1)S(1)}, u32[]{:S(2)}, u32[]{:S(2)}) collective-permute-start(bf16[2,56,1024]{2,1,0:T(8,128)(2,1)S(1)} %collective-permute-done.13), channel_id=1, source_target_pairs={{0,2},{2,0},{16,18},{18,16},{32,34},{34,32},{48,50},{50,48},{64,66... | collective-permute-start | bytes 688136 | tf_op jit(solution)/shard_map/ppermute | solution.py:30
  51.5 1.9 %collective-permute-start.15 = (f32[16,128]{1,0:T(8,128)S(1)}, f32[16,128]{1,0:T(8,128)S(1)}, u32[]{:S(2)}, u32[]{:S(2)}) collective-permute-start(f32[16,128]{1,0:T(8,128)S(1)} %gram.1), channel_id=1, source_target_pairs={{0,2},{2,0},{16,18},{18,16},{32,34},{34,32},{48,50},{50,48},{64,66... | collective-permute-start | bytes 24584 | tf_op jit(solution)/shard_map/ppermute | solution.py:30
  51.9 3.7 %collective-permute-start.16 = (f32[16,128]{1,0:T(8,128)S(1)}, f32[16,128]{1,0:T(8,128)S(1)}, u32[]{:S(2)}, u32[]{:S(2)}) collective-permute-start(f32[16,128]{1,0:T(8,128)S(1)} %gram.1), channel_id=1, source_target_pairs={{0,16},{2,18},{16,0},{18,2},{32,48},{34,50},{48,32},{50,34},{64,80... | collective-permute-start | bytes 24584 | tf_op jit(solution)/shard_map/ppermute | solution.py:30
  52.9 3.1 %collective-permute-start.17 = (f32[16,128]{1,0:T(8,128)S(1)}, f32[16,128]{1,0:T(8,128)S(1)}, u32[]{:S(2)}, u32[]{:S(2)}) collective-permute-start(f32[16,128]{1,0:T(8,128)S(1)} %gram.1), channel_id=1, source_target_pairs={{0,18},{2,16},{16,2},{18,0},{32,50},{34,48},{48,34},{50,32},{64,82... | collective-permute-start | bytes 24584 | tf_op jit(solution)/shard_map/ppermute | solution.py:30
  56.0 8.7 %collective-permute-start.18 = (f32[16,128]{1,0:T(8,128)S(1)}, f32[16,128]{1,0:T(8,128)S(1)}, u32[]{:S(2)}, u32[]{:S(2)}) collective-permute-start(f32[16,128]{1,0:T(8,128)S(1)} %add_add_fusion.1), channel_id=1, source_target_pairs={{0,64},{2,66},{16,80},{18,82},{32,96},{34,98},{48,112},{50,114},{6... | collective-permute-start | bytes 24584 | tf_op jit(solution)/shard_map/ppermute | solution.py:30
  60.6 5.8 %collective-permute-start.19 = (f32[16,128]{1,0:T(8,128)S(1)}, f32[16,128]{1,0:T(8,128)S(1)}, u32[]{:S(2)}, u32[]{:S(2)}) collective-permute-start(f32[16,128]{1,0:T(8,128)S(1)} %add_add_fusion.1), channel_id=1, source_target_pairs={{0,32},{2,34},{16,48},{18,50},{32,64},{34,66},{48,80},{50,82},{64,... | collective-permute-start | bytes 24584 | tf_op jit(solution)/shard_map/ppermute | solution.py:30
  60.6 5.7 %collective-permute-start.20 = (f32[16,128]{1,0:T(8,128)S(1)}, f32[16,128]{1,0:T(8,128)S(1)}, u32[]{:S(2)}, u32[]{:S(2)}) collective-permute-start(f32[16,128]{1,0:T(8,128)S(1)} %add_add_fusion.1), channel_id=1, source_target_pairs={{0,96},{2,98},{16,112},{18,114},{32,0},{34,2},{48,16},{50,18},{64,... | collective-permute-start | bytes 24584 | tf_op jit(solution)/shard_map/ppermute | solution.py:30
  66.4 5.2 %collective-permute-start.21 = (f32[8,128]{1,0:T(8,128)S(1)}, f32[8,128]{1,0:T(8,128)S(1)}, u32[]{:S(2)}, u32[]{:S(2)}) collective-permute-start(f32[8,128]{1,0:T(8,128)S(1)} %stack.37), channel_id=1, source_target_pairs={{0,128},{2,130},{16,144},{18,146},{32,160},{34,162},{48,176},{50,1... | collective-permute-start | bytes 12296 | tf_op jit(solution)/shard_map/ppermute | solution.py:30
  68.3 3.6 %collective-permute-start.22 = (f32[8,128]{1,0:T(8,128)S(1)}, f32[8,128]{1,0:T(8,128)S(1)}, u32[]{:S(2)}, u32[]{:S(2)}) collective-permute-start(f32[8,128]{1,0:T(8,128)S(1)} %stack.37), channel_id=1, source_target_pairs={{0,1},{2,3},{16,17},{18,19},{32,33},{34,35},{48,49},{50,51},{64,65... | collective-permute-start | bytes 12296 | tf_op jit(solution)/shard_map/ppermute | solution.py:30
  69.4 4.8 %collective-permute-start.23 = (f32[8,128]{1,0:T(8,128)S(1)}, f32[8,128]{1,0:T(8,128)S(1)}, u32[]{:S(2)}, u32[]{:S(2)}) collective-permute-start(f32[8,128]{1,0:T(8,128)S(1)} %stack.37), channel_id=1, source_target_pairs={{0,129},{2,131},{16,145},{18,147},{32,161},{34,163},{48,177},{50,1... | collective-permute-start | bytes 12296 | tf_op jit(solution)/shard_map/ppermute | solution.py:30
  74.2 6.7 %collective-permute-start.24 = (f32[8,128]{1,0:T(8,128)S(1)}, f32[8,128]{1,0:T(8,128)S(1)}, u32[]{:S(2)}, u32[]{:S(2)}) collective-permute-start(f32[8,128]{1,0:T(8,128)S(1)} %add_add_fusion.2.sums_ref), channel_id=1, source_target_pairs={{0,8},{2,10},{16,24},{18,26},{32,40},{34,42},{48,56},{50,58},{64,7... | collective-permute-start | bytes 12296 | tf_op jit(solution)/shard_map/ppermute | solution.py:30
  77.6 4.8 %collective-permute-start.25 = (f32[8,128]{1,0:T(8,128)S(1)}, f32[8,128]{1,0:T(8,128)S(1)}, u32[]{:S(2)}, u32[]{:S(2)}) collective-permute-start(f32[8,128]{1,0:T(8,128)S(1)} %add_add_fusion.2.sums_ref), channel_id=1, source_target_pairs={{0,4},{2,6},{16,20},{18,22},{32,36},{34,38},{48,52},{50,54},{64,68... | collective-permute-start | bytes 12296 | tf_op jit(solution)/shard_map/ppermute | solution.py:30
  78.1 4.4 %collective-permute-start.26 = (f32[8,128]{1,0:T(8,128)S(1)}, f32[8,128]{1,0:T(8,128)S(1)}, u32[]{:S(2)}, u32[]{:S(2)}) collective-permute-start(f32[8,128]{1,0:T(8,128)S(1)} %add_add_fusion.2.sums_ref), channel_id=1, source_target_pairs={{0,12},{2,14},{16,28},{18,30},{32,44},{34,46},{48,60},{50,62},{64,... | collective-permute-start | bytes 12296 | tf_op jit(solution)/shard_map/ppermute | solution.py:30

commit v8 on v7

--- a/solution.py
+++ b/solution.py
@@ -234,16 +234,17 @@
     own = lax.optimization_barrier(jnp.stack([layer_one, layer_two]))
     count = own.shape[1]
     near = [shift(own, step, 0) for step in (1, -1, 2)]
+    far = move(own, lambda x, y, z, core: (x, y, z + 4, core))
     chip = jnp.concatenate([own, swap(own)], axis=1)
     strip = jnp.concatenate([own] + near, axis=1)
-    first, strip = lax.optimization_barrier((around(chip), strip))
+    chip, strip, far = lax.optimization_barrier((chip, strip, far))
     pieces = [strip] + [shift(strip, 0, step) for step in (1, -1, 2)]
-    ring = [first]
+    ring = [around(chip)]
     for _ in range(2):
         ring.append(around(ring[-1]))
-    last = around(ring[2][:, :count])
-    ends = jnp.concatenate([last, swap(last)], axis=1)
-    line = [chip] + ring + [swap(block) for block in ring] + [ends]
+    ends = jnp.concatenate([far, swap(far)], axis=1)
+    pieces, late = lax.optimization_barrier((pieces, ring[2]))
+    line = [chip] + ring + [swap(ring[0]), swap(ring[1]), swap(late)] + [ends]
     part = line_sum(gram(spread, *plane_rows(spread, pieces), line))
     r_one, r_two = part[0:7], part[8:15]
     terms = [r_one, r_two, part[7:8], part[15:16], r_one * r_two, r_one * r_one, r_two * r_two]

time: 83.4 us -> 93.9 us (1.13)
  waiting for transfers between devices: 31.5 us -> 37.9 us
  starting transfers between devices: 41.5 us -> 45.5 us
    ppermute x27, waiting for transfers between devices: 31.5 us -> 37.9 us  [move(): return lax.ppermute(array, AXES, pairs)]
    ppermute x27, starting transfers between devices: 41.5 us -> 45.5 us  [move(): return lax.ppermute(array, AXES, pairs)]
  transfers between devices with their start and end apart: 27 -> 27, of which waited for: 14 -> 13; matrix products, arithmetic and copies ran while one was open for 0% -> 0% of each run, Pallas kernels for 2% -> 1%
where the time goes in v8:
time: 93.9 us; the launch traced here: 93.6 us
  starting transfers between devices  45.5 us (48%)
  waiting for transfers between devices  37.9 us (40%)
  Pallas kernels  8.22 us (9%)
  other arithmetic  1.14 us (1%)
    ppermute x27, starting transfers between devices, move(): return lax.ppermute(array, AXES, pairs)  45.5 us
    ppermute x27, waiting for transfers between devices, move(): return lax.ppermute(array, AXES, pairs)  37.9 us
    pallas_call x1, Pallas kernels, gram(): pl.pallas_call(gram_body, out_shape=jax.ShapeDtypeStruct((16, 128), jnp.f...  6.17 us
  transfers between devices with their start and end apart: 27, of which 13 were waited for; matrix products, arithmetic and copies ran while one was open for 0% of the time, Pallas kernels for 1%

profile of v8, /device:TPU:6, one launch (start us, length us, event | category | flops | bytes accessed | tf_op | source)
XLA Modules:
  0.0 93.6 jit_solution(16400550983217920252)
XLA Ops:
  0.6 1.0 %pad_maximum_fusion.3 = bf16[2,56,1024]{2,1,0:T(8,128)(2,1)S(1)} fusion(bf16[1,56,1024]{2,1,0:T(8,128)(2,1)} %bitcast.8, bf16[1,56,1024]{2,1,0:T(8,128)(2,1)} %bitcast.9), kind=kLoop, calls=%fused_computation.3 | loop fusion | flops 114688 | bytes 458752 | tf_op jit(solution)/shard_map/stack | solution.py:234
  1.7 2.3 %collective-permute-start.1 = (bf16[2,56,1024]{2,1,0:T(8,128)(2,1)S(1)}, bf16[2,56,1024]{2,1,0:T(8,128)(2,1)S(1)}, u32[]{:S(2)}, u32[]{:S(2)}) collective-permute-start(bf16[2,56,1024]{2,1,0:T(8,128)(2,1)S(1)} %pad_maximum_fusion.3), channel_id=1, source_target_pairs={{0,1},{2,6},{16,17},{18,22},{32,33},{34,38},{48,49},{50,54},{64,65... | collective-permute-start | bytes 688136 | tf_op jit(solution)/shard_map/ppermute | solution.py:30
  4.0 1.6 %collective-permute-start.3 = (bf16[2,56,1024]{2,1,0:T(8,128)(2,1)S(1)}, bf16[2,56,1024]{2,1,0:T(8,128)(2,1)S(1)}, u32[]{:S(2)}, u32[]{:S(2)}) collective-permute-start(bf16[2,56,1024]{2,1,0:T(8,128)(2,1)S(1)} %pad_maximum_fusion.3), channel_id=1, source_target_pairs={{0,128},{2,10},{16,144},{18,26},{32,160},{34,42},{48,176},{50,58},... | collective-permute-start | bytes 688136 | tf_op jit(solution)/shard_map/ppermute | solution.py:30
  5.6 6.9 %collective-permute-start.4 = (bf16[2,56,1024]{2,1,0:T(8,128)(2,1)S(1)}, bf16[2,56,1024]{2,1,0:T(8,128)(2,1)S(1)}, u32[]{:S(2)}, u32[]{:S(2)}) collective-permute-start(bf16[2,56,1024]{2,1,0:T(8,128)(2,1)S(1)} %pad_maximum_fusion.3), channel_id=1, source_target_pairs={{0,64},{2,66},{16,80},{18,82},{32,96},{34,98},{48,112},{50,114},{6... | collective-permute-start | bytes 688136 | tf_op jit(solution)/shard_map/ppermute | solution.py:30
  12.5 1.2 %collective-permute-done.2 = bf16[2,56,1024]{2,1,0:T(8,128)(2,1)S(1)} collective-permute-done((bf16[2,56,1024]{2,1,0:T(8,128)(2,1)S(1)}, bf16[2,56,1024]{2,1,0:T(8,128)(2,1)S(1)}, u32[]{:S(2)}, u32[]{:S(2)}) %collective-permute-start.2) | collective-permute-done | bytes 229408 | tf_op jit(solution)/shard_map/ppermute | solution.py:30
  13.8 5.2 %collective-permute-done.4 = bf16[2,56,1024]{2,1,0:T(8,128)(2,1)S(1)} collective-permute-done((bf16[2,56,1024]{2,1,0:T(8,128)(2,1)S(1)}, bf16[2,56,1024]{2,1,0:T(8,128)(2,1)S(1)}, u32[]{:S(2)}, u32[]{:S(2)}) %collective-permute-start.4) | collective-permute-done | bytes 229408 | tf_op jit(solution)/shard_map/ppermute | solution.py:30
  19.0 4.9 %collective-permute-start.8 = (bf16[2,112,1024]{2,1,0:T(8,128)(2,1)S(1)}, bf16[2,112,1024]{2,1,0:T(8,128)(2,1)S(1)}, u32[]{:S(2)}, u32[]{:S(2)}) collective-permute-start(bf16[2,112,1024]{2,1,0:T(8,128)(2,1)S(1)} %pad_maximum_fusion.1.refs_0_), channel_id=1, source_target_pairs={{0,16},{2,114},{16,32},{18,2},{32,48},{34,18},{48,64},{50,34},{64,... | collective-permute-start | bytes 1376264 | tf_op jit(solution)/shard_map/ppermute | solution.py:30
  23.9 2.4 %collective-permute-start.5 = (bf16[2,224,1024]{2,1,0:T(8,128)(2,1)S(1)}, bf16[2,224,1024]{2,1,0:T(8,128)(2,1)S(1)}, u32[]{:S(2)}, u32[]{:S(2)}) collective-permute-start(bf16[2,224,1024]{2,1,0:T(8,128)(2,1)S(1)} %pad_maximum_fusion.refs_0_), channel_id=1, source_target_pairs={{0,4},{2,3},{16,20},{18,19},{32,36},{34,35},{48,52},{50,51},{64,68... | collective-permute-start | bytes 2752520 | tf_op jit(solution)/shard_map/ppermute | solution.py:30
  26.3 0.9 collective-permute-start.6
  27.1 2.1 %collective-permute-start.7 = (bf16[2,224,1024]{2,1,0:T(8,128)(2,1)S(1)}, bf16[2,224,1024]{2,1,0:T(8,128)(2,1)S(1)}, u32[]{:S(2)}, u32[]{:S(2)}) collective-permute-start(bf16[2,224,1024]{2,1,0:T(8,128)(2,1)S(1)} %pad_maximum_fusion.refs_0_), channel_id=1, source_target_pairs={{0,8},{2,130},{16,24},{18,146},{32,40},{34,162},{48,56},{50,178},{... | collective-permute-start | bytes 2752520 | tf_op jit(solution)/shard_map/ppermute | solution.py:30
  29.3 3.7 %collective-permute-done.8.refs_1_ = bf16[2,112,1024]{2,1,0:T(8,128)(2,1)S(1)} collective-permute-done((bf16[2,112,1024]{2,1,0:T(8,128)(2,1)S(1)}, bf16[2,112,1024]{2,1,0:T(8,128)(2,1)S(1)}, u32[]{:S(2)}, u32[]{:S(2)}) %collective-permute-start.8) | collective-permute-done | bytes 458784 | tf_op jit(solution)/shard_map/ppermute | solution.py:30
  32.9 9.7 %collective-permute-done.9.refs_2_ = bf16[2,112,1024]{2,1,0:T(8,128)(2,1)S(1)} collective-permute-done((bf16[2,112,1024]{2,1,0:T(8,128)(2,1)S(1)}, bf16[2,112,1024]{2,1,0:T(8,128)(2,1)S(1)}, u32[]{:S(2)}, u32[]{:S(2)}) %collective-permute-start.9) | collective-permute-done | bytes 458784 | tf_op jit(solution)/shard_map/ppermute | solution.py:30
  42.6 1.2 %collective-permute-start.11 = (bf16[2,112,1024]{2,1,0:T(8,128)(2,1)S(1)}, bf16[2,112,1024]{2,1,0:T(8,128)(2,1)S(1)}, u32[]{:S(2)}, u32[]{:S(2)}) collective-permute-start(bf16[2,112,1024]{2,1,0:T(8,128)(2,1)S(1)} %collective-permute-done.8.refs_1_), channel_id=1, source_target_pairs={{0,2},{2,0},{16,18},{18,16},{32,34},{34,32},{48,50},{50,48},{64,66... | collective-permute-start | bytes 1376264 | tf_op jit(solution)/shard_map/ppermute | solution.py:30
  43.9 5.5 %collective-permute-done.7.refs_3_ = bf16[2,224,1024]{2,1,0:T(8,128)(2,1)S(1)} collective-permute-done((bf16[2,224,1024]{2,1,0:T(8,128)(2,1)S(1)}, bf16[2,224,1024]{2,1,0:T(8,128)(2,1)S(1)}, u32[]{:S(2)}, u32[]{:S(2)}) %collective-permute-start.7) | collective-permute-done | bytes 917536 | tf_op jit(solution)/shard_map/ppermute | solution.py:30
  49.4 3.0 %collective-permute-done.10.refs_3_ = bf16[2,112,1024]{2,1,0:T(8,128)(2,1)S(1)} collective-permute-done((bf16[2,112,1024]{2,1,0:T(8,128)(2,1)S(1)}, bf16[2,112,1024]{2,1,0:T(8,128)(2,1)S(1)}, u32[]{:S(2)}, u32[]{:S(2)}) %collective-permute-start.10) | collective-permute-done | bytes 458784 | tf_op jit(solution)/shard_map/ppermute | solution.py:30
  52.3 0.5 collective-permute-start.14
  52.8 1.6 %collective-permute-done.14 = bf16[2,56,1024]{2,1,0:T(8,128)(2,1)S(1)} collective-permute-done((bf16[2,56,1024]{2,1,0:T(8,128)(2,1)S(1)}, bf16[2,56,1024]{2,1,0:T(8,128)(2,1)S(1)}, u32[]{:S(2)}, u32[]{:S(2)}) %collective-permute-start.14) | collective-permute-done | bytes 229408 | tf_op jit(solution)/shard_map/ppermute | solution.py:30
  54.5 1.4 %plane_rows.1 = (bf16[2,896,1024]{2,1,0:T(8,128)(2,1)S(1)}, f32[2,896,128]{2,1,0:T(8,128)S(1)}) custom-call(s32[2]{0:T(128)S(1)} %copy-done, bf16[2,224,1024]{2,1,0:T(8,128)(2,1)S(1)} %pad_maximum_fusion.refs_0_, bf16[2,224,1024]{2,1,0:T(8,128)(2,1)S(1)} %collective-permute-done.5.refs_1_, bf16[2,224,1024]{2,1,0:T(8,128)(2,1)S(1)} %collective-permute-done.6.refs_2_, ...), custom_call_target="tpu_custom_call" | custom-call | flops 3670016 | bytes 7340032 | tf_op jit(solution)/shard_map/plane_rows/pallas_call | solution.py:83
  55.9 6.2 %gram.1 = f32[16,128]{1,0:T(8,128)S(1)} custom-call(s32[2]{0:T(128)S(1)} %copy-done, bf16[2,896,1024]{2,1,0:T(8,128)(2,1)S(1)} %get-tuple-element.20.w_ref, f32[2,896,128]{2,1,0:T(8,128)S(1)} %get-tuple-element.21.norm_ref, bf16[2,112,1024]{2,1,0:T(8,128)(2,1)S(1)} %pad_maximum_fusion.1.refs_0_, bf16[2,112,1024]{2,1,0:T(8,128)(2,1)S(1)} %collective-permute-done.8.refs_1_, ...), custom_call_target="tpu_custom_call" | custom-call | flops 3288334336 | bytes 7340032 | tf_op jit(solution)/shard_map/gram/pallas_call | solution.py:159
  62.3 1.7 %collective-permute-start.17 = (f32[16,128]{1,0:T(8,128)S(1)}, f32[16,128]{1,0:T(8,128)S(1)}, u32[]{:S(2)}, u32[]{:S(2)}) collective-permute-start(f32[16,128]{1,0:T(8,128)S(1)} %gram.1), channel_id=1, source_target_pairs={{0,18},{2,16},{16,2},{18,0},{32,50},{34,48},{48,34},{50,32},{64,82... | collective-permute-start | bytes 24584 | tf_op jit(solution)/shard_map/ppermute | solution.py:30
  64.0 2.0 %collective-permute-done.16 = f32[16,128]{1,0:T(8,128)S(1)} collective-permute-done((f32[16,128]{1,0:T(8,128)S(1)}, f32[16,128]{1,0:T(8,128)S(1)}, u32[]{:S(2)}, u32[]{:S(2)}) %collective-permute-start.16) | collective-permute-done | bytes 8224 | tf_op jit(solution)/shard_map/ppermute | solution.py:30
  65.9 5.8 %collective-permute-start.18 = (f32[16,128]{1,0:T(8,128)S(1)}, f32[16,128]{1,0:T(8,128)S(1)}, u32[]{:S(2)}, u32[]{:S(2)}) collective-permute-start(f32[16,128]{1,0:T(8,128)S(1)} %add_add_fusion.1), channel_id=1, source_target_pairs={{0,64},{2,66},{16,80},{18,82},{32,96},{34,98},{48,112},{50,114},{6... | collective-permute-start | bytes 24584 | tf_op jit(solution)/shard_map/ppermute | solution.py:30
  71.8 4.1 %collective-permute-start.20 = (f32[16,128]{1,0:T(8,128)S(1)}, f32[16,128]{1,0:T(8,128)S(1)}, u32[]{:S(2)}, u32[]{:S(2)}) collective-permute-start(f32[16,128]{1,0:T(8,128)S(1)} %add_add_fusion.1), channel_id=1, source_target_pairs={{0,96},{2,98},{16,112},{18,114},{32,0},{34,2},{48,16},{50,18},{64,... | collective-permute-start | bytes 24584 | tf_op jit(solution)/shard_map/ppermute | solution.py:30
  75.9 1.6 %collective-permute-done.19 = f32[16,128]{1,0:T(8,128)S(1)} collective-permute-done((f32[16,128]{1,0:T(8,128)S(1)}, f32[16,128]{1,0:T(8,128)S(1)}, u32[]{:S(2)}, u32[]{:S(2)}) %collective-permute-start.19) | collective-permute-done | bytes 8224 | tf_op jit(solution)/shard_map/ppermute | solution.py:30
  77.6 1.9 %collective-permute-start.21 = (f32[8,128]{1,0:T(8,128)S(1)}, f32[8,128]{1,0:T(8,128)S(1)}, u32[]{:S(2)}, u32[]{:S(2)}) collective-permute-start(f32[8,128]{1,0:T(8,128)S(1)} %stack.37), channel_id=1, source_target_pairs={{0,128},{2,130},{16,144},{18,146},{32,160},{34,162},{48,176},{50,1... | collective-permute-start | bytes 12296 | tf_op jit(solution)/shard_map/ppermute | solution.py:30
  79.6 2.0 %collective-permute-start.23 = (f32[8,128]{1,0:T(8,128)S(1)}, f32[8,128]{1,0:T(8,128)S(1)}, u32[]{:S(2)}, u32[]{:S(2)}) collective-permute-start(f32[8,128]{1,0:T(8,128)S(1)} %stack.37), channel_id=1, source_target_pairs={{0,129},{2,131},{16,145},{18,147},{32,161},{34,163},{48,177},{50,1... | collective-permute-start | bytes 12296 | tf_op jit(solution)/shard_map/ppermute | solution.py:30
  81.6 1.2 %collective-permute-done.21 = f32[8,128]{1,0:T(8,128)S(1)} collective-permute-done((f32[8,128]{1,0:T(8,128)S(1)}, f32[8,128]{1,0:T(8,128)S(1)}, u32[]{:S(2)}, u32[]{:S(2)}) %collective-permute-start.21) | collective-permute-done | bytes 4128 | tf_op jit(solution)/shard_map/ppermute | solution.py:30
  83.2 1.2 %collective-permute-done.23 = f32[8,128]{1,0:T(8,128)S(1)} collective-permute-done((f32[8,128]{1,0:T(8,128)S(1)}, f32[8,128]{1,0:T(8,128)S(1)}, u32[]{:S(2)}, u32[]{:S(2)}) %collective-permute-start.23) | collective-permute-done | bytes 4128 | tf_op jit(solution)/shard_map/ppermute | solution.py:30
  84.4 3.7 %collective-permute-start.24 = (f32[8,128]{1,0:T(8,128)S(1)}, f32[8,128]{1,0:T(8,128)S(1)}, u32[]{:S(2)}, u32[]{:S(2)}) collective-permute-start(f32[8,128]{1,0:T(8,128)S(1)} %add_add_fusion.2.sums_ref), channel_id=1, source_target_pairs={{0,8},{2,10},{16,24},{18,26},{32,40},{34,42},{48,56},{50,58},{64,7... | collective-permute-start | bytes 12296 | tf_op jit(solution)/shard_map/ppermute | solution.py:30
  88.4 2.9 %collective-permute-start.26 = (f32[8,128]{1,0:T(8,128)S(1)}, f32[8,128]{1,0:T(8,128)S(1)}, u32[]{:S(2)}, u32[]{:S(2)}) collective-permute-start(f32[8,128]{1,0:T(8,128)S(1)} %add_add_fusion.2.sums_ref), channel_id=1, source_target_pairs={{0,12},{2,14},{16,28},{18,30},{32,44},{34,46},{48,60},{50,62},{64,... | collective-permute-start | bytes 12296 | tf_op jit(solution)/shard_map/ppermute | solution.py:30
  91.3 1.6 %collective-permute-done.25.refs_1_ = f32[8,128]{1,0:T(8,128)S(1)} collective-permute-done((f32[8,128]{1,0:T(8,128)S(1)}, f32[8,128]{1,0:T(8,128)S(1)}, u32[]{:S(2)}, u32[]{:S(2)}) %collective-permute-start.25) | collective-permute-done | bytes 4128 | tf_op jit(solution)/shard_map/ppermute | solution.py:30
  92.9 0.7 finish.1
  (38 shorter events, 1.2 us)
Async XLA Ops:
  1.6 52.9 %copy-start = (s32[2]{0:T(128)S(1)}, s32[2]{0:T(128)}, u32[]{:S(2)}) copy-start(s32[2]{0:T(128)} %spread_ref.3) | copy-start | bytes 28
  1.6 10.8 %collective-permute-start = (bf16[2,56,1024]{2,1,0:T(8,128)(2,1)S(1)}, bf16[2,56,1024]{2,1,0:T(8,128)(2,1)S(1)}, u32[]{:S(2)}, u32[]{:S(2)}) collective-permute-start(bf16[2,56,1024]{2,1,0:T(8,128)(2,1)S(1)} %pad_maximum_fusion.3), channel_id=1, source_target_pairs={{0,2},{2,0},{16,18},{18,16},{32,34},{34,32},{48,50},{50,48},{64,66... | collective-permute-start | bytes 688136 | tf_op jit(solution)/shard_map/ppermute | solution.py:30
  1.7 10.7 %collective-permute-start.1 = (bf16[2,56,1024]{2,1,0:T(8,128)(2,1)S(1)}, bf16[2,56,1024]{2,1,0:T(8,128)(2,1)S(1)}, u32[]{:S(2)}, u32[]{:S(2)}) collective-permute-start(bf16[2,56,1024]{2,1,0:T(8,128)(2,1)S(1)} %pad_maximum_fusion.3), channel_id=1, source_target_pairs={{0,1},{2,6},{16,17},{18,22},{32,33},{34,38},{48,49},{50,54},{64,65... | collective-permute-start | bytes 688136 | tf_op jit(solution)/shard_map/ppermute | solution.py:30
  4.0 9.7 %collective-permute-start.2 = (bf16[2,56,1024]{2,1,0:T(8,128)(2,1)S(1)}, bf16[2,56,1024]{2,1,0:T(8,128)(2,1)S(1)}, u32[]{:S(2)}, u32[]{:S(2)}) collective-permute-start(bf16[2,56,1024]{2,1,0:T(8,128)(2,1)S(1)} %pad_maximum_fusion.3), channel_id=1, source_target_pairs={{0,129},{2,14},{16,145},{18,30},{32,161},{34,46},{48,177},{50,62},... | collective-permute-start | bytes 688136 | tf_op jit(solution)/shard_map/ppermute | solution.py:30
  4.0 9.7 %collective-permute-start.3 = (bf16[2,56,1024]{2,1,0:T(8,128)(2,1)S(1)}, bf16[2,56,1024]{2,1,0:T(8,128)(2,1)S(1)}, u32[]{:S(2)}, u32[]{:S(2)}) collective-permute-start(bf16[2,56,1024]{2,1,0:T(8,128)(2,1)S(1)} %pad_maximum_fusion.3), channel_id=1, source_target_pairs={{0,128},{2,10},{16,144},{18,26},{32,160},{34,42},{48,176},{50,58},... | collective-permute-start | bytes 688136 | tf_op jit(solution)/shard_map/ppermute | solution.py:30
  5.6 13.4 %collective-permute-start.4 = (bf16[2,56,1024]{2,1,0:T(8,128)(2,1)S(1)}, bf16[2,56,1024]{2,1,0:T(8,128)(2,1)S(1)}, u32[]{:S(2)}, u32[]{:S(2)}) collective-permute-start(bf16[2,56,1024]{2,1,0:T(8,128)(2,1)S(1)} %pad_maximum_fusion.3), channel_id=1, source_target_pairs={{0,64},{2,66},{16,80},{18,82},{32,96},{34,98},{48,112},{50,114},{6... | collective-permute-start | bytes 688136 | tf_op jit(solution)/shard_map/ppermute | solution.py:30
  19.0 13.9 %collective-permute-start.8 = (bf16[2,112,1024]{2,1,0:T(8,128)(2,1)S(1)}, bf16[2,112,1024]{2,1,0:T(8,128)(2,1)S(1)}, u32[]{:S(2)}, u32[]{:S(2)}) collective-permute-start(bf16[2,112,1024]{2,1,0:T(8,128)(2,1)S(1)} %pad_maximum_fusion.1.refs_0_), channel_id=1, source_target_pairs={{0,16},{2,114},{16,32},{18,2},{32,48},{34,18},{48,64},{50,34},{64,... | collective-permute-start | bytes 1376264 | tf_op jit(solution)/shard_map/ppermute | solution.py:30
  23.9 20.0 %collective-permute-start.5 = (bf16[2,224,1024]{2,1,0:T(8,128)(2,1)S(1)}, bf16[2,224,1024]{2,1,0:T(8,128)(2,1)S(1)}, u32[]{:S(2)}, u32[]{:S(2)}) collective-permute-start(bf16[2,224,1024]{2,1,0:T(8,128)(2,1)S(1)} %pad_maximum_fusion.refs_0_), channel_id=1, source_target_pairs={{0,4},{2,3},{16,20},{18,19},{32,36},{34,35},{48,52},{50,51},{64,68... | collective-permute-start | bytes 2752520 | tf_op jit(solution)/shard_map/ppermute | solution.py:30
  26.3 17.6 %collective-permute-start.6 = (bf16[2,224,1024]{2,1,0:T(8,128)(2,1)S(1)}, bf16[2,224,1024]{2,1,0:T(8,128)(2,1)S(1)}, u32[]{:S(2)}, u32[]{:S(2)}) collective-permute-start(bf16[2,224,1024]{2,1,0:T(8,128)(2,1)S(1)} %pad_maximum_fusion.refs_0_), channel_id=1, source_target_pairs={{0,12},{2,131},{16,28},{18,147},{32,44},{34,163},{48,60},{50,179},... | collective-permute-start | bytes 2752520 | tf_op jit(solution)/shard_map/ppermute | solution.py:30
  27.1 22.2 %collective-permute-start.7 = (bf16[2,224,1024]{2,1,0:T(8,128)(2,1)S(1)}, bf16[2,224,1024]{2,1,0:T(8,128)(2,1)S(1)}, u32[]{:S(2)}, u32[]{:S(2)}) collective-permute-start(bf16[2,224,1024]{2,1,0:T(8,128)(2,1)S(1)} %pad_maximum_fusion.refs_0_), channel_id=1, source_target_pairs={{0,8},{2,130},{16,24},{18,146},{32,40},{34,162},{48,56},{50,178},{... | collective-permute-start | bytes 2752520 | tf_op jit(solution)/shard_map/ppermute | solution.py:30
  32.9 9.7 %collective-permute-start.9 = (bf16[2,112,1024]{2,1,0:T(8,128)(2,1)S(1)}, bf16[2,112,1024]{2,1,0:T(8,128)(2,1)S(1)}, u32[]{:S(2)}, u32[]{:S(2)}) collective-permute-start(bf16[2,112,1024]{2,1,0:T(8,128)(2,1)S(1)} %collective-permute-done.8.refs_1_), channel_id=1, source_target_pairs={{0,16},{2,114},{16,32},{18,2},{32,48},{34,18},{48,64},{50,34},{64,... | collective-permute-start | bytes 1376264 | tf_op jit(solution)/shard_map/ppermute | solution.py:30
  42.6 9.7 %collective-permute-start.10 = (bf16[2,112,1024]{2,1,0:T(8,128)(2,1)S(1)}, bf16[2,112,1024]{2,1,0:T(8,128)(2,1)S(1)}, u32[]{:S(2)}, u32[]{:S(2)}) collective-permute-start(bf16[2,112,1024]{2,1,0:T(8,128)(2,1)S(1)} %collective-permute-done.9.refs_2_), channel_id=1, source_target_pairs={{0,16},{2,114},{16,32},{18,2},{32,48},{34,18},{48,64},{50,34},{64,... | collective-permute-start | bytes 1376264 | tf_op jit(solution)/shard_map/ppermute | solution.py:30
  42.6 13.3 %collective-permute-start.11 = (bf16[2,112,1024]{2,1,0:T(8,128)(2,1)S(1)}, bf16[2,112,1024]{2,1,0:T(8,128)(2,1)S(1)}, u32[]{:S(2)}, u32[]{:S(2)}) collective-permute-start(bf16[2,112,1024]{2,1,0:T(8,128)(2,1)S(1)} %collective-permute-done.8.refs_1_), channel_id=1, source_target_pairs={{0,2},{2,0},{16,18},{18,16},{32,34},{34,32},{48,50},{50,48},{64,66... | collective-permute-start | bytes 1376264 | tf_op jit(solution)/shard_map/ppermute | solution.py:30
  43.9 12.0 %collective-permute-start.12 = (bf16[2,112,1024]{2,1,0:T(8,128)(2,1)S(1)}, bf16[2,112,1024]{2,1,0:T(8,128)(2,1)S(1)}, u32[]{:S(2)}, u32[]{:S(2)}) collective-permute-start(bf16[2,112,1024]{2,1,0:T(8,128)(2,1)S(1)} %collective-permute-done.9.refs_2_), channel_id=1, source_target_pairs={{0,2},{2,0},{16,18},{18,16},{32,34},{34,32},{48,50},{50,48},{64,66... | collective-permute-start | bytes 1376264 | tf_op jit(solution)/shard_map/ppermute | solution.py:30
  52.3 3.6 %collective-permute-start.13 = (bf16[2,112,1024]{2,1,0:T(8,128)(2,1)S(1)}, bf16[2,112,1024]{2,1,0:T(8,128)(2,1)S(1)}, u32[]{:S(2)}, u32[]{:S(2)}) collective-permute-start(bf16[2,112,1024]{2,1,0:T(8,128)(2,1)S(1)} %collective-permute-done.10.refs_3_), channel_id=1, source_target_pairs={{0,2},{2,0},{16,18},{18,16},{32,34},{34,32},{48,50},{50,48},{64,66... | collective-permute-start | bytes 1376264 | tf_op jit(solution)/shard_map/ppermute | solution.py:30
  52.3 2.1 %collective-permute-start.14 = (bf16[2,56,1024]{2,1,0:T(8,128)(2,1)S(1)}, bf16[2,56,1024]{2,1,0:T(8,128)(2,1)S(1)}, u32[]{:S(2)}, u32[]{:S(2)}) collective-permute-start(bf16[2,56,1024]{2,1,0:T(8,128)(2,1)S(1)} %collective-permute-done.4), channel_id=1, source_target_pairs={{0,2},{2,0},{16,18},{18,16},{32,34},{34,32},{48,50},{50,48},{64,66... | collective-permute-start | bytes 688136 | tf_op jit(solution)/shard_map/ppermute | solution.py:30
  62.1 1.9 %collective-permute-start.15 = (f32[16,128]{1,0:T(8,128)S(1)}, f32[16,128]{1,0:T(8,128)S(1)}, u32[]{:S(2)}, u32[]{:S(2)}) collective-permute-start(f32[16,128]{1,0:T(8,128)S(1)} %gram.1), channel_id=1, source_target_pairs={{0,2},{2,0},{16,18},{18,16},{32,34},{34,32},{48,50},{50,48},{64,66... | collective-permute-start | bytes 24584 | tf_op jit(solution)/shard_map/ppermute | solution.py:30
  62.3 3.7 %collective-permute-start.16 = (f32[16,128]{1,0:T(8,128)S(1)}, f32[16,128]{1,0:T(8,128)S(1)}, u32[]{:S(2)}, u32[]{:S(2)}) collective-permute-start(f32[16,128]{1,0:T(8,128)S(1)} %gram.1), channel_id=1, source_target_pairs={{0,16},{2,18},{16,0},{18,2},{32,48},{34,50},{48,32},{50,34},{64,80... | collective-permute-start | bytes 24584 | tf_op jit(solution)/shard_map/ppermute | solution.py:30
  62.3 3.7 %collective-permute-start.17 = (f32[16,128]{1,0:T(8,128)S(1)}, f32[16,128]{1,0:T(8,128)S(1)}, u32[]{:S(2)}, u32[]{:S(2)}) collective-permute-start(f32[16,128]{1,0:T(8,128)S(1)} %gram.1), channel_id=1, source_target_pairs={{0,18},{2,16},{16,2},{18,0},{32,50},{34,48},{48,34},{50,32},{64,82... | collective-permute-start | bytes 24584 | tf_op jit(solution)/shard_map/ppermute | solution.py:30
  65.9 10.0 %collective-permute-start.18 = (f32[16,128]{1,0:T(8,128)S(1)}, f32[16,128]{1,0:T(8,128)S(1)}, u32[]{:S(2)}, u32[]{:S(2)}) collective-permute-start(f32[16,128]{1,0:T(8,128)S(1)} %add_add_fusion.1), channel_id=1, source_target_pairs={{0,64},{2,66},{16,80},{18,82},{32,96},{34,98},{48,112},{50,114},{6... | collective-permute-start | bytes 24584 | tf_op jit(solution)/shard_map/ppermute | solution.py:30
  71.8 5.8 %collective-permute-start.19 = (f32[16,128]{1,0:T(8,128)S(1)}, f32[16,128]{1,0:T(8,128)S(1)}, u32[]{:S(2)}, u32[]{:S(2)}) collective-permute-start(f32[16,128]{1,0:T(8,128)S(1)} %add_add_fusion.1), channel_id=1, source_target_pairs={{0,32},{2,34},{16,48},{18,50},{32,64},{34,66},{48,80},{50,82},{64,... | collective-permute-start | bytes 24584 | tf_op jit(solution)/shard_map/ppermute | solution.py:30
  71.8 5.8 %collective-permute-start.20 = (f32[16,128]{1,0:T(8,128)S(1)}, f32[16,128]{1,0:T(8,128)S(1)}, u32[]{:S(2)}, u32[]{:S(2)}) collective-permute-start(f32[16,128]{1,0:T(8,128)S(1)} %add_add_fusion.1), channel_id=1, source_target_pairs={{0,96},{2,98},{16,112},{18,114},{32,0},{34,2},{48,16},{50,18},{64,... | collective-permute-start | bytes 24584 | tf_op jit(solution)/shard_map/ppermute | solution.py:30
  77.6 5.2 %collective-permute-start.21 = (f32[8,128]{1,0:T(8,128)S(1)}, f32[8,128]{1,0:T(8,128)S(1)}, u32[]{:S(2)}, u32[]{:S(2)}) collective-permute-start(f32[8,128]{1,0:T(8,128)S(1)} %stack.37), channel_id=1, source_target_pairs={{0,128},{2,130},{16,144},{18,146},{32,160},{34,162},{48,176},{50,1... | collective-permute-start | bytes 12296 | tf_op jit(solution)/shard_map/ppermute | solution.py:30
  79.6 3.6 %collective-permute-start.22 = (f32[8,128]{1,0:T(8,128)S(1)}, f32[8,128]{1,0:T(8,128)S(1)}, u32[]{:S(2)}, u32[]{:S(2)}) collective-permute-start(f32[8,128]{1,0:T(8,128)S(1)} %stack.37), channel_id=1, source_target_pairs={{0,1},{2,3},{16,17},{18,19},{32,33},{34,35},{48,49},{50,51},{64,65... | collective-permute-start | bytes 12296 | tf_op jit(solution)/shard_map/ppermute | solution.py:30
  79.6 4.8 %collective-permute-start.23 = (f32[8,128]{1,0:T(8,128)S(1)}, f32[8,128]{1,0:T(8,128)S(1)}, u32[]{:S(2)}, u32[]{:S(2)}) collective-permute-start(f32[8,128]{1,0:T(8,128)S(1)} %stack.37), channel_id=1, source_target_pairs={{0,129},{2,131},{16,145},{18,147},{32,161},{34,163},{48,177},{50,1... | collective-permute-start | bytes 12296 | tf_op jit(solution)/shard_map/ppermute | solution.py:30
  84.4 6.9 %collective-permute-start.24 = (f32[8,128]{1,0:T(8,128)S(1)}, f32[8,128]{1,0:T(8,128)S(1)}, u32[]{:S(2)}, u32[]{:S(2)}) collective-permute-start(f32[8,128]{1,0:T(8,128)S(1)} %add_add_fusion.2.sums_ref), channel_id=1, source_target_pairs={{0,8},{2,10},{16,24},{18,26},{32,40},{34,42},{48,56},{50,58},{64,7... | collective-permute-start | bytes 12296 | tf_op jit(solution)/shard_map/ppermute | solution.py:30
  88.1 4.8 %collective-permute-start.25 = (f32[8,128]{1,0:T(8,128)S(1)}, f32[8,128]{1,0:T(8,128)S(1)}, u32[]{:S(2)}, u32[]{:S(2)}) collective-permute-start(f32[8,128]{1,0:T(8,128)S(1)} %add_add_fusion.2.sums_ref), channel_id=1, source_target_pairs={{0,4},{2,6},{16,20},{18,22},{32,36},{34,38},{48,52},{50,54},{64,68... | collective-permute-start | bytes 12296 | tf_op jit(solution)/shard_map/ppermute | solution.py:30
  88.4 4.5 %collective-permute-start.26 = (f32[8,128]{1,0:T(8,128)S(1)}, f32[8,128]{1,0:T(8,128)S(1)}, u32[]{:S(2)}, u32[]{:S(2)}) collective-permute-start(f32[8,128]{1,0:T(8,128)S(1)} %add_add_fusion.2.sums_ref), channel_id=1, source_target_pairs={{0,12},{2,14},{16,28},{18,30},{32,44},{34,46},{48,60},{50,62},{64,... | collective-permute-start | bytes 12296 | tf_op jit(solution)/shard_map/ppermute | solution.py:30

commit v9 on v7

--- a/solution.py
+++ b/solution.py
@@ -243,7 +243,8 @@
         ring.append(around(ring[-1]))
     last = around(ring[2][:, :count])
     ends = jnp.concatenate([last, swap(last)], axis=1)
-    line = [chip] + ring + [swap(block) for block in ring] + [ends]
+    early = swap(jnp.concatenate(ring[:2], axis=1))
+    line = [chip] + ring + [early, swap(ring[2]), ends]
     part = line_sum(gram(spread, *plane_rows(spread, pieces), line))
     r_one, r_two = part[0:7], part[8:15]
     terms = [r_one, r_two, part[7:8], part[15:16], r_one * r_two, r_one * r_one, r_two * r_two]

time: 83.4 us -> 83.4 us (level)
  starting transfers between devices: 41.5 us -> 38.2 us
  waiting for transfers between devices: 31.5 us -> 34.6 us
    ppermute x27 -> x26, starting transfers between devices: 41.5 us -> 38.2 us  [move(): return lax.ppermute(array, AXES, pairs)]
    ppermute x27 -> x26, waiting for transfers between devices: 31.5 us -> 34.6 us  [move(): return lax.ppermute(array, AXES, pairs)]
  transfers between devices with their start and end apart: 27 -> 26, of which waited for: 14 -> 16; matrix products, arithmetic and copies ran while one was open for 0% -> 0% of each run, Pallas kernels for 2% -> 2%
where the time goes in v9:
time: 83.4 us; the launch traced here: 83.1 us
  starting transfers between devices  38.2 us (46%)
  waiting for transfers between devices  34.6 us (41%)
  Pallas kernels  8.24 us (10%)
  other arithmetic  1.2 us (1%)
    ppermute x26, starting transfers between devices, move(): return lax.ppermute(array, AXES, pairs)  38.2 us
    ppermute x26, waiting for transfers between devices, move(): return lax.ppermute(array, AXES, pairs)  34.6 us
    pallas_call x1, Pallas kernels, gram(): pl.pallas_call(gram_body, out_shape=jax.ShapeDtypeStruct((16, 128), jnp.f...  6.22 us
  transfers between devices with their start and end apart: 26, of which 16 were waited for; matrix products, arithmetic and copies ran while one was open for 0% of the time, Pallas kernels for 2%

profile of v9, /device:TPU:6, one launch (start us, length us, event | category | flops | bytes accessed | tf_op | source)
XLA Modules:
  0.0 83.1 jit_solution(18144381593054331833)
XLA Ops:
  0.6 1.0 %pad_maximum_fusion.4 = bf16[2,56,1024]{2,1,0:T(8,128)(2,1)S(1)} fusion(bf16[1,56,1024]{2,1,0:T(8,128)(2,1)} %bitcast.8, bf16[1,56,1024]{2,1,0:T(8,128)(2,1)} %bitcast.9), kind=kLoop, calls=%fused_computation.4 | loop fusion | flops 114688 | bytes 458752 | tf_op jit(solution)/shard_map/stack | solution.py:234
  1.7 1.5 %collective-permute-done = bf16[2,56,1024]{2,1,0:T(8,128)(2,1)S(1)} collective-permute-done((bf16[2,56,1024]{2,1,0:T(8,128)(2,1)S(1)}, bf16[2,56,1024]{2,1,0:T(8,128)(2,1)S(1)}, u32[]{:S(2)}, u32[]{:S(2)}) %collective-permute-start) | collective-permute-done | bytes 229408 | tf_op jit(solution)/shard_map/ppermute | solution.py:30
  3.2 2.0 %collective-permute-start.1 = (bf16[2,112,1024]{2,1,0:T(8,128)(2,1)S(1)}, bf16[2,112,1024]{2,1,0:T(8,128)(2,1)S(1)}, u32[]{:S(2)}, u32[]{:S(2)}) collective-permute-start(bf16[2,112,1024]{2,1,0:T(8,128)(2,1)S(1)} %pad_maximum_fusion.2.refs_0_), channel_id=1, source_target_pairs={{0,16},{2,114},{16,32},{18,2},{32,48},{34,18},{48,64},{50,34},{64,... | collective-permute-start | bytes 1376264 | tf_op jit(solution)/shard_map/ppermute | solution.py:30
  5.7 1.5 %collective-permute-start.3 = (bf16[2,56,1024]{2,1,0:T(8,128)(2,1)S(1)}, bf16[2,56,1024]{2,1,0:T(8,128)(2,1)S(1)}, u32[]{:S(2)}, u32[]{:S(2)}) collective-permute-start(bf16[2,56,1024]{2,1,0:T(8,128)(2,1)S(1)} %pad_maximum_fusion.4), channel_id=1, source_target_pairs={{0,129},{2,14},{16,145},{18,30},{32,161},{34,46},{48,177},{50,62},... | collective-permute-start | bytes 688136 | tf_op jit(solution)/shard_map/ppermute | solution.py:30
  7.3 1.4 %collective-permute-start.4 = (bf16[2,56,1024]{2,1,0:T(8,128)(2,1)S(1)}, bf16[2,56,1024]{2,1,0:T(8,128)(2,1)S(1)}, u32[]{:S(2)}, u32[]{:S(2)}) collective-permute-start(bf16[2,56,1024]{2,1,0:T(8,128)(2,1)S(1)} %pad_maximum_fusion.4), channel_id=1, source_target_pairs={{0,128},{2,10},{16,144},{18,26},{32,160},{34,42},{48,176},{50,58},... | collective-permute-start | bytes 688136 | tf_op jit(solution)/shard_map/ppermute | solution.py:30
  8.7 2.6 %collective-permute-done.2 = bf16[2,56,1024]{2,1,0:T(8,128)(2,1)S(1)} collective-permute-done((bf16[2,56,1024]{2,1,0:T(8,128)(2,1)S(1)}, bf16[2,56,1024]{2,1,0:T(8,128)(2,1)S(1)}, u32[]{:S(2)}, u32[]{:S(2)}) %collective-permute-start.2) | collective-permute-done | bytes 229408 | tf_op jit(solution)/shard_map/ppermute | solution.py:30
  11.2 4.1 %collective-permute-done.3 = bf16[2,56,1024]{2,1,0:T(8,128)(2,1)S(1)} collective-permute-done((bf16[2,56,1024]{2,1,0:T(8,128)(2,1)S(1)}, bf16[2,56,1024]{2,1,0:T(8,128)(2,1)S(1)}, u32[]{:S(2)}, u32[]{:S(2)}) %collective-permute-start.3) | collective-permute-done | bytes 229408 | tf_op jit(solution)/shard_map/ppermute | solution.py:30
  15.6 1.8 %collective-permute-start.8 = (bf16[2,112,1024]{2,1,0:T(8,128)(2,1)S(1)}, bf16[2,112,1024]{2,1,0:T(8,128)(2,1)S(1)}, u32[]{:S(2)}, u32[]{:S(2)}) collective-permute-start(bf16[2,112,1024]{2,1,0:T(8,128)(2,1)S(1)} %collective-permute-done.1.refs_1_), channel_id=1, source_target_pairs={{0,16},{2,114},{16,32},{18,2},{32,48},{34,18},{48,64},{50,34},{64,... | collective-permute-start | bytes 1376264 | tf_op jit(solution)/shard_map/ppermute | solution.py:30
  17.5 1.6 %collective-permute-start.5 = (bf16[2,224,1024]{2,1,0:T(8,128)(2,1)S(1)}, bf16[2,224,1024]{2,1,0:T(8,128)(2,1)S(1)}, u32[]{:S(2)}, u32[]{:S(2)}) collective-permute-start(bf16[2,224,1024]{2,1,0:T(8,128)(2,1)S(1)} %pad_maximum_fusion.refs_0_), channel_id=1, source_target_pairs={{0,4},{2,3},{16,20},{18,19},{32,36},{34,35},{48,52},{50,51},{64,68... | collective-permute-start | bytes 2752520 | tf_op jit(solution)/shard_map/ppermute | solution.py:30
  19.0 1.7 %collective-permute-start.6 = (bf16[2,224,1024]{2,1,0:T(8,128)(2,1)S(1)}, bf16[2,224,1024]{2,1,0:T(8,128)(2,1)S(1)}, u32[]{:S(2)}, u32[]{:S(2)}) collective-permute-start(bf16[2,224,1024]{2,1,0:T(8,128)(2,1)S(1)} %pad_maximum_fusion.refs_0_), channel_id=1, source_target_pairs={{0,12},{2,131},{16,28},{18,147},{32,44},{34,163},{48,60},{50,179},... | collective-permute-start | bytes 2752520 | tf_op jit(solution)/shard_map/ppermute | solution.py:30
  20.7 2.0 %collective-permute-start.7 = (bf16[2,224,1024]{2,1,0:T(8,128)(2,1)S(1)}, bf16[2,224,1024]{2,1,0:T(8,128)(2,1)S(1)}, u32[]{:S(2)}, u32[]{:S(2)}) collective-permute-start(bf16[2,224,1024]{2,1,0:T(8,128)(2,1)S(1)} %pad_maximum_fusion.refs_0_), channel_id=1, source_target_pairs={{0,8},{2,130},{16,24},{18,146},{32,40},{34,162},{48,56},{50,178},{... | collective-permute-start | bytes 2752520 | tf_op jit(solution)/shard_map/ppermute | solution.py:30
  22.7 3.3 %collective-permute-done.8.refs_2_ = bf16[2,112,1024]{2,1,0:T(8,128)(2,1)S(1)} collective-permute-done((bf16[2,112,1024]{2,1,0:T(8,128)(2,1)S(1)}, bf16[2,112,1024]{2,1,0:T(8,128)(2,1)S(1)}, u32[]{:S(2)}, u32[]{:S(2)}) %collective-permute-start.8) | collective-permute-done | bytes 458784 | tf_op jit(solution)/shard_map/ppermute | solution.py:30
  26.1 2.6 %collective-permute-start.10 = (bf16[2,224,1024]{2,1,0:T(8,128)(2,1)S(1)}, bf16[2,224,1024]{2,1,0:T(8,128)(2,1)S(1)}, u32[]{:S(2)}, u32[]{:S(2)}) collective-permute-start(bf16[2,224,1024]{2,1,0:T(8,128)(2,1)S(1)} %pad_maximum_fusion.1), channel_id=1, source_target_pairs={{0,2},{2,0},{16,18},{18,16},{32,34},{34,32},{48,50},{50,48},{64,66... | collective-permute-start | bytes 2752520 | tf_op jit(solution)/shard_map/ppermute | solution.py:30
  28.7 7.1 %collective-permute-done.9.refs_3_ = bf16[2,112,1024]{2,1,0:T(8,128)(2,1)S(1)} collective-permute-done((bf16[2,112,1024]{2,1,0:T(8,128)(2,1)S(1)}, bf16[2,112,1024]{2,1,0:T(8,128)(2,1)S(1)}, u32[]{:S(2)}, u32[]{:S(2)}) %collective-permute-start.9) | collective-permute-done | bytes 458784 | tf_op jit(solution)/shard_map/ppermute | solution.py:30
  35.8 1.6 %collective-permute-start.11 = (bf16[2,112,1024]{2,1,0:T(8,128)(2,1)S(1)}, bf16[2,112,1024]{2,1,0:T(8,128)(2,1)S(1)}, u32[]{:S(2)}, u32[]{:S(2)}) collective-permute-start(bf16[2,112,1024]{2,1,0:T(8,128)(2,1)S(1)} %collective-permute-done.9.refs_3_), channel_id=1, source_target_pairs={{0,2},{2,0},{16,18},{18,16},{32,34},{34,32},{48,50},{50,48},{64,66... | collective-permute-start | bytes 1376264 | tf_op jit(solution)/shard_map/ppermute | solution.py:30
  37.5 5.6 %collective-permute-done.12 = bf16[2,56,1024]{2,1,0:T(8,128)(2,1)S(1)} collective-permute-done((bf16[2,56,1024]{2,1,0:T(8,128)(2,1)S(1)}, bf16[2,56,1024]{2,1,0:T(8,128)(2,1)S(1)}, u32[]{:S(2)}, u32[]{:S(2)}) %collective-permute-start.12) | collective-permute-done | bytes 229408 | tf_op jit(solution)/shard_map/ppermute | solution.py:30
  43.1 1.3 %plane_rows.1 = (bf16[2,896,1024]{2,1,0:T(8,128)(2,1)S(1)}, f32[2,896,128]{2,1,0:T(8,128)S(1)}) custom-call(s32[2]{0:T(128)S(1)} %copy-done, bf16[2,224,1024]{2,1,0:T(8,128)(2,1)S(1)} %pad_maximum_fusion.refs_0_, bf16[2,224,1024]{2,1,0:T(8,128)(2,1)S(1)} %collective-permute-done.5.refs_1_, bf16[2,224,1024]{2,1,0:T(8,128)(2,1)S(1)} %collective-permute-done.6.refs_2_, ...), custom_call_target="tpu_custom_call" | custom-call | flops 3670016 | bytes 7340032 | tf_op jit(solution)/shard_map/plane_rows/pallas_call | solution.py:83
  44.6 6.2 %gram.1 = f32[16,128]{1,0:T(8,128)S(1)} custom-call(s32[2]{0:T(128)S(1)} %copy-done, bf16[2,896,1024]{2,1,0:T(8,128)(2,1)S(1)} %get-tuple-element.9.w_ref, f32[2,896,128]{2,1,0:T(8,128)S(1)} %get-tuple-element.10.norm_ref, bf16[2,112,1024]{2,1,0:T(8,128)(2,1)S(1)} %pad_maximum_fusion.2.refs_0_, bf16[2,112,1024]{2,1,0:T(8,128)(2,1)S(1)} %collective-permute-done.1.refs_1_, ...), custom_call_target="tpu_custom_call" | custom-call | flops 3288334336 | bytes 7340032 | tf_op jit(solution)/shard_map/gram/pallas_call | solution.py:159
  51.2 1.6 %collective-permute-start.15 = (f32[16,128]{1,0:T(8,128)S(1)}, f32[16,128]{1,0:T(8,128)S(1)}, u32[]{:S(2)}, u32[]{:S(2)}) collective-permute-start(f32[16,128]{1,0:T(8,128)S(1)} %gram.1), channel_id=1, source_target_pairs={{0,16},{2,18},{16,0},{18,2},{32,48},{34,50},{48,32},{50,34},{64,80... | collective-permute-start | bytes 24584 | tf_op jit(solution)/shard_map/ppermute | solution.py:30
  52.9 2.0 %collective-permute-done.15 = f32[16,128]{1,0:T(8,128)S(1)} collective-permute-done((f32[16,128]{1,0:T(8,128)S(1)}, f32[16,128]{1,0:T(8,128)S(1)}, u32[]{:S(2)}, u32[]{:S(2)}) %collective-permute-start.15) | collective-permute-done | bytes 8224 | tf_op jit(solution)/shard_map/ppermute | solution.py:30
  54.9 1.0 %collective-permute-done.16 = f32[16,128]{1,0:T(8,128)S(1)} collective-permute-done((f32[16,128]{1,0:T(8,128)S(1)}, f32[16,128]{1,0:T(8,128)S(1)}, u32[]{:S(2)}, u32[]{:S(2)}) %collective-permute-start.16) | collective-permute-done | bytes 8224 | tf_op jit(solution)/shard_map/ppermute | solution.py:30
  55.9 4.7 %collective-permute-start.17 = (f32[16,128]{1,0:T(8,128)S(1)}, f32[16,128]{1,0:T(8,128)S(1)}, u32[]{:S(2)}, u32[]{:S(2)}) collective-permute-start(f32[16,128]{1,0:T(8,128)S(1)} %add_add_fusion.1), channel_id=1, source_target_pairs={{0,64},{2,66},{16,80},{18,82},{32,96},{34,98},{48,112},{50,114},{6... | collective-permute-start | bytes 24584 | tf_op jit(solution)/shard_map/ppermute | solution.py:30
  60.6 4.1 %collective-permute-start.19 = (f32[16,128]{1,0:T(8,128)S(1)}, f32[16,128]{1,0:T(8,128)S(1)}, u32[]{:S(2)}, u32[]{:S(2)}) collective-permute-start(f32[16,128]{1,0:T(8,128)S(1)} %add_add_fusion.1), channel_id=1, source_target_pairs={{0,96},{2,98},{16,112},{18,114},{32,0},{34,2},{48,16},{50,18},{64,... | collective-permute-start | bytes 24584 | tf_op jit(solution)/shard_map/ppermute | solution.py:30
  64.7 1.6 %collective-permute-done.18 = f32[16,128]{1,0:T(8,128)S(1)} collective-permute-done((f32[16,128]{1,0:T(8,128)S(1)}, f32[16,128]{1,0:T(8,128)S(1)}, u32[]{:S(2)}, u32[]{:S(2)}) %collective-permute-start.18) | collective-permute-done | bytes 8224 | tf_op jit(solution)/shard_map/ppermute | solution.py:30
  66.4 1.9 %collective-permute-start.20 = (f32[8,128]{1,0:T(8,128)S(1)}, f32[8,128]{1,0:T(8,128)S(1)}, u32[]{:S(2)}, u32[]{:S(2)}) collective-permute-start(f32[8,128]{1,0:T(8,128)S(1)} %stack.37), channel_id=1, source_target_pairs={{0,128},{2,130},{16,144},{18,146},{32,160},{34,162},{48,176},{50,1... | collective-permute-start | bytes 12296 | tf_op jit(solution)/shard_map/ppermute | solution.py:30
  68.3 1.1 %collective-permute-start.21 = (f32[8,128]{1,0:T(8,128)S(1)}, f32[8,128]{1,0:T(8,128)S(1)}, u32[]{:S(2)}, u32[]{:S(2)}) collective-permute-start(f32[8,128]{1,0:T(8,128)S(1)} %stack.37), channel_id=1, source_target_pairs={{0,1},{2,3},{16,17},{18,19},{32,33},{34,35},{48,49},{50,51},{64,65... | collective-permute-start | bytes 12296 | tf_op jit(solution)/shard_map/ppermute | solution.py:30
  69.4 1.0 %collective-permute-start.22 = (f32[8,128]{1,0:T(8,128)S(1)}, f32[8,128]{1,0:T(8,128)S(1)}, u32[]{:S(2)}, u32[]{:S(2)}) collective-permute-start(f32[8,128]{1,0:T(8,128)S(1)} %stack.37), channel_id=1, source_target_pairs={{0,129},{2,131},{16,145},{18,147},{32,161},{34,163},{48,177},{50,1... | collective-permute-start | bytes 12296 | tf_op jit(solution)/shard_map/ppermute | solution.py:30
  70.3 1.3 %collective-permute-done.20 = f32[8,128]{1,0:T(8,128)S(1)} collective-permute-done((f32[8,128]{1,0:T(8,128)S(1)}, f32[8,128]{1,0:T(8,128)S(1)}, u32[]{:S(2)}, u32[]{:S(2)}) %collective-permute-start.20) | collective-permute-done | bytes 4128 | tf_op jit(solution)/shard_map/ppermute | solution.py:30
  71.9 2.3 %collective-permute-done.22 = f32[8,128]{1,0:T(8,128)S(1)} collective-permute-done((f32[8,128]{1,0:T(8,128)S(1)}, f32[8,128]{1,0:T(8,128)S(1)}, u32[]{:S(2)}, u32[]{:S(2)}) %collective-permute-start.22) | collective-permute-done | bytes 4128 | tf_op jit(solution)/shard_map/ppermute | solution.py:30
  74.2 3.4 %collective-permute-start.23 = (f32[8,128]{1,0:T(8,128)S(1)}, f32[8,128]{1,0:T(8,128)S(1)}, u32[]{:S(2)}, u32[]{:S(2)}) collective-permute-start(f32[8,128]{1,0:T(8,128)S(1)} %add_add_fusion.2.sums_ref), channel_id=1, source_target_pairs={{0,8},{2,10},{16,24},{18,26},{32,40},{34,42},{48,56},{50,58},{64,7... | collective-permute-start | bytes 12296 | tf_op jit(solution)/shard_map/ppermute | solution.py:30
  78.0 2.8 %collective-permute-start.25 = (f32[8,128]{1,0:T(8,128)S(1)}, f32[8,128]{1,0:T(8,128)S(1)}, u32[]{:S(2)}, u32[]{:S(2)}) collective-permute-start(f32[8,128]{1,0:T(8,128)S(1)} %add_add_fusion.2.sums_ref), channel_id=1, source_target_pairs={{0,12},{2,14},{16,28},{18,30},{32,44},{34,46},{48,60},{50,62},{64,... | collective-permute-start | bytes 12296 | tf_op jit(solution)/shard_map/ppermute | solution.py:30
  80.8 1.6 %collective-permute-done.24.refs_1_ = f32[8,128]{1,0:T(8,128)S(1)} collective-permute-done((f32[8,128]{1,0:T(8,128)S(1)}, f32[8,128]{1,0:T(8,128)S(1)}, u32[]{:S(2)}, u32[]{:S(2)}) %collective-permute-start.24) | collective-permute-done | bytes 4128 | tf_op jit(solution)/shard_map/ppermute | solution.py:30
  (38 shorter events, 3.2 us)
Async XLA Ops:
  1.6 1.6 %collective-permute-start = (bf16[2,56,1024]{2,1,0:T(8,128)(2,1)S(1)}, bf16[2,56,1024]{2,1,0:T(8,128)(2,1)S(1)}, u32[]{:S(2)}, u32[]{:S(2)}) collective-permute-start(bf16[2,56,1024]{2,1,0:T(8,128)(2,1)S(1)} %pad_maximum_fusion.4), channel_id=1, source_target_pairs={{0,2},{2,0},{16,18},{18,16},{32,34},{34,32},{48,50},{50,48},{64,66... | collective-permute-start | bytes 688136 | tf_op jit(solution)/shard_map/ppermute | solution.py:30
  3.2 39.9 %copy-start = (s32[2]{0:T(128)S(1)}, s32[2]{0:T(128)}, u32[]{:S(2)}) copy-start(s32[2]{0:T(128)} %spread_ref.3) | copy-start | bytes 28
  3.2 12.4 %collective-permute-start.1 = (bf16[2,112,1024]{2,1,0:T(8,128)(2,1)S(1)}, bf16[2,112,1024]{2,1,0:T(8,128)(2,1)S(1)}, u32[]{:S(2)}, u32[]{:S(2)}) collective-permute-start(bf16[2,112,1024]{2,1,0:T(8,128)(2,1)S(1)} %pad_maximum_fusion.2.refs_0_), channel_id=1, source_target_pairs={{0,16},{2,114},{16,32},{18,2},{32,48},{34,18},{48,64},{50,34},{64,... | collective-permute-start | bytes 1376264 | tf_op jit(solution)/shard_map/ppermute | solution.py:30
  5.2 6.0 %collective-permute-start.2 = (bf16[2,56,1024]{2,1,0:T(8,128)(2,1)S(1)}, bf16[2,56,1024]{2,1,0:T(8,128)(2,1)S(1)}, u32[]{:S(2)}, u32[]{:S(2)}) collective-permute-start(bf16[2,56,1024]{2,1,0:T(8,128)(2,1)S(1)} %pad_maximum_fusion.4), channel_id=1, source_target_pairs={{0,1},{2,6},{16,17},{18,22},{32,33},{34,38},{48,49},{50,54},{64,65... | collective-permute-start | bytes 688136 | tf_op jit(solution)/shard_map/ppermute | solution.py:30
  5.7 9.7 %collective-permute-start.3 = (bf16[2,56,1024]{2,1,0:T(8,128)(2,1)S(1)}, bf16[2,56,1024]{2,1,0:T(8,128)(2,1)S(1)}, u32[]{:S(2)}, u32[]{:S(2)}) collective-permute-start(bf16[2,56,1024]{2,1,0:T(8,128)(2,1)S(1)} %pad_maximum_fusion.4), channel_id=1, source_target_pairs={{0,129},{2,14},{16,145},{18,30},{32,161},{34,46},{48,177},{50,62},... | collective-permute-start | bytes 688136 | tf_op jit(solution)/shard_map/ppermute | solution.py:30
  7.3 8.1 %collective-permute-start.4 = (bf16[2,56,1024]{2,1,0:T(8,128)(2,1)S(1)}, bf16[2,56,1024]{2,1,0:T(8,128)(2,1)S(1)}, u32[]{:S(2)}, u32[]{:S(2)}) collective-permute-start(bf16[2,56,1024]{2,1,0:T(8,128)(2,1)S(1)} %pad_maximum_fusion.4), channel_id=1, source_target_pairs={{0,128},{2,10},{16,144},{18,26},{32,160},{34,42},{48,176},{50,58},... | collective-permute-start | bytes 688136 | tf_op jit(solution)/shard_map/ppermute | solution.py:30
  15.6 10.4 %collective-permute-start.8 = (bf16[2,112,1024]{2,1,0:T(8,128)(2,1)S(1)}, bf16[2,112,1024]{2,1,0:T(8,128)(2,1)S(1)}, u32[]{:S(2)}, u32[]{:S(2)}) collective-permute-start(bf16[2,112,1024]{2,1,0:T(8,128)(2,1)S(1)} %collective-permute-done.1.refs_1_), channel_id=1, source_target_pairs={{0,16},{2,114},{16,32},{18,2},{32,48},{34,18},{48,64},{50,34},{64,... | collective-permute-start | bytes 1376264 | tf_op jit(solution)/shard_map/ppermute | solution.py:30
  17.5 18.4 %collective-permute-start.5 = (bf16[2,224,1024]{2,1,0:T(8,128)(2,1)S(1)}, bf16[2,224,1024]{2,1,0:T(8,128)(2,1)S(1)}, u32[]{:S(2)}, u32[]{:S(2)}) collective-permute-start(bf16[2,224,1024]{2,1,0:T(8,128)(2,1)S(1)} %pad_maximum_fusion.refs_0_), channel_id=1, source_target_pairs={{0,4},{2,3},{16,20},{18,19},{32,36},{34,35},{48,52},{50,51},{64,68... | collective-permute-start | bytes 2752520 | tf_op jit(solution)/shard_map/ppermute | solution.py:30
  19.0 24.0 %collective-permute-start.6 = (bf16[2,224,1024]{2,1,0:T(8,128)(2,1)S(1)}, bf16[2,224,1024]{2,1,0:T(8,128)(2,1)S(1)}, u32[]{:S(2)}, u32[]{:S(2)}) collective-permute-start(bf16[2,224,1024]{2,1,0:T(8,128)(2,1)S(1)} %pad_maximum_fusion.refs_0_), channel_id=1, source_target_pairs={{0,12},{2,131},{16,28},{18,147},{32,44},{34,163},{48,60},{50,179},... | collective-permute-start | bytes 2752520 | tf_op jit(solution)/shard_map/ppermute | solution.py:30
  20.7 22.4 %collective-permute-start.7 = (bf16[2,224,1024]{2,1,0:T(8,128)(2,1)S(1)}, bf16[2,224,1024]{2,1,0:T(8,128)(2,1)S(1)}, u32[]{:S(2)}, u32[]{:S(2)}) collective-permute-start(bf16[2,224,1024]{2,1,0:T(8,128)(2,1)S(1)} %pad_maximum_fusion.refs_0_), channel_id=1, source_target_pairs={{0,8},{2,130},{16,24},{18,146},{32,40},{34,162},{48,56},{50,178},{... | collective-permute-start | bytes 2752520 | tf_op jit(solution)/shard_map/ppermute | solution.py:30
  26.0 9.7 %collective-permute-start.9 = (bf16[2,112,1024]{2,1,0:T(8,128)(2,1)S(1)}, bf16[2,112,1024]{2,1,0:T(8,128)(2,1)S(1)}, u32[]{:S(2)}, u32[]{:S(2)}) collective-permute-start(bf16[2,112,1024]{2,1,0:T(8,128)(2,1)S(1)} %collective-permute-done.8.refs_2_), channel_id=1, source_target_pairs={{0,16},{2,114},{16,32},{18,2},{32,48},{34,18},{48,64},{50,34},{64,... | collective-permute-start | bytes 1376264 | tf_op jit(solution)/shard_map/ppermute | solution.py:30
  26.1 18.5 %collective-permute-start.10 = (bf16[2,224,1024]{2,1,0:T(8,128)(2,1)S(1)}, bf16[2,224,1024]{2,1,0:T(8,128)(2,1)S(1)}, u32[]{:S(2)}, u32[]{:S(2)}) collective-permute-start(bf16[2,224,1024]{2,1,0:T(8,128)(2,1)S(1)} %pad_maximum_fusion.1), channel_id=1, source_target_pairs={{0,2},{2,0},{16,18},{18,16},{32,34},{34,32},{48,50},{50,48},{64,66... | collective-permute-start | bytes 2752520 | tf_op jit(solution)/shard_map/ppermute | solution.py:30
  35.7 7.3 %collective-permute-start.12 = (bf16[2,56,1024]{2,1,0:T(8,128)(2,1)S(1)}, bf16[2,56,1024]{2,1,0:T(8,128)(2,1)S(1)}, u32[]{:S(2)}, u32[]{:S(2)}) collective-permute-start(bf16[2,56,1024]{2,1,0:T(8,128)(2,1)S(1)} %slice.20), channel_id=1, source_target_pairs={{0,16},{2,114},{16,32},{18,2},{32,48},{34,18},{48,64},{50,34},{64,... | collective-permute-start | bytes 688136 | tf_op jit(solution)/shard_map/ppermute | solution.py:30
  35.8 8.7 %collective-permute-start.11 = (bf16[2,112,1024]{2,1,0:T(8,128)(2,1)S(1)}, bf16[2,112,1024]{2,1,0:T(8,128)(2,1)S(1)}, u32[]{:S(2)}, u32[]{:S(2)}) collective-permute-start(bf16[2,112,1024]{2,1,0:T(8,128)(2,1)S(1)} %collective-permute-done.9.refs_3_), channel_id=1, source_target_pairs={{0,2},{2,0},{16,18},{18,16},{32,34},{34,32},{48,50},{50,48},{64,66... | collective-permute-start | bytes 1376264 | tf_op jit(solution)/shard_map/ppermute | solution.py:30
  43.1 1.5 %collective-permute-start.13 = (bf16[2,56,1024]{2,1,0:T(8,128)(2,1)S(1)}, bf16[2,56,1024]{2,1,0:T(8,128)(2,1)S(1)}, u32[]{:S(2)}, u32[]{:S(2)}) collective-permute-start(bf16[2,56,1024]{2,1,0:T(8,128)(2,1)S(1)} %collective-permute-done.12), channel_id=1, source_target_pairs={{0,2},{2,0},{16,18},{18,16},{32,34},{34,32},{48,50},{50,48},{64,66... | collective-permute-start | bytes 688136 | tf_op jit(solution)/shard_map/ppermute | solution.py:30
  50.8 2.1 %collective-permute-start.14 = (f32[16,128]{1,0:T(8,128)S(1)}, f32[16,128]{1,0:T(8,128)S(1)}, u32[]{:S(2)}, u32[]{:S(2)}) collective-permute-start(f32[16,128]{1,0:T(8,128)S(1)} %gram.1), channel_id=1, source_target_pairs={{0,2},{2,0},{16,18},{18,16},{32,34},{34,32},{48,50},{50,48},{64,66... | collective-permute-start | bytes 24584 | tf_op jit(solution)/shard_map/ppermute | solution.py:30
  51.2 3.7 %collective-permute-start.15 = (f32[16,128]{1,0:T(8,128)S(1)}, f32[16,128]{1,0:T(8,128)S(1)}, u32[]{:S(2)}, u32[]{:S(2)}) collective-permute-start(f32[16,128]{1,0:T(8,128)S(1)} %gram.1), channel_id=1, source_target_pairs={{0,16},{2,18},{16,0},{18,2},{32,48},{34,50},{48,32},{50,34},{64,80... | collective-permute-start | bytes 24584 | tf_op jit(solution)/shard_map/ppermute | solution.py:30
  52.8 3.1 %collective-permute-start.16 = (f32[16,128]{1,0:T(8,128)S(1)}, f32[16,128]{1,0:T(8,128)S(1)}, u32[]{:S(2)}, u32[]{:S(2)}) collective-permute-start(f32[16,128]{1,0:T(8,128)S(1)} %gram.1), channel_id=1, source_target_pairs={{0,18},{2,16},{16,2},{18,0},{32,50},{34,48},{48,34},{50,32},{64,82... | collective-permute-start | bytes 24584 | tf_op jit(solution)/shard_map/ppermute | solution.py:30
  55.9 8.8 %collective-permute-start.17 = (f32[16,128]{1,0:T(8,128)S(1)}, f32[16,128]{1,0:T(8,128)S(1)}, u32[]{:S(2)}, u32[]{:S(2)}) collective-permute-start(f32[16,128]{1,0:T(8,128)S(1)} %add_add_fusion.1), channel_id=1, source_target_pairs={{0,64},{2,66},{16,80},{18,82},{32,96},{34,98},{48,112},{50,114},{6... | collective-permute-start | bytes 24584 | tf_op jit(solution)/shard_map/ppermute | solution.py:30
  60.6 5.8 %collective-permute-start.18 = (f32[16,128]{1,0:T(8,128)S(1)}, f32[16,128]{1,0:T(8,128)S(1)}, u32[]{:S(2)}, u32[]{:S(2)}) collective-permute-start(f32[16,128]{1,0:T(8,128)S(1)} %add_add_fusion.1), channel_id=1, source_target_pairs={{0,32},{2,34},{16,48},{18,50},{32,64},{34,66},{48,80},{50,82},{64,... | collective-permute-start | bytes 24584 | tf_op jit(solution)/shard_map/ppermute | solution.py:30
  60.6 5.7 %collective-permute-start.19 = (f32[16,128]{1,0:T(8,128)S(1)}, f32[16,128]{1,0:T(8,128)S(1)}, u32[]{:S(2)}, u32[]{:S(2)}) collective-permute-start(f32[16,128]{1,0:T(8,128)S(1)} %add_add_fusion.1), channel_id=1, source_target_pairs={{0,96},{2,98},{16,112},{18,114},{32,0},{34,2},{48,16},{50,18},{64,... | collective-permute-start | bytes 24584 | tf_op jit(solution)/shard_map/ppermute | solution.py:30
  66.4 5.2 %collective-permute-start.20 = (f32[8,128]{1,0:T(8,128)S(1)}, f32[8,128]{1,0:T(8,128)S(1)}, u32[]{:S(2)}, u32[]{:S(2)}) collective-permute-start(f32[8,128]{1,0:T(8,128)S(1)} %stack.37), channel_id=1, source_target_pairs={{0,128},{2,130},{16,144},{18,146},{32,160},{34,162},{48,176},{50,1... | collective-permute-start | bytes 12296 | tf_op jit(solution)/shard_map/ppermute | solution.py:30
  68.3 3.6 %collective-permute-start.21 = (f32[8,128]{1,0:T(8,128)S(1)}, f32[8,128]{1,0:T(8,128)S(1)}, u32[]{:S(2)}, u32[]{:S(2)}) collective-permute-start(f32[8,128]{1,0:T(8,128)S(1)} %stack.37), channel_id=1, source_target_pairs={{0,1},{2,3},{16,17},{18,19},{32,33},{34,35},{48,49},{50,51},{64,65... | collective-permute-start | bytes 12296 | tf_op jit(solution)/shard_map/ppermute | solution.py:30
  69.4 4.8 %collective-permute-start.22 = (f32[8,128]{1,0:T(8,128)S(1)}, f32[8,128]{1,0:T(8,128)S(1)}, u32[]{:S(2)}, u32[]{:S(2)}) collective-permute-start(f32[8,128]{1,0:T(8,128)S(1)} %stack.37), channel_id=1, source_target_pairs={{0,129},{2,131},{16,145},{18,147},{32,161},{34,163},{48,177},{50,1... | collective-permute-start | bytes 12296 | tf_op jit(solution)/shard_map/ppermute | solution.py:30
  74.2 6.6 %collective-permute-start.23 = (f32[8,128]{1,0:T(8,128)S(1)}, f32[8,128]{1,0:T(8,128)S(1)}, u32[]{:S(2)}, u32[]{:S(2)}) collective-permute-start(f32[8,128]{1,0:T(8,128)S(1)} %add_add_fusion.2.sums_ref), channel_id=1, source_target_pairs={{0,8},{2,10},{16,24},{18,26},{32,40},{34,42},{48,56},{50,58},{64,7... | collective-permute-start | bytes 12296 | tf_op jit(solution)/shard_map/ppermute | solution.py:30
  77.6 4.8 %collective-permute-start.24 = (f32[8,128]{1,0:T(8,128)S(1)}, f32[8,128]{1,0:T(8,128)S(1)}, u32[]{:S(2)}, u32[]{:S(2)}) collective-permute-start(f32[8,128]{1,0:T(8,128)S(1)} %add_add_fusion.2.sums_ref), channel_id=1, source_target_pairs={{0,4},{2,6},{16,20},{18,22},{32,36},{34,38},{48,52},{50,54},{64,68... | collective-permute-start | bytes 12296 | tf_op jit(solution)/shard_map/ppermute | solution.py:30
  78.0 4.4 %collective-permute-start.25 = (f32[8,128]{1,0:T(8,128)S(1)}, f32[8,128]{1,0:T(8,128)S(1)}, u32[]{:S(2)}, u32[]{:S(2)}) collective-permute-start(f32[8,128]{1,0:T(8,128)S(1)} %add_add_fusion.2.sums_ref), channel_id=1, source_target_pairs={{0,12},{2,14},{16,28},{18,30},{32,44},{34,46},{48,60},{50,62},{64,... | collective-permute-start | bytes 12296 | tf_op jit(solution)/shard_map/ppermute | solution.py:30
